TPU v7x, 256 devices: a whole 4x4x8 slice. The times are simulated.
256 devices in a mesh: row: 16 (over z, core), col: 16 (over y, x).
Axes of the slice: x: 4, y: 4, z: 8, core: 2. Of those that a mesh axis runs over, the one named last changes fastest.
Arguments:
- hessian_inverse: float32 [6656, 6656], P('row', 'col'), may hold values from -9 to 13, as said below
- weights: bfloat16 [32768, 6656], P('row', 'col'), may hold values from -6 to 6
- pruned: int32 [512], replicated, may hold values from 0 to 6655, as said below
Outputs:
- inverse_updated: float32 [6656, 6656], P('row', 'col')
- weights_updated: float32 [32768, 6656], P('row', 'col')
Inputs may be any that keep to these rules, and one draw needn't show every extreme that they name: `pruned`: 512 distinct hidden units in increasing order; at most 64 of them fall in one column tile of 416 consecutive units, and exactly 64 in some tile. `hessian_inverse`: symmetric positive definite.
All inputs are finite; a program needn't handle non-finite values.
Results may differ from a plain program's by a relative error of at most 0.0003.
Values may be sent and summed in bfloat16 or wider, within the bound.
No kernel may reach another device: no remote copies, remote signals or barrier semaphores. Data moves between devices by JAX's collectives and lax.ppermute only.
A program may use at most 128 MiB of HBM per device.

v0:
```python
import functools
import math

import jax
import jax.numpy as jnp
from jax import lax
from jax.experimental import pallas as pl
from jax.experimental.pallas import tpu as pltpu
from jax.sharding import PartitionSpec as P


HIGH = lax.Precision.HIGHEST
F32 = jnp.float32
BF16 = jnp.bfloat16
VMEM = pl.BlockSpec(memory_space=pltpu.VMEM)
SMEM = pl.BlockSpec(memory_space=pltpu.SMEM)
BASE = 128


def across(a, b, dims, precision=None):
    return lax.dot_general(a, b, (dims, ((), ())), precision=precision, preferred_element_type=F32)


def one_hot(index, width):
    slots = index.shape[0]
    return jnp.where(index == lax.broadcasted_iota(jnp.int32, (slots, width), 1), 1.0, 0.0)


def held(pruned, tile, width, place):
    low = tile * width
    before = jnp.sum(jnp.where(pruned < low, 1, 0), axis=1, keepdims=True)
    place = place(before)
    lane = lax.broadcasted_iota(jnp.int32, (place.shape[0], pruned.shape[1]), 1)
    here = (lane == place) & (pruned >= low) & (pruned < low + width)
    return jnp.sum(jnp.where(here, pruned - low + 1, 0), axis=1, keepdims=True) - 1


def in_turn(cap):
    slot = lax.broadcasted_iota(jnp.int32, (cap, 1), 0)
    return lambda before: before + slot


def dealt(cap, hands):
    slot = lax.broadcasted_iota(jnp.int32, (cap, 1), 0)
    each = cap // hands
    hand, turn = slot // each, slot % each

    def place(before):
        return hand + hands * ((before - hand + hands - 1) // hands + turn)

    return place


def pack_rows(at_ref, pruned_ref, h_ref, rows_ref):
    height, _ = h_ref.shape
    pruned = pruned_ref[...]
    tiles = rows_ref.shape[0]
    cap = 2 * pruned.shape[1] // tiles
    pick = one_hot(held(pruned, at_ref[0], height, in_turn(cap)), height)
    rows = across(pick, h_ref[...], ((1,), (0,)), HIGH)
    for core in range(2):
        part = strips_of(rows[cap // 2 * core : cap // 2 * (core + 1)])
        for d in range(core, tiles, 2):
            rows_ref[d] = part


def strips_of(rows):
    count, width = rows.shape
    full = width // 128 * 128
    rest = width - full
    groups = 128 // rest
    each = count // groups
    strips = [rows[:, j : j + 128] for j in range(0, full, 128)]
    strips.append(jnp.concatenate([rows[each * i : each * i + each, full:] for i in range(groups)], axis=1))
    return jnp.concatenate(strips, axis=0)


def place_strips(ref, start, packed, count, width):
    full = width // 128
    rest = width - 128 * full
    each = count * rest // 128
    for j in range(full):
        ref[j, pl.ds(start, count), :] = packed[count * j : count * j + count]
    last = packed[count * full :]
    for i in range(128 // rest):
        ref[full, pl.ds(start + each * i, each), 0:rest] = last[:, rest * i : rest * i + rest]


def pack_cols(at_ref, pruned_ref, h_ref, w_ref, out_ref):
    pruned = pruned_ref[...]
    cap = out_ref.shape[0]
    width = h_ref.shape[1]
    tiles = 2 * pruned.shape[1] // cap
    pick = one_hot(held(pruned, at_ref[1], width, dealt(cap, tiles)), width)
    w = across(pick.astype(BF16), w_ref[...], ((1,), (0,))).astype(BF16)
    c = across(pick, h_ref[...], ((1,), (1,)), HIGH)
    c_high = c.astype(BF16)
    c_low = (c - c_high.astype(F32)).astype(BF16)
    out_ref[...] = jnp.concatenate([w, c_high, c_low], axis=1)


def gather_hand(at_ref, pruned_ref, got_ref, low_ref, high_ref, piece_ref, *, height, width):
    pruned = pruned_ref[...]
    cap, length = got_ref.shape
    tiles = piece_ref.shape[0]
    mine = cap // 2
    each = cap // tiles
    slot = lax.broadcasted_iota(jnp.int32, (cap, 1), 0)
    tile, turn = slot // each, slot % each
    before = jnp.sum(jnp.where(pruned < tile * width, 1, 0), axis=1, keepdims=True)
    after = jnp.sum(jnp.where(pruned < tile * width + width, 1, 0), axis=1, keepdims=True)
    hand = at_ref[1]
    turn = (before - hand + tiles - 1) // tiles + turn
    place = hand + tiles * turn
    turn = jnp.where(place < after, turn, -1)
    out = across(one_hot(turn, mine).astype(BF16), got_ref[...], ((0,), (0,)))
    cols = out[:, length - 2 * height : length - height] + out[:, length - height :]
    pick = one_hot(held(pruned, at_ref[0], height, in_turn(cap)), height)
    piece = across(pick, cols, ((1,), (1,)), HIGH)
    quarter = cap // 4
    piece = jnp.concatenate([piece[quarter * i : quarter * i + quarter] for i in range(4)], axis=1)
    for d in range(tiles):
        piece_ref[d] = piece
    low_ref[...] = out[: mine // 2].astype(BF16)
    high_ref[...] = out[mine // 2 :].astype(BF16)


def pack_slab(first_ref, at_ref, got_ref, out_ref, slab_ref, turned_ref):
    tiles, quarter, four = got_ref.shape
    mine = four // 4
    for t in range(tiles):
        got = got_ref[t]
        for i in range(4):
            slab_ref[pl.ds(first_ref[t] + quarter * i, quarter), 0:mine] = got[:, mine * i : mine * i + mine]
    turned_ref[...] = slab_ref[0 : turned_ref.shape[1], :].T[0:mine, :]
    half = mine // 2
    slab = turned_ref[pl.ds(pl.multiple_of(at_ref[0] % 2 * half, half), half), :]
    for d in range(tiles):
        out_ref[d] = slab


def place_rows(ref, at, start, value):
    rows, width = value.shape
    for j in range(0, width, 128):
        strip = value[:, j : j + 128]
        ref[at + j // 128, pl.ds(start, rows), 0 : strip.shape[1]] = strip


def rows_at(ref, start, rows, width):
    strips = [ref[j, pl.ds(start, rows), :] for j in range(ref.shape[0])]
    return jnp.concatenate(strips, axis=1)[:, :width]


def spread(v, i):
    return jnp.broadcast_to(v[i : i + 1, :], v.shape)


def invert_base(tiles):
    width = tiles[0].shape[1]
    lane = lax.broadcasted_iota(jnp.int32, (8, width), 1)
    sub = lax.broadcasted_iota(jnp.int32, (8, width), 0)
    tiles = list(tiles)
    count = len(tiles)
    for t in range(count):
        q = 8 * t
        own = tiles[t]
        cols = [jnp.broadcast_to(own[:, q + j : q + j + 1], (8, width)) for j in range(8)]
        here = (lane >= q) & (lane < q + 8)
        panel = jnp.where(here, jnp.where(lane - q == sub, 1.0, 0.0), own)
        for j in range(0, 8, 2):
            k = j + 1
            a, b, b2, c = spread(cols[j], j), spread(cols[k], j), spread(cols[j], k), spread(cols[k], k)
            r = 1.0 / (a * c - b * b2)
            i00, i01, i10, i11 = c * r, -(b * r), -(b2 * r), a * r
            is_j, is_k = sub == j, sub == k
            f_j = jnp.where(is_j, -i00, jnp.where(is_k, -i10, cols[j] * i00 + cols[k] * i10))
            f_k = jnp.where(is_j, -i01, jnp.where(is_k, -i11, cols[j] * i01 + cols[k] * i11))
            pivot = is_j | is_k

            def swept(v):
                return jnp.where(pivot, 0.0, v) - (f_j * spread(v, j) + f_k * spread(v, k))

            for m in range(j + 2, 8):
                cols[m] = swept(cols[m])
            panel = swept(panel)
        rows = [spread(panel, j) for j in range(8)]
        for s in range(1, count):
            s = (t + s) % count
            v = tiles[s]
            p = [jnp.broadcast_to(v[:, q + j : q + j + 1], (8, width)) * rows[j] for j in range(8)]
            total = ((p[0] + p[1]) + (p[2] + p[3])) + ((p[4] + p[5]) + (p[6] + p[7]))
            tiles[s] = jnp.where(here, 0.0, v) - total
        tiles[t] = panel
    return tiles


def invert(at_ref, own_ref, other_ref, out_ref, block_ref):
    tiles, half, n = own_ref.shape
    low_is_own = at_ref[0] % 2 == 0
    for t in range(tiles):
        own, other = own_ref[t], other_ref[t]
        low, high = jnp.where(low_is_own, own, other), jnp.where(low_is_own, other, own)
        for j in range(n // 128):
            lanes = slice(128 * j, 128 * j + 128)
            block_ref[j, pl.ds(t, half, stride=tiles), :] = low[:, lanes]
            block_ref[j, pl.ds(t + half * tiles, half, stride=tiles), :] = high[:, lanes]
    for j in range(n // 128):
        out_ref[:, 128 * j : 128 * j + 128] = block_ref[j]
    for lo in range(0, n, BASE):
        hi = lo + BASE
        diagonal = out_ref[lo:hi, lo:hi]
        base = jnp.concatenate(invert_base([diagonal[s : s + 8] for s in range(0, BASE, 8)]), axis=0)
        cols = out_ref[:, lo:hi]
        rows = jnp.dot(base, out_ref[lo:hi, :], precision=HIGH, preferred_element_type=F32)
        rows = jnp.concatenate([p for p in (rows[:, :lo], base, rows[:, hi:]) if p.shape[1]], axis=1)
        lane = lax.broadcasted_iota(jnp.int32, (BASE, n), 1)
        here = (lane >= lo) & (lane < hi)
        for r in range(0, n, BASE):
            if r != lo:
                kept = jnp.where(here, 0.0, out_ref[r : r + BASE, :])
                out_ref[r : r + BASE, :] = kept - jnp.dot(
                    cols[r : r + BASE], rows, precision=HIGH, preferred_element_type=F32
                )
        out_ref[lo:hi, :] = rows


def update(first_ref, at_ref, pruned_ref, inv_ref, own_ref, other_ref, *refs):
    blocks, (h_ref, w_ref, h_out_ref, w_out_ref, panel_ref, high_ref, low_ref, keep_ref) = refs[:-8], refs[-8:]
    step = pl.program_id(0)
    tiles = own_ref.shape[0]
    n = inv_ref.shape[0]
    width = h_ref.shape[1]
    half = n // tiles
    side = len(blocks) // 2
    block = w_ref.shape[1]
    rows_w = block * pl.num_programs(0)
    apply = ((1,), (0,))

    def cols(start, size):
        return jnp.concatenate([b[:, pl.ds(start, size)] for b in blocks], axis=0)

    @pl.when(step == 0)
    def _():
        low_is_own = at_ref[0] % 2 == 0
        for t in range(tiles):
            own, other = own_ref[t], other_ref[t]
            place_strips(panel_ref, first_ref[t], jnp.where(low_is_own, own, other), half, width)
            place_strips(panel_ref, first_ref[t] + half, jnp.where(low_is_own, other, own), half, width)
        panel = rows_at(panel_ref, 0, n, width)
        solved = jnp.dot(inv_ref[...], panel, precision=HIGH, preferred_element_type=F32)
        place_rows(panel_ref, 0, 0, solved)
        x, y = at_ref[1] % side, at_ref[1] // side
        hands = []
        for path in range(2):
            for far in range(side):
                for near in range(side):
                    dx, dy = (near, far) if path == 0 else (far, near)
                    hand = (y + side - dy) % side * side + (x + side - dx) % side
                    hands.append(hand + path * (n // 2))
        solved = jnp.concatenate(
            [
                jnp.concatenate([panel_ref[j, pl.ds(h, n // tiles // 2, stride=tiles), :] for h in hands], axis=0)
                for j in range(panel_ref.shape[0])
            ],
            axis=1,
        ).T[:width, :]
        high = solved.astype(BF16)
        high_ref[...] = high
        low_ref[...] = (solved - high.astype(F32)).astype(BF16)
        c_high, c_low = cols(rows_w, width), cols(rows_w + width, width)
        total = across(high_ref[...], c_high, apply)
        total = total + (across(low_ref[...], c_high, apply) + across(high_ref[...], c_low, apply))
        h_out_ref[...] = h_ref[...] - total.T
        unit = lax.broadcasted_iota(jnp.int32, (width, n), 0) + at_ref[1] * width
        hits = jnp.sum(jnp.where(unit == pruned_ref[...], 1.0, 0.0), axis=1, keepdims=True)
        keep_ref[...] = jnp.broadcast_to(1.0 - hits, keep_ref.shape)

    got = cols(pl.multiple_of(step * block, block), block)
    total = across(high_ref[...], got, apply) + across(low_ref[...], got, apply)
    w_out_ref[...] = (w_ref[...].astype(F32) - total) * keep_ref[:, 0:1]


def sent_to_all(copies, axis):
    return lax.all_to_all(copies, axis, split_axis=0, concat_axis=0, tiled=True)


def on_device(hessian_inverse, weights, pruned):
    tile_rows, tile_cols = hessian_inverse.shape
    rows_w = weights.shape[0]
    n = pruned.shape[0]
    tiles = lax.axis_size("row")
    cap = 2 * n // tiles
    half = cap // 2
    at = jnp.stack([lax.axis_index("row"), lax.axis_index("col")]).astype(jnp.int32)
    weights = weights.T
    listed = pruned.reshape(1, n)
    edges = jnp.arange(tiles, dtype=jnp.int32) * tile_cols
    first = jnp.sum((listed < edges[:, None]).astype(jnp.int32), axis=1)
    length = rows_w + 2 * tile_rows
    hands = pl.pallas_call(
        pack_cols,
        out_shape=jax.ShapeDtypeStruct((cap, length), BF16),
        in_specs=[SMEM, VMEM, VMEM, VMEM],
        out_specs=VMEM,
        name="pack_cols",
    )(at, listed, hessian_inverse, weights)
    hands = sent_to_all(hands, "col")
    mine = n // tiles
    rows = pl.pallas_call(
        pack_rows,
        out_shape=jax.ShapeDtypeStruct((tiles, half * tile_cols // 128, 128), F32),
        in_specs=[SMEM, VMEM, VMEM],
        out_specs=VMEM,
        name="pack_rows",
    )(at, listed, hessian_inverse)
    low, high, pieces = pl.pallas_call(
        functools.partial(gather_hand, height=tile_rows, width=tile_cols),
        out_shape=(
            jax.ShapeDtypeStruct((mine // 2, length), BF16),
            jax.ShapeDtypeStruct((mine // 2, length), BF16),
            jax.ShapeDtypeStruct((tiles, cap // 4, 4 * mine), F32),
        ),
        in_specs=[SMEM, VMEM, VMEM],
        out_specs=(VMEM, VMEM, VMEM),
        name="gather_hand",
    )(at, listed, hands)
    pieces = sent_to_all(pieces, "row")
    side = math.isqrt(tiles)

    def along_x(value, d):
        return lax.ppermute(value, "col", [(c, c // side * side + (c + d) % side) for c in range(tiles)])

    def along_y(value, d):
        return lax.ppermute(value, "col", [(c, (c + d * side) % tiles) for c in range(tiles)])

    low = jnp.concatenate([low] + [along_x(low, d) for d in range(1, side)], axis=0)
    high = jnp.concatenate([high] + [along_y(high, d) for d in range(1, side)], axis=0)
    slab = pl.pallas_call(
        pack_slab,
        out_shape=jax.ShapeDtypeStruct((tiles, mine // 2, n), F32),
        in_specs=[SMEM, SMEM, VMEM],
        out_specs=VMEM,
        scratch_shapes=[pltpu.VMEM((n + cap, 128), F32), pltpu.VMEM((mine, n), F32)],
        name="pack_slab",
    )(first, at, pieces)
    slab = sent_to_all(slab, "col")
    cols = [low] + [along_y(low, d) for d in range(1, side)]
    cols += [high] + [along_x(high, d) for d in range(1, side)]
    rows = sent_to_all(rows, "row")
    twin = [(i, i ^ 1) for i in range(tiles)]
    slab_twin = lax.ppermute(slab, "row", twin)
    inverse = pl.pallas_call(
        invert,
        out_shape=jax.ShapeDtypeStruct((n, n), F32),
        in_specs=[SMEM, VMEM, VMEM],
        out_specs=VMEM,
        scratch_shapes=[pltpu.VMEM((n // 128, n, 128), F32)],
        name="invert",
    )(at, slab, slab_twin)
    rows_twin = lax.ppermute(rows, "row", twin)
    steps = 8
    block = rows_w // steps
    whole = lambda shape: pl.BlockSpec(shape, lambda i: (0,) * len(shape), pipeline_mode=pl.Buffered(1))
    strip = pl.BlockSpec((tile_cols, block), lambda i: (0, i))
    h_new, w_new = pl.pallas_call(
        update,
        grid=(steps,),
        out_shape=(
            jax.ShapeDtypeStruct(hessian_inverse.shape, F32),
            jax.ShapeDtypeStruct(weights.shape, F32),
        ),
        in_specs=[SMEM, SMEM] + [whole(a.shape) for a in (listed, inverse, rows, rows_twin, *cols, hessian_inverse)] + [strip],
        out_specs=(whole(hessian_inverse.shape), strip),
        scratch_shapes=[
            pltpu.VMEM((-(-tile_cols // 128), n + cap, 128), F32),
            pltpu.VMEM((tile_cols, n), BF16),
            pltpu.VMEM((tile_cols, n), BF16),
            pltpu.VMEM((tile_cols, 128), F32),
        ],
        name="update",
    )(first, at, listed, inverse, rows, rows_twin, *cols, hessian_inverse, weights)
    return h_new, w_new.T


def solution(mesh):
    specs = (P("row", "col"), P("row", "col"))

    return jax.shard_map(on_device, mesh=mesh, in_specs=(*specs, P()), out_specs=specs, check_vma=False)
```

profile of v0, /device:TPU:8, one launch (start us, length us, event | category | flops | bytes accessed | tf_op | source)
XLA Modules:
  0.0 137.7 jit_solution(13406124996196486877)
XLA Ops:
  0.6 0.0 copy-start.9
  0.6 0.6 pad_add_fusion.at_ref
  1.3 3.9 %pack_cols.1 = bf16[64,2880]{1,0:T(8,128)(2,1)} custom-call(s32[2]{0:T(128)} %pad_add_fusion.at_ref, s32[1,512]{1,0:T(1,128)} %bitcast.7, f32[416,416]{1,0:T(8,128)} %refs_8_.1, bf16[416,2048]{1,0:T(8,128)(2,1)} %bitcast.5), custom_call_target="tpu_custom_call" | custom-call | tf_op jit(solution)/shard_map/pack_cols/pallas_call | solution.py:300
  5.1 1.1 all_to_all.16
  6.2 15.0 %all_to_all.26 = bf16[16,4,2880]{2,1,0:T(4,128)(2,1)S(1)} all-to-all(bf16[16,4,2880]{2,1,0:T(4,128)(2,1)S(1)} %all_to_all.16), channel_id=1, replica_groups=mesh['row'=16,'col'=16] {'col'}, dimensions={0} | all-to-all | bytes 737280 | tf_op jit(solution)/shard_map/all_to_all | solution.py:284
  21.2 0.9 all_to_all.18.got_ref
  22.1 2.4 %gather_hand.1 = (bf16[16,2880]{1,0:T(8,128)(2,1)}, bf16[16,2880]{1,0:T(8,128)(2,1)}, f32[16,16,128]{2,1,0:T(8,128)}) custom-call(s32[2]{0:T(128)} %pad_add_fusion.at_ref, s32[1,512]{1,0:T(1,128)} %bitcast.8, bf16[64,2880]{1,0:T(8,128)(2,1)} %all_to_all.18.got_ref), custom_call_target="tpu_custom_call" | custom-call | tf_op jit(solution)/shard_map/gather_hand/pallas_call | solution.py:316
  24.6 8.7 %all-to-all-start.1 = ((f32[16,16,128]{2,1,0:T(8,128)}), f32[16,16,128]{2,1,0:T(8,128)S(1)}, u32[]{:S(2)}, u32[]{:S(2)}) async-start(f32[16,16,128]{2,1,0:T(8,128)} %get-tuple-element.7), calls=%async_computation.1 | async-start | bytes 262144 | tf_op jit(solution)/shard_map/all_to_all | solution.py:284
  33.3 0.8 convert_reduce_fusion.first_ref
  34.1 7.9 %all-to-all-done.1.got_ref = f32[16,16,128]{2,1,0:T(8,128)S(1)} async-done(((f32[16,16,128]{2,1,0:T(8,128)}), f32[16,16,128]{2,1,0:T(8,128)S(1)}, u32[]{:S(2)}, u32[]{:S(2)}) %all-to-all-start.1) | async-done | bytes 131104 | tf_op jit(solution)/shard_map/all_to_all | solution.py:284
  41.9 0.7 copy-done.6
  42.6 2.0 %pack_slab.1 = f32[16,16,512]{2,1,0:T(8,128)} custom-call(s32[16]{0:T(128)} %convert_reduce_fusion.first_ref, s32[2]{0:T(128)} %pad_add_fusion.at_ref, f32[16,16,128]{2,1,0:T(8,128)} %copy-done.6), custom_call_target="tpu_custom_call" | custom-call | tf_op jit(solution)/shard_map/pack_slab/pallas_call | solution.py:338
  44.6 5.6 %all-to-all-start.2 = ((f32[16,16,512]{2,1,0:T(8,128)}), f32[16,16,512]{2,1,0:T(8,128)S(1)}, u32[]{:S(2)}, u32[]{:S(2)}) async-start(f32[16,16,512]{2,1,0:T(8,128)} %pack_slab.1), calls=%async_computation.2 | async-start | bytes 1048576 | tf_op jit(solution)/shard_map/all_to_all | solution.py:284
  50.2 2.9 %pack_rows.1 = f32[16,104,128]{2,1,0:T(8,128)} custom-call(s32[2]{0:T(128)} %pad_add_fusion.at_ref, s32[1,512]{1,0:T(1,128)} %bitcast.9, f32[416,416]{1,0:T(8,128)} %refs_8_.1), custom_call_target="tpu_custom_call" | custom-call | tf_op jit(solution)/shard_map/pack_rows/pallas_call | solution.py:309
  53.1 2.7 %collective-permute-start.4 = (bf16[16,2880]{1,0:T(8,128)(2,1)}, bf16[16,2880]{1,0:T(8,128)(2,1)}, u32[]{:S(2)}, u32[]{:S(2)}) collective-permute-start(bf16[16,2880]{1,0:T(8,128)(2,1)} %get-tuple-element.8), channel_id=1, source_target_pairs={{0,3},{1,0},{2,1},{3,2},{4,7},{5,4},{6,5},{7,6},{8,11},{9,8},{10,9... | collective-permute-start | bytes 276488 | tf_op jit(solution)/shard_map/ppermute | solution.py:331
  55.8 0.8 collective-permute-start.3
  56.6 0.9 collective-permute-start.2
  57.5 0.5 collective-permute-start.10
  58.0 1.5 %collective-permute-start.8 = (bf16[16,2880]{1,0:T(8,128)(2,1)S(1)}, bf16[16,2880]{1,0:T(8,128)(2,1)S(1)}, u32[]{:S(2)}, u32[]{:S(2)}) collective-permute-start(bf16[16,2880]{1,0:T(8,128)(2,1)S(1)} %copy-done.8), channel_id=1, source_target_pairs={{0,4},{1,5},{2,6},{3,7},{4,8},{5,9},{6,10},{7,11},{8,12},{9,13},{1... | collective-permute-start | bytes 276488 | tf_op jit(solution)/shard_map/ppermute | solution.py:334
  59.5 0.9 constant_dynamic-update-slice_fusion.3
  60.4 0.0 all-to-all-done.2.own_ref
  60.4 3.6 %all-to-all-start.3 = ((f32[16,104,128]{2,1,0:T(8,128)}), f32[16,104,128]{2,1,0:T(8,128)S(1)}, u32[]{:S(2)}, u32[]{:S(2)}) async-start(f32[16,104,128]{2,1,0:T(8,128)} %pack_rows.1), calls=%async_computation.3 | async-start | bytes 1703936 | tf_op jit(solution)/shard_map/all_to_all | solution.py:284
  64.1 0.0 collective-permute-done.8
  64.1 3.4 %collective-permute-start.9 = (bf16[16,2880]{1,0:T(8,128)(2,1)S(1)}, bf16[16,2880]{1,0:T(8,128)(2,1)S(1)}, u32[]{:S(2)}, u32[]{:S(2)}) collective-permute-start(bf16[16,2880]{1,0:T(8,128)(2,1)S(1)} %copy-done.8), channel_id=1, source_target_pairs={{0,8},{1,9},{2,10},{3,11},{4,12},{5,13},{6,14},{7,15},{8,0},{9,1},... | collective-permute-start | bytes 276488 | tf_op jit(solution)/shard_map/ppermute | solution.py:334
  67.5 3.1 %collective-permute-done.9 = bf16[16,2880]{1,0:T(8,128)(2,1)S(1)} collective-permute-done((bf16[16,2880]{1,0:T(8,128)(2,1)S(1)}, bf16[16,2880]{1,0:T(8,128)(2,1)S(1)}, u32[]{:S(2)}, u32[]{:S(2)}) %collective-permute-start.9) | collective-permute-done | bytes 92192 | tf_op jit(solution)/shard_map/ppermute | solution.py:334
  70.7 2.5 %collective-permute-start.13 = (bf16[64,2880]{1,0:T(8,128)(2,1)S(1)}, bf16[64,2880]{1,0:T(8,128)(2,1)}, u32[]{:S(2)}, u32[]{:S(2)}) collective-permute-start(bf16[64,2880]{1,0:T(8,128)(2,1)S(1)} %constant_dynamic-update-slice_fusion.4.refs_4_), channel_id=1, source_target_pairs={{0,3},{1,0},{2,1},{3,2},{4,7},{5,4},{6,5},{7,6},{8,11},{9,8},{10,9... | collective-permute-start | bytes 1105928 | tf_op jit(solution)/shard_map/ppermute | solution.py:331
  73.2 1.5 %collective-permute-start.12 = (bf16[64,2880]{1,0:T(8,128)(2,1)S(1)}, bf16[64,2880]{1,0:T(8,128)(2,1)}, u32[]{:S(2)}, u32[]{:S(2)}) collective-permute-start(bf16[64,2880]{1,0:T(8,128)(2,1)S(1)} %constant_dynamic-update-slice_fusion.4.refs_4_), channel_id=1, source_target_pairs={{0,2},{1,3},{2,0},{3,1},{4,6},{5,7},{6,4},{7,5},{8,10},{9,11},{10,... | collective-permute-start | bytes 1105928 | tf_op jit(solution)/shard_map/ppermute | solution.py:331
  74.6 0.0 collective-permute-done.2
  74.7 0.1 collective-permute-start
  74.8 0.0 collective-permute-done.3
  74.8 0.6 copy-done.7
  75.4 10.4 %all-to-all-done.3.own_ref = f32[16,104,128]{2,1,0:T(8,128)S(1)} async-done(((f32[16,104,128]{2,1,0:T(8,128)}), f32[16,104,128]{2,1,0:T(8,128)S(1)}, u32[]{:S(2)}, u32[]{:S(2)}) %all-to-all-start.3) | async-done | bytes 852000 | tf_op jit(solution)/shard_map/all_to_all | solution.py:284
  85.8 2.7 %collective-permute-start.1 = (f32[16,104,128]{2,1,0:T(8,128)S(1)}, f32[16,104,128]{2,1,0:T(8,128)S(1)}, u32[]{:S(2)}, u32[]{:S(2)}) collective-permute-start(f32[16,104,128]{2,1,0:T(8,128)S(1)} %all-to-all-done.3.own_ref), channel_id=1, source_target_pairs={{0,16},{16,0},{32,48},{48,32},{64,80},{80,64},{96,112},{112,96},{1... | collective-permute-start | bytes 2555912 | tf_op jit(solution)/shard_map/ppermute | solution.py:360
  88.4 0.9 constant_dynamic-update-slice_fusion.1
  89.4 0.0 collective-permute-done.4
  89.4 1.9 %collective-permute-start.11 = (bf16[64,2880]{1,0:T(8,128)(2,1)S(1)}, bf16[64,2880]{1,0:T(8,128)(2,1)}, u32[]{:S(2)}, u32[]{:S(2)}) collective-permute-start(bf16[64,2880]{1,0:T(8,128)(2,1)S(1)} %constant_dynamic-update-slice_fusion.4.refs_4_), channel_id=1, source_target_pairs={{0,1},{1,2},{2,3},{3,0},{4,5},{5,6},{6,7},{7,4},{8,9},{9,10},{10,1... | collective-permute-start | bytes 1105928 | tf_op jit(solution)/shard_map/ppermute | solution.py:331
  91.2 0.9 constant_dynamic-update-slice_fusion.refs_0_
  92.1 1.7 %collective-permute-start.7 = (bf16[64,2880]{1,0:T(8,128)(2,1)S(1)}, bf16[64,2880]{1,0:T(8,128)(2,1)}, u32[]{:S(2)}, u32[]{:S(2)}) collective-permute-start(bf16[64,2880]{1,0:T(8,128)(2,1)S(1)} %constant_dynamic-update-slice_fusion.refs_0_), channel_id=1, source_target_pairs={{0,12},{1,13},{2,14},{3,15},{4,0},{5,1},{6,2},{7,3},{8,4},{9,5},{1... | collective-permute-start | bytes 1105928 | tf_op jit(solution)/shard_map/ppermute | solution.py:334
  93.9 2.0 %collective-permute-start.6 = (bf16[64,2880]{1,0:T(8,128)(2,1)S(1)}, bf16[64,2880]{1,0:T(8,128)(2,1)}, u32[]{:S(2)}, u32[]{:S(2)}) collective-permute-start(bf16[64,2880]{1,0:T(8,128)(2,1)S(1)} %constant_dynamic-update-slice_fusion.refs_0_), channel_id=1, source_target_pairs={{0,8},{1,9},{2,10},{3,11},{4,12},{5,13},{6,14},{7,15},{8,0},{9,1},... | collective-permute-start | bytes 1105928 | tf_op jit(solution)/shard_map/ppermute | solution.py:334
  95.8 0.0 collective-permute-done.other_ref
  95.8 2.3 %collective-permute-start.5 = (bf16[64,2880]{1,0:T(8,128)(2,1)S(1)}, bf16[64,2880]{1,0:T(8,128)(2,1)}, u32[]{:S(2)}, u32[]{:S(2)}) collective-permute-start(bf16[64,2880]{1,0:T(8,128)(2,1)S(1)} %constant_dynamic-update-slice_fusion.refs_0_), channel_id=1, source_target_pairs={{0,4},{1,5},{2,6},{3,7},{4,8},{5,9},{6,10},{7,11},{8,12},{9,13},{1... | collective-permute-start | bytes 1105928 | tf_op jit(solution)/shard_map/ppermute | solution.py:334
  98.2 25.6 %invert.1.inv_ref = f32[512,512]{1,0:T(8,128)} custom-call(s32[2]{0:T(128)} %pad_add_fusion.at_ref, f32[16,16,512]{2,1,0:T(8,128)} %copy-done.1, f32[16,16,512]{2,1,0:T(8,128)} %copy-done.5), custom_call_target="tpu_custom_call" | custom-call | tf_op jit(solution)/shard_map/invert/pallas_call | solution.py:352
  123.8 0.0 collective-permute-done.11.refs_5_
  123.8 0.0 collective-permute-done.7.refs_3_
  123.8 0.0 collective-permute-done.6.refs_2_
  123.8 0.0 collective-permute-done.1.other_ref
  123.9 0.9 copy-done.2
  124.8 12.9 %update.1 = (f32[416,416]{1,0:T(8,128)}, f32[416,2048]{1,0:T(8,128)}) custom-call(s32[16]{0:T(128)} %convert_reduce_fusion.first_ref, s32[2]{0:T(128)} %pad_add_fusion.at_ref, s32[1,512]{1,0:T(1,128)} %bitcast.10, f32[512,512]{1,0:T(8,128)} %invert.1.inv_ref, f32[16,104,128]{2,1,0:T(8,128)} %copy-done, f32[16,104,128]{2,1,0:T(8,128)} %copy-done.2, ...), custom_call_target="tpu_custom_call" | custom-call | tf_op jit(solution)/shard_map/update/pallas_call | solution.py:365
  (26 shorter events, 0.1 us)
Async XLA Ops:
  0.6 32.7 %copy-start.9 = (s32[512]{0:T(512)S(1)}, s32[512]{0:T(512)}, u32[]{:S(2)}) copy-start(s32[512]{0:T(512)} %param.5) | copy-start | bytes 6148
  24.6 32.9 %copy-start.8 = (bf16[16,2880]{1,0:T(8,128)(2,1)S(1)}, bf16[16,2880]{1,0:T(8,128)(2,1)}, u32[]{:S(2)}) copy-start(bf16[16,2880]{1,0:T(8,128)(2,1)} %get-tuple-element.9) | copy-start | bytes 276484
  24.6 17.4 %all-to-all-start.1 = ((f32[16,16,128]{2,1,0:T(8,128)}), f32[16,16,128]{2,1,0:T(8,128)S(1)}, u32[]{:S(2)}, u32[]{:S(2)}) async-start(f32[16,16,128]{2,1,0:T(8,128)} %get-tuple-element.7), calls=%async_computation.1 | async-start | bytes 262144 | tf_op jit(solution)/shard_map/all_to_all | solution.py:284
  41.9 0.7 copy-start.6
  44.6 15.8 %all-to-all-start.2 = ((f32[16,16,512]{2,1,0:T(8,128)}), f32[16,16,512]{2,1,0:T(8,128)S(1)}, u32[]{:S(2)}, u32[]{:S(2)}) async-start(f32[16,16,512]{2,1,0:T(8,128)} %pack_slab.1), calls=%async_computation.2 | async-start | bytes 1048576 | tf_op jit(solution)/shard_map/all_to_all | solution.py:284
  53.1 36.3 %collective-permute-start.4 = (bf16[16,2880]{1,0:T(8,128)(2,1)}, bf16[16,2880]{1,0:T(8,128)(2,1)}, u32[]{:S(2)}, u32[]{:S(2)}) collective-permute-start(bf16[16,2880]{1,0:T(8,128)(2,1)} %get-tuple-element.8), channel_id=1, source_target_pairs={{0,3},{1,0},{2,1},{3,2},{4,7},{5,4},{6,5},{7,6},{8,11},{9,8},{10,9... | collective-permute-start | bytes 276488 | tf_op jit(solution)/shard_map/ppermute | solution.py:331
  55.8 19.0 %collective-permute-start.3 = (bf16[16,2880]{1,0:T(8,128)(2,1)}, bf16[16,2880]{1,0:T(8,128)(2,1)S(1)}, u32[]{:S(2)}, u32[]{:S(2)}) collective-permute-start(bf16[16,2880]{1,0:T(8,128)(2,1)} %get-tuple-element.8), channel_id=1, source_target_pairs={{0,2},{1,3},{2,0},{3,1},{4,6},{5,7},{6,4},{7,5},{8,10},{9,11},{10,... | collective-permute-start | bytes 276488 | tf_op jit(solution)/shard_map/ppermute | solution.py:331
  56.6 18.0 %collective-permute-start.2 = (bf16[16,2880]{1,0:T(8,128)(2,1)}, bf16[16,2880]{1,0:T(8,128)(2,1)S(1)}, u32[]{:S(2)}, u32[]{:S(2)}) collective-permute-start(bf16[16,2880]{1,0:T(8,128)(2,1)} %get-tuple-element.8), channel_id=1, source_target_pairs={{0,1},{1,2},{2,3},{3,0},{4,5},{5,6},{6,7},{7,4},{8,9},{9,10},{10,1... | collective-permute-start | bytes 276488 | tf_op jit(solution)/shard_map/ppermute | solution.py:331
  57.5 13.2 %collective-permute-start.10 = (bf16[16,2880]{1,0:T(8,128)(2,1)S(1)}, bf16[16,2880]{1,0:T(8,128)(2,1)S(1)}, u32[]{:S(2)}, u32[]{:S(2)}) collective-permute-start(bf16[16,2880]{1,0:T(8,128)(2,1)S(1)} %copy-done.8), channel_id=1, source_target_pairs={{0,12},{1,13},{2,14},{3,15},{4,0},{5,1},{6,2},{7,3},{8,4},{9,5},{1... | collective-permute-start | bytes 276488 | tf_op jit(solution)/shard_map/ppermute | solution.py:334
  58.0 6.1 %collective-permute-start.8 = (bf16[16,2880]{1,0:T(8,128)(2,1)S(1)}, bf16[16,2880]{1,0:T(8,128)(2,1)S(1)}, u32[]{:S(2)}, u32[]{:S(2)}) collective-permute-start(bf16[16,2880]{1,0:T(8,128)(2,1)S(1)} %copy-done.8), channel_id=1, source_target_pairs={{0,4},{1,5},{2,6},{3,7},{4,8},{5,9},{6,10},{7,11},{8,12},{9,13},{1... | collective-permute-start | bytes 276488 | tf_op jit(solution)/shard_map/ppermute | solution.py:334
  60.4 37.8 %copy-start.1 = (f32[16,16,512]{2,1,0:T(8,128)}, f32[16,16,512]{2,1,0:T(8,128)S(1)}, u32[]{:S(2)}) copy-start(f32[16,16,512]{2,1,0:T(8,128)S(1)} %all-to-all-done.2.own_ref) | copy-start | bytes 1572868
  60.4 25.3 %all-to-all-start.3 = ((f32[16,104,128]{2,1,0:T(8,128)}), f32[16,104,128]{2,1,0:T(8,128)S(1)}, u32[]{:S(2)}, u32[]{:S(2)}) async-start(f32[16,104,128]{2,1,0:T(8,128)} %pack_rows.1), calls=%async_computation.3 | async-start | bytes 1703936 | tf_op jit(solution)/shard_map/all_to_all | solution.py:284
  64.1 6.6 %collective-permute-start.9 = (bf16[16,2880]{1,0:T(8,128)(2,1)S(1)}, bf16[16,2880]{1,0:T(8,128)(2,1)S(1)}, u32[]{:S(2)}, u32[]{:S(2)}) collective-permute-start(bf16[16,2880]{1,0:T(8,128)(2,1)S(1)} %copy-done.8), channel_id=1, source_target_pairs={{0,8},{1,9},{2,10},{3,11},{4,12},{5,13},{6,14},{7,15},{8,0},{9,1},... | collective-permute-start | bytes 276488 | tf_op jit(solution)/shard_map/ppermute | solution.py:334
  70.7 53.2 %copy-start.4 = (bf16[64,2880]{1,0:T(8,128)(2,1)}, bf16[64,2880]{1,0:T(8,128)(2,1)S(1)}, u32[]{:S(2)}) copy-start(bf16[64,2880]{1,0:T(8,128)(2,1)S(1)} %constant_dynamic-update-slice_fusion.4.refs_4_) | copy-start | bytes 1105924
  70.7 21.4 %collective-permute-start.13 = (bf16[64,2880]{1,0:T(8,128)(2,1)S(1)}, bf16[64,2880]{1,0:T(8,128)(2,1)}, u32[]{:S(2)}, u32[]{:S(2)}) collective-permute-start(bf16[64,2880]{1,0:T(8,128)(2,1)S(1)} %constant_dynamic-update-slice_fusion.4.refs_4_), channel_id=1, source_target_pairs={{0,3},{1,0},{2,1},{3,2},{4,7},{5,4},{6,5},{7,6},{8,11},{9,8},{10,9... | collective-permute-start | bytes 1105928 | tf_op jit(solution)/shard_map/ppermute | solution.py:331
  73.2 20.7 %collective-permute-start.12 = (bf16[64,2880]{1,0:T(8,128)(2,1)S(1)}, bf16[64,2880]{1,0:T(8,128)(2,1)}, u32[]{:S(2)}, u32[]{:S(2)}) collective-permute-start(bf16[64,2880]{1,0:T(8,128)(2,1)S(1)} %constant_dynamic-update-slice_fusion.4.refs_4_), channel_id=1, source_target_pairs={{0,2},{1,3},{2,0},{3,1},{4,6},{5,7},{6,4},{7,5},{8,10},{9,11},{10,... | collective-permute-start | bytes 1105928 | tf_op jit(solution)/shard_map/ppermute | solution.py:331
  74.7 21.2 %collective-permute-start = (f32[16,16,512]{2,1,0:T(8,128)S(1)}, f32[16,16,512]{2,1,0:T(8,128)S(1)}, u32[]{:S(2)}, u32[]{:S(2)}) collective-permute-start(f32[16,16,512]{2,1,0:T(8,128)S(1)} %all-to-all-done.2.own_ref), channel_id=1, source_target_pairs={{0,16},{16,0},{32,48},{48,32},{64,80},{80,64},{96,112},{112,96},{1... | collective-permute-start | bytes 1572872 | tf_op jit(solution)/shard_map/ppermute | solution.py:351
  74.8 0.6 copy-start.7
  85.8 38.1 %copy-start = (f32[16,104,128]{2,1,0:T(8,128)}, f32[16,104,128]{2,1,0:T(8,128)S(1)}, u32[]{:S(2)}) copy-start(f32[16,104,128]{2,1,0:T(8,128)S(1)} %all-to-all-done.3.own_ref) | copy-start | bytes 2555908
  85.8 38.1 %collective-permute-start.1 = (f32[16,104,128]{2,1,0:T(8,128)S(1)}, f32[16,104,128]{2,1,0:T(8,128)S(1)}, u32[]{:S(2)}, u32[]{:S(2)}) collective-permute-start(f32[16,104,128]{2,1,0:T(8,128)S(1)} %all-to-all-done.3.own_ref), channel_id=1, source_target_pairs={{0,16},{16,0},{32,48},{48,32},{64,80},{80,64},{96,112},{112,96},{1... | collective-permute-start | bytes 2555912 | tf_op jit(solution)/shard_map/ppermute | solution.py:360
  89.4 34.5 %collective-permute-start.11 = (bf16[64,2880]{1,0:T(8,128)(2,1)S(1)}, bf16[64,2880]{1,0:T(8,128)(2,1)}, u32[]{:S(2)}, u32[]{:S(2)}) collective-permute-start(bf16[64,2880]{1,0:T(8,128)(2,1)S(1)} %constant_dynamic-update-slice_fusion.4.refs_4_), channel_id=1, source_target_pairs={{0,1},{1,2},{2,3},{3,0},{4,5},{5,6},{6,7},{7,4},{8,9},{9,10},{10,1... | collective-permute-start | bytes 1105928 | tf_op jit(solution)/shard_map/ppermute | solution.py:331
  92.1 31.8 %copy-start.3 = (bf16[64,2880]{1,0:T(8,128)(2,1)}, bf16[64,2880]{1,0:T(8,128)(2,1)S(1)}, u32[]{:S(2)}) copy-start(bf16[64,2880]{1,0:T(8,128)(2,1)S(1)} %constant_dynamic-update-slice_fusion.refs_0_) | copy-start | bytes 1105924
  92.1 31.7 %collective-permute-start.7 = (bf16[64,2880]{1,0:T(8,128)(2,1)S(1)}, bf16[64,2880]{1,0:T(8,128)(2,1)}, u32[]{:S(2)}, u32[]{:S(2)}) collective-permute-start(bf16[64,2880]{1,0:T(8,128)(2,1)S(1)} %constant_dynamic-update-slice_fusion.refs_0_), channel_id=1, source_target_pairs={{0,12},{1,13},{2,14},{3,15},{4,0},{5,1},{6,2},{7,3},{8,4},{9,5},{1... | collective-permute-start | bytes 1105928 | tf_op jit(solution)/shard_map/ppermute | solution.py:334
  93.9 30.0 %collective-permute-start.6 = (bf16[64,2880]{1,0:T(8,128)(2,1)S(1)}, bf16[64,2880]{1,0:T(8,128)(2,1)}, u32[]{:S(2)}, u32[]{:S(2)}) collective-permute-start(bf16[64,2880]{1,0:T(8,128)(2,1)S(1)} %constant_dynamic-update-slice_fusion.refs_0_), channel_id=1, source_target_pairs={{0,8},{1,9},{2,10},{3,11},{4,12},{5,13},{6,14},{7,15},{8,0},{9,1},... | collective-permute-start | bytes 1105928 | tf_op jit(solution)/shard_map/ppermute | solution.py:334
  95.8 2.4 %copy-start.5 = (f32[16,16,512]{2,1,0:T(8,128)}, f32[16,16,512]{2,1,0:T(8,128)S(1)}, u32[]{:S(2)}) copy-start(f32[16,16,512]{2,1,0:T(8,128)S(1)} %collective-permute-done.other_ref) | copy-start | bytes 1572868
  95.8 28.0 %collective-permute-start.5 = (bf16[64,2880]{1,0:T(8,128)(2,1)S(1)}, bf16[64,2880]{1,0:T(8,128)(2,1)}, u32[]{:S(2)}, u32[]{:S(2)}) collective-permute-start(bf16[64,2880]{1,0:T(8,128)(2,1)S(1)} %constant_dynamic-update-slice_fusion.refs_0_), channel_id=1, source_target_pairs={{0,4},{1,5},{2,6},{3,7},{4,8},{5,9},{6,10},{7,11},{8,12},{9,13},{1... | collective-permute-start | bytes 1105928 | tf_op jit(solution)/shard_map/ppermute | solution.py:334
  123.9 0.9 copy-start.2
where the time goes:
time: 139 us; the launch traced here: 138 us
  Pallas kernels  49.8 us (36%)
  starting transfers between devices  42.4 us (31%)
  waiting for transfers between devices  21.4 us (15%)
  blocking collectives  15 us (11%)
  local copies, waits for them, and re-layouts  6.96 us (5%)
    pallas_call x1, Pallas kernels, on_device(): pl.pallas_call(invert, out_shape=jax.ShapeDtypeStruct((n, n), F32), in_sp...  25.6 us
    all_to_all x3, waiting for transfers between devices, sent_to_all(): return lax.all_to_all(copies, axis, split_axis=0, concat_axis=0, tiled=True)  18.2 us
    all_to_all x3, starting transfers between devices, sent_to_all(): return lax.all_to_all(copies, axis, split_axis=0, concat_axis=0, tiled=True)  17.9 us
    all_to_all x1, blocking collectives, sent_to_all(): return lax.all_to_all(copies, axis, split_axis=0, concat_axis=0, tiled=True)  15 us
    pallas_call x1, Pallas kernels, on_device(): pl.pallas_call(update, grid=(steps,), out_shape=(jax.ShapeDtypeStruct(hes...  12.9 us
    ppermute x6, starting transfers between devices, along_y(): lax.ppermute(value, 'col', [(c, (c + d * side) % tiles) for c in range(ti...  11.5 us
    ppermute x6, starting transfers between devices, along_x(): lax.ppermute(value, 'col', [(c, c // side * side + (c + d) % side) for c...  10.2 us
    unnamed x26, local copies, waits for them, and re-layouts  4.05 us
  transfers between devices with their start and end apart: 17, of which 3 were waited for; matrix products, arithmetic and copies ran while one was open for 3% of the time, Pallas kernels for 21%

commit v1 on v0

--- a/solution.py
+++ b/solution.py
@@ -40,28 +40,25 @@
     return lambda before: before + slot
 
 
-def dealt(cap, hands):
-    slot = lax.broadcasted_iota(jnp.int32, (cap, 1), 0)
-    each = cap // hands
-    hand, turn = slot // each, slot % each
-
-    def place(before):
-        return hand + hands * ((before - hand + hands - 1) // hands + turn)
-
-    return place
-
-
-def pack_rows(at_ref, pruned_ref, h_ref, rows_ref):
-    height, _ = h_ref.shape
-    pruned = pruned_ref[...]
-    tiles = rows_ref.shape[0]
-    cap = 2 * pruned.shape[1] // tiles
-    pick = one_hot(held(pruned, at_ref[0], height, in_turn(cap)), height)
+def dealt(before, tiles, slots):
+    slot = lax.broadcasted_iota(jnp.int32, (tiles * 2 * slots, 1), 0)
+    hand, second, turn = slot // (2 * slots), slot // slots % 2, slot % slots
+    return hand, second, (before - hand + tiles - 1) // tiles + turn
+
+
+def lanes_for(width):
+    return -(-width // 128) * 128
+
+
+def pack_rows(at_ref, pruned_ref, h_ref, mine_ref, other_ref):
+    height = h_ref.shape[0]
+    pick = one_hot(held(pruned_ref[...], at_ref[0], height, in_turn(2 * mine_ref.shape[0] * 128 // h_ref.shape[1])), height)
     rows = across(pick, h_ref[...], ((1,), (0,)), HIGH)
-    for core in range(2):
-        part = strips_of(rows[cap // 2 * core : cap // 2 * (core + 1)])
-        for d in range(core, tiles, 2):
-            rows_ref[d] = part
+    half = rows.shape[0] // 2
+    low, high = strips_of(rows[:half]), strips_of(rows[half:])
+    core = at_ref[0] % 2
+    mine_ref[...] = jnp.where(core == 0, low, high)
+    other_ref[...] = jnp.where(core == 0, high, low)
 
 
 def strips_of(rows):
@@ -88,41 +85,66 @@
 
 def pack_cols(at_ref, pruned_ref, h_ref, w_ref, out_ref):
     pruned = pruned_ref[...]
-    cap = out_ref.shape[0]
+    slots, half = out_ref.shape
     width = h_ref.shape[1]
-    tiles = 2 * pruned.shape[1] // cap
-    pick = one_hot(held(pruned, at_ref[1], width, dealt(cap, tiles)), width)
-    w = across(pick.astype(BF16), w_ref[...], ((1,), (0,))).astype(BF16)
+    tiles = slots // 8
+    pick = one_hot(held(pruned, at_ref[1], width, lambda before: dealt_places(before, tiles, 4)), width)
+    w = w_ref[...]
+    picked = pick.astype(BF16)
+    first = across(picked, w[:, :half], ((1,), (0,)))
+    last = across(picked, w[:, half:], ((1,), (0,)))
     c = across(pick, h_ref[...], ((1,), (1,)), HIGH)
-    c_high = c.astype(BF16)
-    c_low = (c - c_high.astype(F32)).astype(BF16)
-    out_ref[...] = jnp.concatenate([w, c_high, c_low], axis=1)
+    c_high = c.astype(BF16).astype(F32)
+    spare = jnp.zeros((slots, lanes_for(width) - width), F32)
+    last = jnp.concatenate([last, c_high, spare, c - c_high, spare], axis=1)
+    second = lax.broadcasted_iota(jnp.int32, (slots, 1), 0) // 4 % 2
+    out_ref[...] = jnp.where(second == 1, last, first).astype(BF16)
+
+
+def dealt_places(before, tiles, slots):
+    hand, _, turn = dealt(before, tiles, slots)
+    return hand + tiles * turn
 
 
 def gather_hand(at_ref, pruned_ref, got_ref, low_ref, high_ref, piece_ref, *, height, width):
     pruned = pruned_ref[...]
-    cap, length = got_ref.shape
+    slots, half = got_ref.shape
     tiles = piece_ref.shape[0]
-    mine = cap // 2
-    each = cap // tiles
-    slot = lax.broadcasted_iota(jnp.int32, (cap, 1), 0)
-    tile, turn = slot // each, slot % each
+    mine = pruned.shape[1] // tiles
+    slot = lax.broadcasted_iota(jnp.int32, (slots, 1), 0)
+    tile, second, turn = slot // 8, slot // 4 % 2, slot % 4
     before = jnp.sum(jnp.where(pruned < tile * width, 1, 0), axis=1, keepdims=True)
     after = jnp.sum(jnp.where(pruned < tile * width + width, 1, 0), axis=1, keepdims=True)
     hand = at_ref[1]
     turn = (before - hand + tiles - 1) // tiles + turn
-    place = hand + tiles * turn
-    turn = jnp.where(place < after, turn, -1)
-    out = across(one_hot(turn, mine).astype(BF16), got_ref[...], ((0,), (0,)))
-    cols = out[:, length - 2 * height : length - height] + out[:, length - height :]
+    turn = jnp.where(hand + tiles * turn < after, turn, -1)
+    got = got_ref[...]
+    parts = [
+        across(one_hot(jnp.where(second == part, turn, -1), mine).astype(BF16), got, ((0,), (0,)))
+        for part in range(2)
+    ]
+    wide = lanes_for(height)
+    c = parts[1][:, half - 2 * wide : half - 2 * wide + height] + parts[1][:, half - wide : half - wide + height]
+    cap = 2 * mine
     pick = one_hot(held(pruned, at_ref[0], height, in_turn(cap)), height)
-    piece = across(pick, cols, ((1,), (1,)), HIGH)
+    piece = across(pick, c, ((1,), (1,)), HIGH)
     quarter = cap // 4
     piece = jnp.concatenate([piece[quarter * i : quarter * i + quarter] for i in range(4)], axis=1)
     for d in range(tiles):
         piece_ref[d] = piece
-    low_ref[...] = out[: mine // 2].astype(BF16)
-    high_ref[...] = out[mine // 2 :].astype(BF16)
+    for part in range(2):
+        lanes = slice(half * part, half * part + half)
+        low_ref[:, lanes] = parts[part][: mine // 2].astype(BF16)
+        high_ref[:, lanes] = parts[part][mine // 2 :].astype(BF16)
+
+
+def join(*refs):
+    count = (len(refs) - 2) // 2
+    for path in range(2):
+        out = refs[2 * count + path]
+        rows = out.shape[0] // count
+        for d in range(count):
+            out[rows * d : rows * d + rows, :] = refs[count * path + d][...]
 
 
 def pack_slab(first_ref, at_ref, got_ref, out_ref, slab_ref, turned_ref):
@@ -155,18 +177,21 @@
     return jnp.broadcast_to(v[i : i + 1, :], v.shape)
 
 
-def invert_base(tiles):
+def base_factors(tiles, zero, work):
     width = tiles[0].shape[1]
     lane = lax.broadcasted_iota(jnp.int32, (8, width), 1)
     sub = lax.broadcasted_iota(jnp.int32, (8, width), 0)
     tiles = list(tiles)
     count = len(tiles)
+    lower, scaled = [], []
     for t in range(count):
         q = 8 * t
         own = tiles[t]
-        cols = [jnp.broadcast_to(own[:, q + j : q + j + 1], (8, width)) for j in range(8)]
+        cols = [jnp.broadcast_to(own[:, q + j : q + j + 1], (8, width)) + zero for j in range(8)]
         here = (lane >= q) & (lane < q + 8)
+        known = lane < q + 8
         panel = jnp.where(here, jnp.where(lane - q == sub, 1.0, 0.0), own)
+        lower.append(jnp.where(known, panel, 0.0))
         for j in range(0, 8, 2):
             k = j + 1
             a, b, b2, c = spread(cols[j], j), spread(cols[k], j), spread(cols[j], k), spread(cols[k], k)
@@ -183,18 +208,19 @@
             for m in range(j + 2, 8):
                 cols[m] = swept(cols[m])
             panel = swept(panel)
+        scaled.append(jnp.where(known, panel, 0.0))
         rows = [spread(panel, j) for j in range(8)]
-        for s in range(1, count):
-            s = (t + s) % count
+        if work and t % 2:
+            work.pop(0)()
+        for s in range(t + 1, count):
             v = tiles[s]
             p = [jnp.broadcast_to(v[:, q + j : q + j + 1], (8, width)) * rows[j] for j in range(8)]
             total = ((p[0] + p[1]) + (p[2] + p[3])) + ((p[4] + p[5]) + (p[6] + p[7]))
             tiles[s] = jnp.where(here, 0.0, v) - total
-        tiles[t] = panel
-    return tiles
-
-
-def invert(at_ref, own_ref, other_ref, out_ref, block_ref):
+    return jnp.concatenate(lower, axis=0), jnp.concatenate(scaled, axis=0)
+
+
+def invert(at_ref, zero_ref, own_ref, other_ref, out_ref, block_ref):
     tiles, half, n = own_ref.shape
     low_is_own = at_ref[0] % 2 == 0
     for t in range(tiles):
@@ -206,30 +232,42 @@
             block_ref[j, pl.ds(t + half * tiles, half, stride=tiles), :] = high[:, lanes]
     for j in range(n // 128):
         out_ref[:, 128 * j : 128 * j + 128] = block_ref[j]
+    zero = zero_ref[...]
+    work = []
     for lo in range(0, n, BASE):
-        hi = lo + BASE
-        diagonal = out_ref[lo:hi, lo:hi]
-        base = jnp.concatenate(invert_base([diagonal[s : s + 8] for s in range(0, BASE, 8)]), axis=0)
-        cols = out_ref[:, lo:hi]
-        rows = jnp.dot(base, out_ref[lo:hi, :], precision=HIGH, preferred_element_type=F32)
-        rows = jnp.concatenate([p for p in (rows[:, :lo], base, rows[:, hi:]) if p.shape[1]], axis=1)
-        lane = lax.broadcasted_iota(jnp.int32, (BASE, n), 1)
-        here = (lane >= lo) & (lane < hi)
-        for r in range(0, n, BASE):
-            if r != lo:
-                kept = jnp.where(here, 0.0, out_ref[r : r + BASE, :])
-                out_ref[r : r + BASE, :] = kept - jnp.dot(
-                    cols[r : r + BASE], rows, precision=HIGH, preferred_element_type=F32
-                )
-        out_ref[lo:hi, :] = rows
-
-
-def update(first_ref, at_ref, pruned_ref, inv_ref, own_ref, other_ref, *refs):
+        own = slice(lo, lo + BASE)
+        diagonal = out_ref[own, own]
+        lower, scaled = base_factors([diagonal[s : s + 8] for s in range(0, BASE, 8)], zero, work)
+        while work:
+            work.pop(0)()
+        base = across(lower, scaled, ((0,), (0,)), HIGH)
+        rows = {c: base if c == lo else across(base, out_ref[own, c : c + BASE], ((1,), (0,)), HIGH) for c in range(0, n, BASE)}
+        cols = {r: out_ref[r : r + BASE, own] for r in range(0, n, BASE) if r != lo}
+
+        def product(r, c, lo=lo, rows=rows, cols=cols):
+            at = (slice(r, r + BASE), slice(c, c + BASE))
+            total = across(cols[r], rows[c], ((1,), (0,)), HIGH)
+            out_ref[at] = -total if c == lo else out_ref[at] - total
+
+        for i in range(BASE, n, BASE):
+            r = (lo + i) % n
+            for c in range(0, n, BASE):
+                if r == c == lo + BASE:
+                    product(r, c)
+                else:
+                    work.append(functools.partial(product, r, c))
+        for c in range(0, n, BASE):
+            out_ref[own, c : c + BASE] = rows[c]
+    while work:
+        work.pop(0)()
+
+
+def update(first_ref, at_ref, pruned_ref, inv_ref, near_ref, far_ref, twin_near_ref, twin_far_ref, *refs):
     blocks, (h_ref, w_ref, h_out_ref, w_out_ref, panel_ref, high_ref, low_ref, keep_ref) = refs[:-8], refs[-8:]
     step = pl.program_id(0)
-    tiles = own_ref.shape[0]
     n = inv_ref.shape[0]
     width = h_ref.shape[1]
+    tiles = first_ref.shape[0]
     half = n // tiles
     side = len(blocks) // 2
     block = w_ref.shape[1]
@@ -241,11 +279,20 @@
 
     @pl.when(step == 0)
     def _():
-        low_is_own = at_ref[0] % 2 == 0
-        for t in range(tiles):
-            own, other = own_ref[t], other_ref[t]
-            place_strips(panel_ref, first_ref[t], jnp.where(low_is_own, own, other), half, width)
-            place_strips(panel_ref, first_ref[t] + half, jnp.where(low_is_own, other, own), half, width)
+        core, z = at_ref[0] % 2, at_ref[0] // 2
+        near = tiles // 4
+
+        def place(t, _):
+            apart = (t // 2) ^ z
+            for h in range(2):
+                mine = core == h
+                of = apart % near * 2 + (t % 2) ^ jnp.where(mine, core, 1 - core)
+                kept = jnp.where(apart < near, near_ref[of], far_ref[of])
+                sent = jnp.where(apart < near, twin_near_ref[of], twin_far_ref[of])
+                place_strips(panel_ref, first_ref[t] + h * half, jnp.where(mine, kept, sent), half, width)
+            return 0
+
+        lax.fori_loop(0, tiles, place, 0)
         panel = rows_at(panel_ref, 0, n, width)
         solved = jnp.dot(inv_ref[...], panel, precision=HIGH, preferred_element_type=F32)
         place_rows(panel_ref, 0, 0, solved)
@@ -267,7 +314,7 @@
         high = solved.astype(BF16)
         high_ref[...] = high
         low_ref[...] = (solved - high.astype(F32)).astype(BF16)
-        c_high, c_low = cols(rows_w, width), cols(rows_w + width, width)
+        c_high, c_low = cols(rows_w, width), cols(rows_w + lanes_for(width), width)
         total = across(high_ref[...], c_high, apply)
         total = total + (across(low_ref[...], c_high, apply) + across(high_ref[...], c_low, apply))
         h_out_ref[...] = h_ref[...] - total.T
@@ -296,23 +343,30 @@
     listed = pruned.reshape(1, n)
     edges = jnp.arange(tiles, dtype=jnp.int32) * tile_cols
     first = jnp.sum((listed < edges[:, None]).astype(jnp.int32), axis=1)
-    length = rows_w + 2 * tile_rows
+    length = rows_w + 2 * lanes_for(tile_rows)
     hands = pl.pallas_call(
         pack_cols,
-        out_shape=jax.ShapeDtypeStruct((cap, length), BF16),
+        out_shape=jax.ShapeDtypeStruct((8 * tiles, length // 2), BF16),
         in_specs=[SMEM, VMEM, VMEM, VMEM],
         out_specs=VMEM,
         name="pack_cols",
     )(at, listed, hessian_inverse, weights)
     hands = sent_to_all(hands, "col")
     mine = n // tiles
-    rows = pl.pallas_call(
+    strips = half * tile_cols // 128
+    mine_rows, other_rows = pl.pallas_call(
         pack_rows,
-        out_shape=jax.ShapeDtypeStruct((tiles, half * tile_cols // 128, 128), F32),
+        out_shape=(jax.ShapeDtypeStruct((strips, 128), F32),) * 2,
         in_specs=[SMEM, VMEM, VMEM],
-        out_specs=VMEM,
+        out_specs=(VMEM, VMEM),
         name="pack_rows",
     )(at, listed, hessian_inverse)
+
+    def swapped(value, mask):
+        return lax.ppermute(value, "row", [(i, i ^ mask) for i in range(tiles)])
+
+    rows = jnp.stack([mine_rows, swapped(other_rows, 1)])
+    rows = jnp.concatenate([rows, swapped(rows, 2)], axis=0)
     low, high, pieces = pl.pallas_call(
         functools.partial(gather_hand, height=tile_rows, width=tile_cols),
         out_shape=(
@@ -333,8 +387,9 @@
     def along_y(value, d):
         return lax.ppermute(value, "col", [(c, (c + d * side) % tiles) for c in range(tiles)])
 
-    low = jnp.concatenate([low] + [along_x(low, d) for d in range(1, side)], axis=0)
-    high = jnp.concatenate([high] + [along_y(high, d) for d in range(1, side)], axis=0)
+    rows = jnp.concatenate([rows, swapped(rows, 4)], axis=0)
+    lows = [low] + [along_x(low, d) for d in range(1, side)]
+    highs = [high] + [along_y(high, d) for d in range(1, side)]
     slab = pl.pallas_call(
         pack_slab,
         out_shape=jax.ShapeDtypeStruct((tiles, mine // 2, n), F32),
@@ -344,20 +399,27 @@
         name="pack_slab",
     )(first, at, pieces)
     slab = sent_to_all(slab, "col")
+    low, high = pl.pallas_call(
+        join,
+        out_shape=(jax.ShapeDtypeStruct((side * mine // 2, length), BF16),) * 2,
+        in_specs=[VMEM] * (2 * side),
+        out_specs=(VMEM, VMEM),
+        name="join",
+    )(*lows, *highs)
     cols = [low] + [along_y(low, d) for d in range(1, side)]
     cols += [high] + [along_x(high, d) for d in range(1, side)]
-    rows = sent_to_all(rows, "row")
-    twin = [(i, i ^ 1) for i in range(tiles)]
-    slab_twin = lax.ppermute(slab, "row", twin)
+    far_rows = swapped(rows, 8)
+    twin_rows = swapped(rows, 1)
+    slab_twin = swapped(slab, 1)
     inverse = pl.pallas_call(
         invert,
         out_shape=jax.ShapeDtypeStruct((n, n), F32),
-        in_specs=[SMEM, VMEM, VMEM],
+        in_specs=[SMEM, VMEM, VMEM, VMEM],
         out_specs=VMEM,
         scratch_shapes=[pltpu.VMEM((n // 128, n, 128), F32)],
         name="invert",
-    )(at, slab, slab_twin)
-    rows_twin = lax.ppermute(rows, "row", twin)
+    )(at, jnp.zeros((8, BASE), F32), slab, slab_twin)
+    twin_far = swapped(far_rows, 1)
     steps = 8
     block = rows_w // steps
     whole = lambda shape: pl.BlockSpec(shape, lambda i: (0,) * len(shape), pipeline_mode=pl.Buffered(1))
@@ -369,7 +431,7 @@
             jax.ShapeDtypeStruct(hessian_inverse.shape, F32),
             jax.ShapeDtypeStruct(weights.shape, F32),
         ),
-        in_specs=[SMEM, SMEM] + [whole(a.shape) for a in (listed, inverse, rows, rows_twin, *cols, hessian_inverse)] + [strip],
+        in_specs=[SMEM, SMEM] + [whole(a.shape) for a in (listed, inverse, rows, far_rows, twin_rows, twin_far, *cols, hessian_inverse)] + [strip],
         out_specs=(whole(hessian_inverse.shape), strip),
         scratch_shapes=[
             pltpu.VMEM((-(-tile_cols // 128), n + cap, 128), F32),
@@ -378,7 +440,9 @@
             pltpu.VMEM((tile_cols, 128), F32),
         ],
         name="update",
-    )(first, at, listed, inverse, rows, rows_twin, *cols, hessian_inverse, weights)
+    )(
+        first, at, listed, inverse, rows, far_rows, twin_rows, twin_far, *cols, hessian_inverse, weights
+    )
     return h_new, w_new.T
 
 

time: 139 us -> 138 us (level)
  the two profiles are of different devices: /device:TPU:8 before, /device:TPU:26 now
where the time goes in v1:
time: 138 us
  Pallas kernels  46.6 us (34%)
  starting transfers between devices  36.8 us (27%)
  waiting for transfers between devices  31.8 us (23%)
  blocking collectives  14.1 us (10%)
  other arithmetic  3.86 us (3%)
  local copies, waits for them, and re-layouts  3.31 us (2%)
    ppermute x7, waiting for transfers between devices, swapped(): return lax.ppermute(value, 'row', [(i, i ^ mask) for i in range(tiles)])  24.1 us
    pallas_call x1, Pallas kernels, on_device(): pl.pallas_call(invert, out_shape=jax.ShapeDtypeStruct((n, n), F32), in_sp...  19.1 us
    all_to_all x2, starting transfers between devices, sent_to_all(): return lax.all_to_all(copies, axis, split_axis=0, concat_axis=0, tiled=True)  15.4 us
    pallas_call x1, Pallas kernels, on_device(): pl.pallas_call(update, grid=(steps,), out_shape=(jax.ShapeDtypeStruct(hes...  14.3 us
    all_to_all x1, blocking collectives, sent_to_all(): return lax.all_to_all(copies, axis, split_axis=0, concat_axis=0, tiled=True)  14.1 us
    ppermute x6, starting transfers between devices, along_x(): lax.ppermute(value, 'col', [(c, c // side * side + (c + d) % side) for c...  9.42 us
    ppermute x6, starting transfers between devices, along_y(): lax.ppermute(value, 'col', [(c, (c + d * side) % tiles) for c in range(ti...  8.98 us
    all_to_all x2, waiting for transfers between devices, sent_to_all(): return lax.all_to_all(copies, axis, split_axis=0, concat_axis=0, tiled=True)  4.91 us
  transfers between devices with their start and end apart: 21, of which 6 were waited for; matrix products, arithmetic and copies ran while one was open for 3% of the time, Pallas kernels for 19%

profile of v1, /device:TPU:26, one launch (start us, length us, event | category | flops | bytes accessed | tf_op | source)
XLA Modules:
  0.0 137.5 jit_solution(11401916818621197671)
XLA Ops:
  0.6 0.0 copy-start.17
  0.6 0.6 pad_add_fusion.at_ref
  1.3 3.9 %pack_cols.1 = bf16[128,1536]{1,0:T(8,128)(2,1)} custom-call(s32[2]{0:T(128)} %pad_add_fusion.at_ref, s32[1,512]{1,0:T(1,128)} %bitcast.19, f32[416,416]{1,0:T(8,128)} %refs_8_.1, bf16[416,2048]{1,0:T(8,128)(2,1)} %bitcast.9), custom_call_target="tpu_custom_call" | custom-call | tf_op jit(solution)/shard_map/pack_cols/pallas_call | solution.py:347
  5.2 14.1 %all_to_all.21 = bf16[16,8,1536]{2,1,0:T(8,128)(2,1)} all-to-all(bf16[16,8,1536]{2,1,0:T(8,128)(2,1)} %bitcast.12), channel_id=1, replica_groups=mesh['row'=16,'col'=16] {'col'}, dimensions={0} | all-to-all | bytes 786432 | tf_op jit(solution)/shard_map/all_to_all | solution.py:331
  19.3 2.6 %gather_hand.1 = (bf16[16,3072]{1,0:T(8,128)(2,1)}, bf16[16,3072]{1,0:T(8,128)(2,1)}, f32[16,16,128]{2,1,0:T(8,128)}) custom-call(s32[2]{0:T(128)} %pad_add_fusion.at_ref, s32[1,512]{1,0:T(1,128)} %bitcast.20, bf16[128,1536]{1,0:T(8,128)(2,1)} %bitcast.11), custom_call_target="tpu_custom_call" | custom-call | tf_op jit(solution)/shard_map/gather_hand/pallas_call | solution.py:370
  21.9 8.7 %all-to-all-start.1 = ((f32[16,16,128]{2,1,0:T(8,128)}), f32[16,16,128]{2,1,0:T(8,128)S(1)}, u32[]{:S(2)}, u32[]{:S(2)}) async-start(f32[16,16,128]{2,1,0:T(8,128)} %get-tuple-element.11), calls=%async_computation.1 | async-start | bytes 262144 | tf_op jit(solution)/shard_map/all_to_all | solution.py:331
  30.6 2.6 %pack_rows.1 = (f32[104,128]{1,0:T(8,128)}, f32[104,128]{1,0:T(8,128)}) custom-call(s32[2]{0:T(128)} %pad_add_fusion.at_ref, s32[1,512]{1,0:T(1,128)} %bitcast.21, f32[416,416]{1,0:T(8,128)} %refs_8_.1), custom_call_target="tpu_custom_call" | custom-call | tf_op jit(solution)/shard_map/pack_rows/pallas_call | solution.py:357
  33.2 0.4 collective-permute-start.1
  33.7 0.7 convert_reduce_fusion.first_ref
  34.4 4.9 %all-to-all-done.1.got_ref = f32[16,16,128]{2,1,0:T(8,128)S(1)} async-done(((f32[16,16,128]{2,1,0:T(8,128)}), f32[16,16,128]{2,1,0:T(8,128)S(1)}, u32[]{:S(2)}, u32[]{:S(2)}) %all-to-all-start.1) | async-done | bytes 131104 | tf_op jit(solution)/shard_map/all_to_all | solution.py:331
  39.3 0.7 copy-done.3
  39.9 2.0 %pack_slab.1 = f32[16,16,512]{2,1,0:T(8,128)} custom-call(s32[16]{0:T(128)} %convert_reduce_fusion.first_ref, s32[2]{0:T(128)} %pad_add_fusion.at_ref, f32[16,16,128]{2,1,0:T(8,128)} %copy-done.3), custom_call_target="tpu_custom_call" | custom-call | tf_op jit(solution)/shard_map/pack_slab/pallas_call | solution.py:393
  41.9 6.7 %all-to-all-start.2 = ((f32[16,16,512]{2,1,0:T(8,128)}), f32[16,16,512]{2,1,0:T(8,128)S(1)}, u32[]{:S(2)}, u32[]{:S(2)}) async-start(f32[16,16,512]{2,1,0:T(8,128)} %pack_slab.1), calls=%async_computation.2 | async-start | bytes 1048576 | tf_op jit(solution)/shard_map/all_to_all | solution.py:331
  48.7 0.0 collective-permute-done.1
  48.7 0.8 pad_maximum_fusion.2
  49.5 0.7 collective-permute-start.2
  50.1 4.6 %collective-permute-done.2 = f32[2,104,128]{2,1,0:T(8,128)S(1)} collective-permute-done((f32[2,104,128]{2,1,0:T(8,128)S(1)}, f32[2,104,128]{2,1,0:T(8,128)S(1)}, u32[]{:S(2)}, u32[]{:S(2)}) %collective-permute-start.2) | collective-permute-done | bytes 106528 | tf_op jit(solution)/shard_map/ppermute | solution.py:366
  54.7 0.8 pad_maximum_fusion.1
  55.6 0.8 collective-permute-start.3
  56.4 0.6 collective-permute-start.9
  56.9 2.4 %collective-permute-start.8 = (bf16[16,3072]{1,0:T(8,128)(2,1)S(1)}, bf16[16,3072]{1,0:T(8,128)(2,1)S(1)}, u32[]{:S(2)}, u32[]{:S(2)}) collective-permute-start(bf16[16,3072]{1,0:T(8,128)(2,1)S(1)} %copy-done.9), channel_id=1, source_target_pairs={{0,2},{1,3},{2,0},{3,1},{4,6},{5,7},{6,4},{7,5},{8,10},{9,11},{10,... | collective-permute-start | bytes 294920 | tf_op jit(solution)/shard_map/ppermute | solution.py:385
  59.3 1.8 %collective-permute-start.7 = (bf16[16,3072]{1,0:T(8,128)(2,1)S(1)}, bf16[16,3072]{1,0:T(8,128)(2,1)S(1)}, u32[]{:S(2)}, u32[]{:S(2)}) collective-permute-start(bf16[16,3072]{1,0:T(8,128)(2,1)S(1)} %copy-done.9), channel_id=1, source_target_pairs={{0,1},{1,2},{2,3},{3,0},{4,5},{5,6},{6,7},{7,4},{8,9},{9,10},{10,1... | collective-permute-start | bytes 294920 | tf_op jit(solution)/shard_map/ppermute | solution.py:385
  61.1 0.8 collective-permute-start.12
  61.9 5.7 %collective-permute-done.3 = f32[4,104,128]{2,1,0:T(8,128)S(1)} collective-permute-done((f32[4,104,128]{2,1,0:T(8,128)S(1)}, f32[4,104,128]{2,1,0:T(8,128)S(1)}, u32[]{:S(2)}, u32[]{:S(2)}) %collective-permute-start.3) | collective-permute-done | bytes 213024 | tf_op jit(solution)/shard_map/ppermute | solution.py:366
  67.7 1.4 %collective-permute-start.11 = (bf16[16,3072]{1,0:T(8,128)(2,1)S(1)}, bf16[16,3072]{1,0:T(8,128)(2,1)S(1)}, u32[]{:S(2)}, u32[]{:S(2)}) collective-permute-start(bf16[16,3072]{1,0:T(8,128)(2,1)S(1)} %copy-done.10), channel_id=1, source_target_pairs={{0,8},{1,9},{2,10},{3,11},{4,12},{5,13},{6,14},{7,15},{8,0},{9,1},... | collective-permute-start | bytes 294920 | tf_op jit(solution)/shard_map/ppermute | solution.py:388
  69.1 2.1 %collective-permute-start.10 = (bf16[16,3072]{1,0:T(8,128)(2,1)S(1)}, bf16[16,3072]{1,0:T(8,128)(2,1)S(1)}, u32[]{:S(2)}, u32[]{:S(2)}) collective-permute-start(bf16[16,3072]{1,0:T(8,128)(2,1)S(1)} %copy-done.10), channel_id=1, source_target_pairs={{0,4},{1,5},{2,6},{3,7},{4,8},{5,9},{6,10},{7,11},{8,12},{9,13},{1... | collective-permute-start | bytes 294920 | tf_op jit(solution)/shard_map/ppermute | solution.py:388
  71.2 0.0 copy-start
  71.2 0.1 collective-permute-start
  71.3 0.9 pad_maximum_fusion.near_ref
  72.2 0.0 copy-start.13
  72.2 0.9 collective-permute-start.4
  73.1 0.2 collective-permute-start.5
  73.3 0.6 collective-permute-done.11.refs_6_
  73.9 0.0 collective-permute-done.10.refs_5_
  73.9 0.6 copy-done.15
  74.5 0.6 copy-done.16
  75.2 2.1 %join.1 = (bf16[64,3072]{1,0:T(8,128)(2,1)}, bf16[64,3072]{1,0:T(8,128)(2,1)}) custom-call(bf16[16,3072]{1,0:T(8,128)(2,1)} %get-tuple-element.14.refs_0_, bf16[16,3072]{1,0:T(8,128)(2,1)} %copy-done.13, bf16[16,3072]{1,0:T(8,128)(2,1)} %copy-done.12, bf16[16,3072]{1,0:T(8,128)(2,1)} %copy-done.11, bf16[16,3072]{1,0:T(8,128)(2,1)} %get-tuple-element.15.refs_4_, ...), custom_call_target="tpu_custom_call" | custom-call | tf_op jit(solution)/shard_map/join/pallas_call | solution.py:402
  77.3 1.8 %collective-permute-start.15 = (bf16[64,3072]{1,0:T(8,128)(2,1)}, bf16[64,3072]{1,0:T(8,128)(2,1)S(1)}, u32[]{:S(2)}, u32[]{:S(2)}) collective-permute-start(bf16[64,3072]{1,0:T(8,128)(2,1)} %get-tuple-element.16.refs_0_), channel_id=1, source_target_pairs={{0,12},{1,13},{2,14},{3,15},{4,0},{5,1},{6,2},{7,3},{8,4},{9,5},{1... | collective-permute-start | bytes 1179656 | tf_op jit(solution)/shard_map/ppermute | solution.py:388
  79.1 2.1 %collective-permute-start.14 = (bf16[64,3072]{1,0:T(8,128)(2,1)}, bf16[64,3072]{1,0:T(8,128)(2,1)S(1)}, u32[]{:S(2)}, u32[]{:S(2)}) collective-permute-start(bf16[64,3072]{1,0:T(8,128)(2,1)} %get-tuple-element.16.refs_0_), channel_id=1, source_target_pairs={{0,8},{1,9},{2,10},{3,11},{4,12},{5,13},{6,14},{7,15},{8,0},{9,1},... | collective-permute-start | bytes 1179656 | tf_op jit(solution)/shard_map/ppermute | solution.py:388
  81.3 13.7 %collective-permute-done.4.far_ref = f32[8,104,128]{2,1,0:T(8,128)S(1)} collective-permute-done((f32[8,104,128]{2,1,0:T(8,128)S(1)}, f32[8,104,128]{2,1,0:T(8,128)S(1)}, u32[]{:S(2)}, u32[]{:S(2)}) %collective-permute-start.4) | collective-permute-done | bytes 426016 | tf_op jit(solution)/shard_map/ppermute | solution.py:366
  95.0 0.7 collective-permute-start.13
  95.7 2.2 %collective-permute-done.15.refs_3_ = bf16[64,3072]{1,0:T(8,128)(2,1)S(1)} collective-permute-done((bf16[64,3072]{1,0:T(8,128)(2,1)}, bf16[64,3072]{1,0:T(8,128)(2,1)S(1)}, u32[]{:S(2)}, u32[]{:S(2)}) %collective-permute-start.15) | collective-permute-done | bytes 393248 | tf_op jit(solution)/shard_map/ppermute | solution.py:388
  97.9 2.9 %collective-permute-start.17 = (bf16[64,3072]{1,0:T(8,128)(2,1)}, bf16[64,3072]{1,0:T(8,128)(2,1)}, u32[]{:S(2)}, u32[]{:S(2)}) collective-permute-start(bf16[64,3072]{1,0:T(8,128)(2,1)} %get-tuple-element.17.refs_4_), channel_id=1, source_target_pairs={{0,2},{1,3},{2,0},{3,1},{4,6},{5,7},{6,4},{7,5},{8,10},{9,11},{10,... | collective-permute-start | bytes 1179656 | tf_op jit(solution)/shard_map/ppermute | solution.py:385
  100.8 1.8 %collective-permute-start.16 = (bf16[64,3072]{1,0:T(8,128)(2,1)}, bf16[64,3072]{1,0:T(8,128)(2,1)}, u32[]{:S(2)}, u32[]{:S(2)}) collective-permute-start(bf16[64,3072]{1,0:T(8,128)(2,1)} %get-tuple-element.17.refs_4_), channel_id=1, source_target_pairs={{0,1},{1,2},{2,3},{3,0},{4,5},{5,6},{6,7},{7,4},{8,9},{9,10},{10,1... | collective-permute-start | bytes 1179656 | tf_op jit(solution)/shard_map/ppermute | solution.py:385
  102.6 0.6 broadcast_in_dim.4.zero_ref
  103.2 19.1 %invert.1.inv_ref = f32[512,512]{1,0:T(8,128)} custom-call(s32[2]{0:T(128)} %pad_add_fusion.at_ref, f32[8,128]{1,0:T(8,128)} %broadcast_in_dim.4.zero_ref, f32[16,16,512]{2,1,0:T(8,128)} %copy-done, f32[16,16,512]{2,1,0:T(8,128)} %copy-done.2), custom_call_target="tpu_custom_call" | custom-call | tf_op jit(solution)/shard_map/invert/pallas_call | solution.py:414
  122.4 0.8 copy-done.6
  123.2 14.3 %update.1 = (f32[416,416]{1,0:T(8,128)}, f32[416,2048]{1,0:T(8,128)}) custom-call(s32[16]{0:T(128)} %convert_reduce_fusion.first_ref, s32[2]{0:T(128)} %pad_add_fusion.at_ref, s32[1,512]{1,0:T(1,128)} %bitcast.22, f32[512,512]{1,0:T(8,128)} %invert.1.inv_ref, f32[8,104,128]{2,1,0:T(8,128)} %copy-done.1, f32[8,104,128]{2,1,0:T(8,128)} %copy-done.4, ...), custom_call_target="tpu_custom_call" | custom-call | tf_op jit(solution)/shard_map/update/pallas_call | solution.py:427
  (45 shorter events, 0.1 us)
Async XLA Ops:
  0.6 33.0 %copy-start.17 = (s32[512]{0:T(512)S(1)}, s32[512]{0:T(512)}, u32[]{:S(2)}) copy-start(s32[512]{0:T(512)} %param.5) | copy-start | bytes 6148
  21.9 34.5 %copy-start.9 = (bf16[16,3072]{1,0:T(8,128)(2,1)S(1)}, bf16[16,3072]{1,0:T(8,128)(2,1)}, u32[]{:S(2)}) copy-start(bf16[16,3072]{1,0:T(8,128)(2,1)} %get-tuple-element.14.refs_0_) | copy-start | bytes 294916
  21.9 39.2 %copy-start.10 = (bf16[16,3072]{1,0:T(8,128)(2,1)S(1)}, bf16[16,3072]{1,0:T(8,128)(2,1)}, u32[]{:S(2)}) copy-start(bf16[16,3072]{1,0:T(8,128)(2,1)} %get-tuple-element.15.refs_4_) | copy-start | bytes 294916
  21.9 17.4 %all-to-all-start.1 = ((f32[16,16,128]{2,1,0:T(8,128)}), f32[16,16,128]{2,1,0:T(8,128)S(1)}, u32[]{:S(2)}, u32[]{:S(2)}) async-start(f32[16,16,128]{2,1,0:T(8,128)} %get-tuple-element.11), calls=%async_computation.1 | async-start | bytes 262144 | tf_op jit(solution)/shard_map/all_to_all | solution.py:331
  33.2 15.4 %collective-permute-start.1 = (f32[104,128]{1,0:T(8,128)}, f32[104,128]{1,0:T(8,128)S(1)}, u32[]{:S(2)}, u32[]{:S(2)}) collective-permute-start(f32[104,128]{1,0:T(8,128)} %get-tuple-element.13), channel_id=1, source_target_pairs={{0,16},{16,0},{32,48},{48,32},{64,80},{80,64},{96,112},{112,96},{1... | collective-permute-start | bytes 159752 | tf_op jit(solution)/shard_map/ppermute | solution.py:366
  39.3 0.7 copy-start.3
  41.9 29.3 %all-to-all-start.2 = ((f32[16,16,512]{2,1,0:T(8,128)}), f32[16,16,512]{2,1,0:T(8,128)S(1)}, u32[]{:S(2)}, u32[]{:S(2)}) async-start(f32[16,16,512]{2,1,0:T(8,128)} %pack_slab.1), calls=%async_computation.2 | async-start | bytes 1048576 | tf_op jit(solution)/shard_map/all_to_all | solution.py:331
  49.5 5.3 %collective-permute-start.2 = (f32[2,104,128]{2,1,0:T(8,128)S(1)}, f32[2,104,128]{2,1,0:T(8,128)S(1)}, u32[]{:S(2)}, u32[]{:S(2)}) collective-permute-start(f32[2,104,128]{2,1,0:T(8,128)S(1)} %pad_maximum_fusion.2), channel_id=1, source_target_pairs={{0,32},{16,48},{32,0},{48,16},{64,96},{80,112},{96,64},{112,80},{1... | collective-permute-start | bytes 319496 | tf_op jit(solution)/shard_map/ppermute | solution.py:366
  55.6 12.1 %collective-permute-start.3 = (f32[4,104,128]{2,1,0:T(8,128)S(1)}, f32[4,104,128]{2,1,0:T(8,128)S(1)}, u32[]{:S(2)}, u32[]{:S(2)}) collective-permute-start(f32[4,104,128]{2,1,0:T(8,128)S(1)} %pad_maximum_fusion.1), channel_id=1, source_target_pairs={{0,64},{16,80},{32,96},{48,112},{64,0},{80,16},{96,32},{112,48},{1... | collective-permute-start | bytes 638984 | tf_op jit(solution)/shard_map/ppermute | solution.py:366
  56.4 12.7 %collective-permute-start.9 = (bf16[16,3072]{1,0:T(8,128)(2,1)S(1)}, bf16[16,3072]{1,0:T(8,128)(2,1)S(1)}, u32[]{:S(2)}, u32[]{:S(2)}) collective-permute-start(bf16[16,3072]{1,0:T(8,128)(2,1)S(1)} %copy-done.9), channel_id=1, source_target_pairs={{0,3},{1,0},{2,1},{3,2},{4,7},{5,4},{6,5},{7,6},{8,11},{9,8},{10,9... | collective-permute-start | bytes 294920 | tf_op jit(solution)/shard_map/ppermute | solution.py:385
  56.9 14.2 %collective-permute-start.8 = (bf16[16,3072]{1,0:T(8,128)(2,1)S(1)}, bf16[16,3072]{1,0:T(8,128)(2,1)S(1)}, u32[]{:S(2)}, u32[]{:S(2)}) collective-permute-start(bf16[16,3072]{1,0:T(8,128)(2,1)S(1)} %copy-done.9), channel_id=1, source_target_pairs={{0,2},{1,3},{2,0},{3,1},{4,6},{5,7},{6,4},{7,5},{8,10},{9,11},{10,... | collective-permute-start | bytes 294920 | tf_op jit(solution)/shard_map/ppermute | solution.py:385
  59.3 12.9 %collective-permute-start.7 = (bf16[16,3072]{1,0:T(8,128)(2,1)S(1)}, bf16[16,3072]{1,0:T(8,128)(2,1)S(1)}, u32[]{:S(2)}, u32[]{:S(2)}) collective-permute-start(bf16[16,3072]{1,0:T(8,128)(2,1)S(1)} %copy-done.9), channel_id=1, source_target_pairs={{0,1},{1,2},{2,3},{3,0},{4,5},{5,6},{6,7},{7,4},{8,9},{9,10},{10,1... | collective-permute-start | bytes 294920 | tf_op jit(solution)/shard_map/ppermute | solution.py:385
  61.1 12.0 %collective-permute-start.12 = (bf16[16,3072]{1,0:T(8,128)(2,1)S(1)}, bf16[16,3072]{1,0:T(8,128)(2,1)S(1)}, u32[]{:S(2)}, u32[]{:S(2)}) collective-permute-start(bf16[16,3072]{1,0:T(8,128)(2,1)S(1)} %copy-done.10), channel_id=1, source_target_pairs={{0,12},{1,13},{2,14},{3,15},{4,0},{5,1},{6,2},{7,3},{8,4},{9,5},{1... | collective-permute-start | bytes 294920 | tf_op jit(solution)/shard_map/ppermute | solution.py:388
  67.7 6.2 %collective-permute-start.11 = (bf16[16,3072]{1,0:T(8,128)(2,1)S(1)}, bf16[16,3072]{1,0:T(8,128)(2,1)S(1)}, u32[]{:S(2)}, u32[]{:S(2)}) collective-permute-start(bf16[16,3072]{1,0:T(8,128)(2,1)S(1)} %copy-done.10), channel_id=1, source_target_pairs={{0,8},{1,9},{2,10},{3,11},{4,12},{5,13},{6,14},{7,15},{8,0},{9,1},... | collective-permute-start | bytes 294920 | tf_op jit(solution)/shard_map/ppermute | solution.py:388
  69.1 4.8 %copy-start.11 = (bf16[16,3072]{1,0:T(8,128)(2,1)}, bf16[16,3072]{1,0:T(8,128)(2,1)S(1)}, u32[]{:S(2)}) copy-start(bf16[16,3072]{1,0:T(8,128)(2,1)S(1)} %collective-permute-done.9.refs_3_) | copy-start | bytes 294916
  69.1 4.8 %collective-permute-start.10 = (bf16[16,3072]{1,0:T(8,128)(2,1)S(1)}, bf16[16,3072]{1,0:T(8,128)(2,1)S(1)}, u32[]{:S(2)}, u32[]{:S(2)}) collective-permute-start(bf16[16,3072]{1,0:T(8,128)(2,1)S(1)} %copy-done.10), channel_id=1, source_target_pairs={{0,4},{1,5},{2,6},{3,7},{4,8},{5,9},{6,10},{7,11},{8,12},{9,13},{1... | collective-permute-start | bytes 294920 | tf_op jit(solution)/shard_map/ppermute | solution.py:388
  71.2 2.7 %copy-start.12 = (bf16[16,3072]{1,0:T(8,128)(2,1)}, bf16[16,3072]{1,0:T(8,128)(2,1)S(1)}, u32[]{:S(2)}) copy-start(bf16[16,3072]{1,0:T(8,128)(2,1)S(1)} %collective-permute-done.8.refs_2_) | copy-start | bytes 294916
  71.2 32.0 %copy-start = (f32[16,16,512]{2,1,0:T(8,128)}, f32[16,16,512]{2,1,0:T(8,128)S(1)}, u32[]{:S(2)}) copy-start(f32[16,16,512]{2,1,0:T(8,128)S(1)} %all-to-all-done.2.own_ref) | copy-start | bytes 1572868
  71.2 29.6 %collective-permute-start = (f32[16,16,512]{2,1,0:T(8,128)S(1)}, f32[16,16,512]{2,1,0:T(8,128)S(1)}, u32[]{:S(2)}, u32[]{:S(2)}) collective-permute-start(f32[16,16,512]{2,1,0:T(8,128)S(1)} %all-to-all-done.2.own_ref), channel_id=1, source_target_pairs={{0,16},{16,0},{32,48},{48,32},{64,80},{80,64},{96,112},{112,96},{1... | collective-permute-start | bytes 1572872 | tf_op jit(solution)/shard_map/ppermute | solution.py:366
  72.2 50.1 %copy-start.1 = (f32[8,104,128]{2,1,0:T(8,128)}, f32[8,104,128]{2,1,0:T(8,128)S(1)}, u32[]{:S(2)}) copy-start(f32[8,104,128]{2,1,0:T(8,128)S(1)} %pad_maximum_fusion.near_ref) | copy-start | bytes 1277956
  72.2 1.7 %copy-start.13 = (bf16[16,3072]{1,0:T(8,128)(2,1)}, bf16[16,3072]{1,0:T(8,128)(2,1)S(1)}, u32[]{:S(2)}) copy-start(bf16[16,3072]{1,0:T(8,128)(2,1)S(1)} %collective-permute-done.7.refs_1_) | copy-start | bytes 294916
  72.2 22.8 %collective-permute-start.4 = (f32[8,104,128]{2,1,0:T(8,128)S(1)}, f32[8,104,128]{2,1,0:T(8,128)S(1)}, u32[]{:S(2)}, u32[]{:S(2)}) collective-permute-start(f32[8,104,128]{2,1,0:T(8,128)S(1)} %pad_maximum_fusion.near_ref), channel_id=1, source_target_pairs={{0,128},{16,144},{32,160},{48,176},{64,192},{80,208},{96,224},{112... | collective-permute-start | bytes 1277960 | tf_op jit(solution)/shard_map/ppermute | solution.py:366
  73.1 0.8 copy-start.14
  73.1 21.9 %collective-permute-start.5 = (f32[8,104,128]{2,1,0:T(8,128)S(1)}, f32[8,104,128]{2,1,0:T(8,128)S(1)}, u32[]{:S(2)}, u32[]{:S(2)}) collective-permute-start(f32[8,104,128]{2,1,0:T(8,128)S(1)} %pad_maximum_fusion.near_ref), channel_id=1, source_target_pairs={{0,16},{16,0},{32,48},{48,32},{64,80},{80,64},{96,112},{112,96},{1... | collective-permute-start | bytes 1277960 | tf_op jit(solution)/shard_map/ppermute | solution.py:366
  73.9 0.6 copy-start.15
  74.5 0.6 copy-start.16
  77.3 20.6 %collective-permute-start.15 = (bf16[64,3072]{1,0:T(8,128)(2,1)}, bf16[64,3072]{1,0:T(8,128)(2,1)S(1)}, u32[]{:S(2)}, u32[]{:S(2)}) collective-permute-start(bf16[64,3072]{1,0:T(8,128)(2,1)} %get-tuple-element.16.refs_0_), channel_id=1, source_target_pairs={{0,12},{1,13},{2,14},{3,15},{4,0},{5,1},{6,2},{7,3},{8,4},{9,5},{1... | collective-permute-start | bytes 1179656 | tf_op jit(solution)/shard_map/ppermute | solution.py:388
  79.1 18.8 %collective-permute-start.14 = (bf16[64,3072]{1,0:T(8,128)(2,1)}, bf16[64,3072]{1,0:T(8,128)(2,1)S(1)}, u32[]{:S(2)}, u32[]{:S(2)}) collective-permute-start(bf16[64,3072]{1,0:T(8,128)(2,1)} %get-tuple-element.16.refs_0_), channel_id=1, source_target_pairs={{0,8},{1,9},{2,10},{3,11},{4,12},{5,13},{6,14},{7,15},{8,0},{9,1},... | collective-permute-start | bytes 1179656 | tf_op jit(solution)/shard_map/ppermute | solution.py:388
  95.0 27.3 %copy-start.4 = (f32[8,104,128]{2,1,0:T(8,128)}, f32[8,104,128]{2,1,0:T(8,128)S(1)}, u32[]{:S(2)}) copy-start(f32[8,104,128]{2,1,0:T(8,128)S(1)} %collective-permute-done.4.far_ref) | copy-start | bytes 1277956
  95.0 27.3 %collective-permute-start.6 = (f32[8,104,128]{2,1,0:T(8,128)S(1)}, f32[8,104,128]{2,1,0:T(8,128)S(1)}, u32[]{:S(2)}, u32[]{:S(2)}) collective-permute-start(f32[8,104,128]{2,1,0:T(8,128)S(1)} %collective-permute-done.4.far_ref), channel_id=1, source_target_pairs={{0,16},{16,0},{32,48},{48,32},{64,80},{80,64},{96,112},{112,96},{1... | collective-permute-start | bytes 1277960 | tf_op jit(solution)/shard_map/ppermute | solution.py:366
  95.0 27.3 %copy-start.5 = (f32[8,104,128]{2,1,0:T(8,128)}, f32[8,104,128]{2,1,0:T(8,128)S(1)}, u32[]{:S(2)}) copy-start(f32[8,104,128]{2,1,0:T(8,128)S(1)} %collective-permute-done.5.twin_near_ref) | copy-start | bytes 1277956
  95.0 27.3 %collective-permute-start.13 = (bf16[64,3072]{1,0:T(8,128)(2,1)}, bf16[64,3072]{1,0:T(8,128)(2,1)}, u32[]{:S(2)}, u32[]{:S(2)}) collective-permute-start(bf16[64,3072]{1,0:T(8,128)(2,1)} %get-tuple-element.16.refs_0_), channel_id=1, source_target_pairs={{0,4},{1,5},{2,6},{3,7},{4,8},{5,9},{6,10},{7,11},{8,12},{9,13},{1... | collective-permute-start | bytes 1179656 | tf_op jit(solution)/shard_map/ppermute | solution.py:388
  97.9 24.5 %copy-start.7 = (bf16[64,3072]{1,0:T(8,128)(2,1)}, bf16[64,3072]{1,0:T(8,128)(2,1)S(1)}, u32[]{:S(2)}) copy-start(bf16[64,3072]{1,0:T(8,128)(2,1)S(1)} %collective-permute-done.15.refs_3_) | copy-start | bytes 1179652
  97.9 24.4 %collective-permute-start.18 = (bf16[64,3072]{1,0:T(8,128)(2,1)}, bf16[64,3072]{1,0:T(8,128)(2,1)}, u32[]{:S(2)}, u32[]{:S(2)}) collective-permute-start(bf16[64,3072]{1,0:T(8,128)(2,1)} %get-tuple-element.17.refs_4_), channel_id=1, source_target_pairs={{0,3},{1,0},{2,1},{3,2},{4,7},{5,4},{6,5},{7,6},{8,11},{9,8},{10,9... | collective-permute-start | bytes 1179656 | tf_op jit(solution)/shard_map/ppermute | solution.py:385
  97.9 24.5 %copy-start.8 = (bf16[64,3072]{1,0:T(8,128)(2,1)}, bf16[64,3072]{1,0:T(8,128)(2,1)S(1)}, u32[]{:S(2)}) copy-start(bf16[64,3072]{1,0:T(8,128)(2,1)S(1)} %collective-permute-done.14.refs_2_) | copy-start | bytes 1179652
  97.9 24.4 %collective-permute-start.17 = (bf16[64,3072]{1,0:T(8,128)(2,1)}, bf16[64,3072]{1,0:T(8,128)(2,1)}, u32[]{:S(2)}, u32[]{:S(2)}) collective-permute-start(bf16[64,3072]{1,0:T(8,128)(2,1)} %get-tuple-element.17.refs_4_), channel_id=1, source_target_pairs={{0,2},{1,3},{2,0},{3,1},{4,6},{5,7},{6,4},{7,5},{8,10},{9,11},{10,... | collective-permute-start | bytes 1179656 | tf_op jit(solution)/shard_map/ppermute | solution.py:385
  100.8 2.4 %copy-start.2 = (f32[16,16,512]{2,1,0:T(8,128)}, f32[16,16,512]{2,1,0:T(8,128)S(1)}, u32[]{:S(2)}) copy-start(f32[16,16,512]{2,1,0:T(8,128)S(1)} %collective-permute-done.other_ref) | copy-start | bytes 1572868
  100.8 21.5 %collective-permute-start.16 = (bf16[64,3072]{1,0:T(8,128)(2,1)}, bf16[64,3072]{1,0:T(8,128)(2,1)}, u32[]{:S(2)}, u32[]{:S(2)}) collective-permute-start(bf16[64,3072]{1,0:T(8,128)(2,1)} %get-tuple-element.17.refs_4_), channel_id=1, source_target_pairs={{0,1},{1,2},{2,3},{3,0},{4,5},{5,6},{6,7},{7,4},{8,9},{9,10},{10,1... | collective-permute-start | bytes 1179656 | tf_op jit(solution)/shard_map/ppermute | solution.py:385
  122.4 0.8 copy-start.6

commit v2 on v1

--- a/solution.py
+++ b/solution.py
@@ -15,6 +15,7 @@
 VMEM = pl.BlockSpec(memory_space=pltpu.VMEM)
 SMEM = pl.BlockSpec(memory_space=pltpu.SMEM)
 BASE = 128
+BLOCK = 256
 
 
 def across(a, b, dims, precision=None):
@@ -50,15 +51,16 @@
     return -(-width // 128) * 128
 
 
-def pack_rows(at_ref, pruned_ref, h_ref, mine_ref, other_ref):
+def pack_rows(at_ref, pruned_ref, h_ref, rows_ref):
     height = h_ref.shape[0]
-    pick = one_hot(held(pruned_ref[...], at_ref[0], height, in_turn(2 * mine_ref.shape[0] * 128 // h_ref.shape[1])), height)
+    tiles = rows_ref.shape[0]
+    cap = 2 * pruned_ref.shape[1] // tiles
+    pick = one_hot(held(pruned_ref[...], at_ref[0], height, in_turn(cap)), height)
     rows = across(pick, h_ref[...], ((1,), (0,)), HIGH)
-    half = rows.shape[0] // 2
-    low, high = strips_of(rows[:half]), strips_of(rows[half:])
-    core = at_ref[0] % 2
-    mine_ref[...] = jnp.where(core == 0, low, high)
-    other_ref[...] = jnp.where(core == 0, high, low)
+    for core in range(2):
+        part = strips_of(rows[cap // 2 * core : cap // 2 * (core + 1)])
+        for d in range(core, tiles, 2):
+            rows_ref[d] = part
 
 
 def strips_of(rows):
@@ -161,18 +163,6 @@
         out_ref[d] = slab
 
 
-def place_rows(ref, at, start, value):
-    rows, width = value.shape
-    for j in range(0, width, 128):
-        strip = value[:, j : j + 128]
-        ref[at + j // 128, pl.ds(start, rows), 0 : strip.shape[1]] = strip
-
-
-def rows_at(ref, start, rows, width):
-    strips = [ref[j, pl.ds(start, rows), :] for j in range(ref.shape[0])]
-    return jnp.concatenate(strips, axis=1)[:, :width]
-
-
 def spread(v, i):
     return jnp.broadcast_to(v[i : i + 1, :], v.shape)
 
@@ -220,111 +210,103 @@
     return jnp.concatenate(lower, axis=0), jnp.concatenate(scaled, axis=0)
 
 
-def invert(at_ref, zero_ref, own_ref, other_ref, out_ref, block_ref):
+def invert(at_ref, own_ref, other_ref, out_ref, zero_ref):
     tiles, half, n = own_ref.shape
     low_is_own = at_ref[0] % 2 == 0
     for t in range(tiles):
         own, other = own_ref[t], other_ref[t]
         low, high = jnp.where(low_is_own, own, other), jnp.where(low_is_own, other, own)
-        for j in range(n // 128):
-            lanes = slice(128 * j, 128 * j + 128)
-            block_ref[j, pl.ds(t, half, stride=tiles), :] = low[:, lanes]
-            block_ref[j, pl.ds(t + half * tiles, half, stride=tiles), :] = high[:, lanes]
-    for j in range(n // 128):
-        out_ref[:, 128 * j : 128 * j + 128] = block_ref[j]
+        for j in range(n // BASE):
+            lanes = slice(BASE * j, BASE * j + BASE)
+            out_ref[j, pl.ds(t, half, stride=tiles), :] = low[:, lanes]
+            out_ref[j, pl.ds(t + half * tiles, half, stride=tiles), :] = high[:, lanes]
+    zero_ref[...] = jnp.zeros_like(zero_ref)
     zero = zero_ref[...]
+    blocks = n // BASE
     work = []
-    for lo in range(0, n, BASE):
-        own = slice(lo, lo + BASE)
-        diagonal = out_ref[own, own]
+    for k in range(blocks):
+        own = slice(BASE * k, BASE * k + BASE)
+        diagonal = out_ref[k, own, :]
         lower, scaled = base_factors([diagonal[s : s + 8] for s in range(0, BASE, 8)], zero, work)
         while work:
             work.pop(0)()
         base = across(lower, scaled, ((0,), (0,)), HIGH)
-        rows = {c: base if c == lo else across(base, out_ref[own, c : c + BASE], ((1,), (0,)), HIGH) for c in range(0, n, BASE)}
-        cols = {r: out_ref[r : r + BASE, own] for r in range(0, n, BASE) if r != lo}
-
-        def product(r, c, lo=lo, rows=rows, cols=cols):
-            at = (slice(r, r + BASE), slice(c, c + BASE))
+        rows = [base if c == k else across(base, out_ref[c, own, :], ((1,), (0,)), HIGH) for c in range(blocks)]
+        cols = [out_ref[k, BASE * r : BASE * r + BASE, :] for r in range(blocks)]
+
+        def product(r, c, k=k, rows=rows, cols=cols):
+            at = (c, slice(BASE * r, BASE * r + BASE))
             total = across(cols[r], rows[c], ((1,), (0,)), HIGH)
-            out_ref[at] = -total if c == lo else out_ref[at] - total
-
-        for i in range(BASE, n, BASE):
-            r = (lo + i) % n
-            for c in range(0, n, BASE):
-                if r == c == lo + BASE:
+            out_ref[at] = -total if c == k else out_ref[at] - total
+
+        for i in range(1, blocks):
+            r = (k + i) % blocks
+            for c in range(blocks):
+                if r == c == k + 1:
                     product(r, c)
                 else:
                     work.append(functools.partial(product, r, c))
-        for c in range(0, n, BASE):
-            out_ref[own, c : c + BASE] = rows[c]
+        for c in range(blocks):
+            out_ref[c, own, :] = rows[c]
     while work:
         work.pop(0)()
 
 
-def update(first_ref, at_ref, pruned_ref, inv_ref, near_ref, far_ref, twin_near_ref, twin_far_ref, *refs):
-    blocks, (h_ref, w_ref, h_out_ref, w_out_ref, panel_ref, high_ref, low_ref, keep_ref) = refs[:-8], refs[-8:]
-    step = pl.program_id(0)
-    n = inv_ref.shape[0]
+def update(first_ref, at_ref, pruned_ref, inv_ref, own_ref, other_ref, *refs):
+    blocks, (h_ref, w_ref, h_out, w_out, panel_ref, w_new_ref, h_new_ref, sems) = refs[:-8], refs[-8:]
+    strips, n, _ = inv_ref.shape
     width = h_ref.shape[1]
     tiles = first_ref.shape[0]
     half = n // tiles
     side = len(blocks) // 2
-    block = w_ref.shape[1]
-    rows_w = block * pl.num_programs(0)
+    rows_w = w_ref.shape[1]
+    steps = rows_w // BLOCK
+    low_is_own = at_ref[0] % 2 == 0
+    for t in range(tiles):
+        own, other = own_ref[t], other_ref[t]
+        place_strips(panel_ref, first_ref[t], jnp.where(low_is_own, own, other), half, width)
+        place_strips(panel_ref, first_ref[t] + half, jnp.where(low_is_own, other, own), half, width)
+    panel = jnp.concatenate([panel_ref[j, 0:n, :] for j in range(panel_ref.shape[0])], axis=1).T[:width, :]
+    x, y = at_ref[1] % side, at_ref[1] // side
+    hands = []
+    for path in range(2):
+        for far in range(side):
+            for near in range(side):
+                dx, dy = (near, far) if path == 0 else (far, near)
+                hand = (y + side - dy) % side * side + (x + side - dx) % side
+                hands.append(hand + path * (n // 2))
+    inverse = jnp.concatenate(
+        [
+            jnp.concatenate([inv_ref[j, pl.ds(h, n // tiles // 2, stride=tiles), :] for h in hands], axis=0)
+            for j in range(strips)
+        ],
+        axis=1,
+    )
+    solved = across(panel, inverse, ((1,), (1,)), HIGH)
+    high = solved.astype(BF16)
+    low = (solved - high.astype(F32)).astype(BF16)
+    unit = lax.broadcasted_iota(jnp.int32, (width, n), 0) + at_ref[1] * width
+    keep = 1.0 - jnp.sum(jnp.where(unit == pruned_ref[...], 1.0, 0.0), axis=1, keepdims=True)
     apply = ((1,), (0,))
 
     def cols(start, size):
-        return jnp.concatenate([b[:, pl.ds(start, size)] for b in blocks], axis=0)
-
-    @pl.when(step == 0)
-    def _():
-        core, z = at_ref[0] % 2, at_ref[0] // 2
-        near = tiles // 4
-
-        def place(t, _):
-            apart = (t // 2) ^ z
-            for h in range(2):
-                mine = core == h
-                of = apart % near * 2 + (t % 2) ^ jnp.where(mine, core, 1 - core)
-                kept = jnp.where(apart < near, near_ref[of], far_ref[of])
-                sent = jnp.where(apart < near, twin_near_ref[of], twin_far_ref[of])
-                place_strips(panel_ref, first_ref[t] + h * half, jnp.where(mine, kept, sent), half, width)
-            return 0
-
-        lax.fori_loop(0, tiles, place, 0)
-        panel = rows_at(panel_ref, 0, n, width)
-        solved = jnp.dot(inv_ref[...], panel, precision=HIGH, preferred_element_type=F32)
-        place_rows(panel_ref, 0, 0, solved)
-        x, y = at_ref[1] % side, at_ref[1] // side
-        hands = []
-        for path in range(2):
-            for far in range(side):
-                for near in range(side):
-                    dx, dy = (near, far) if path == 0 else (far, near)
-                    hand = (y + side - dy) % side * side + (x + side - dx) % side
-                    hands.append(hand + path * (n // 2))
-        solved = jnp.concatenate(
-            [
-                jnp.concatenate([panel_ref[j, pl.ds(h, n // tiles // 2, stride=tiles), :] for h in hands], axis=0)
-                for j in range(panel_ref.shape[0])
-            ],
-            axis=1,
-        ).T[:width, :]
-        high = solved.astype(BF16)
-        high_ref[...] = high
-        low_ref[...] = (solved - high.astype(F32)).astype(BF16)
-        c_high, c_low = cols(rows_w, width), cols(rows_w + lanes_for(width), width)
-        total = across(high_ref[...], c_high, apply)
-        total = total + (across(low_ref[...], c_high, apply) + across(high_ref[...], c_low, apply))
-        h_out_ref[...] = h_ref[...] - total.T
-        unit = lax.broadcasted_iota(jnp.int32, (width, n), 0) + at_ref[1] * width
-        hits = jnp.sum(jnp.where(unit == pruned_ref[...], 1.0, 0.0), axis=1, keepdims=True)
-        keep_ref[...] = jnp.broadcast_to(1.0 - hits, keep_ref.shape)
-
-    got = cols(pl.multiple_of(step * block, block), block)
-    total = across(high_ref[...], got, apply) + across(low_ref[...], got, apply)
-    w_out_ref[...] = (w_ref[...].astype(F32) - total) * keep_ref[:, 0:1]
+        return jnp.concatenate([b[:, start : start + size] for b in blocks], axis=0)
+
+    copies = []
+    for i in range(steps):
+        at = slice(BLOCK * i, BLOCK * i + BLOCK)
+        got = cols(BLOCK * i, BLOCK)
+        total = across(high, got, apply) + across(low, got, apply)
+        w_new_ref[:, at] = (w_ref[:, at].astype(F32) - total) * keep
+        copies.append(pltpu.make_async_copy(w_new_ref.at[:, at], w_out.at[:, at], sems.at[i]))
+        copies[-1].start()
+    c_high, c_low = cols(rows_w, width), cols(rows_w + lanes_for(width), width)
+    total = across(high, c_high, apply) + (across(low, c_high, apply) + across(high, c_low, apply))
+    h_new_ref[...] = h_ref[...] - total.T
+    copies.append(pltpu.make_async_copy(h_new_ref, h_out, sems.at[steps]))
+    copies[-1].start()
+    for copy in copies:
+        copy.wait()
 
 
 def sent_to_all(copies, axis):
@@ -353,20 +335,17 @@
     )(at, listed, hessian_inverse, weights)
     hands = sent_to_all(hands, "col")
     mine = n // tiles
-    strips = half * tile_cols // 128
-    mine_rows, other_rows = pl.pallas_call(
+    rows = pl.pallas_call(
         pack_rows,
-        out_shape=(jax.ShapeDtypeStruct((strips, 128), F32),) * 2,
+        out_shape=jax.ShapeDtypeStruct((tiles, half * tile_cols // 128, 128), F32),
         in_specs=[SMEM, VMEM, VMEM],
-        out_specs=(VMEM, VMEM),
+        out_specs=VMEM,
         name="pack_rows",
     )(at, listed, hessian_inverse)
 
     def swapped(value, mask):
         return lax.ppermute(value, "row", [(i, i ^ mask) for i in range(tiles)])
 
-    rows = jnp.stack([mine_rows, swapped(other_rows, 1)])
-    rows = jnp.concatenate([rows, swapped(rows, 2)], axis=0)
     low, high, pieces = pl.pallas_call(
         functools.partial(gather_hand, height=tile_rows, width=tile_cols),
         out_shape=(
@@ -387,7 +366,6 @@
     def along_y(value, d):
         return lax.ppermute(value, "col", [(c, (c + d * side) % tiles) for c in range(tiles)])
 
-    rows = jnp.concatenate([rows, swapped(rows, 4)], axis=0)
     lows = [low] + [along_x(low, d) for d in range(1, side)]
     highs = [high] + [along_y(high, d) for d in range(1, side)]
     slab = pl.pallas_call(
@@ -408,41 +386,34 @@
     )(*lows, *highs)
     cols = [low] + [along_y(low, d) for d in range(1, side)]
     cols += [high] + [along_x(high, d) for d in range(1, side)]
-    far_rows = swapped(rows, 8)
-    twin_rows = swapped(rows, 1)
+    rows = sent_to_all(rows, "row")
     slab_twin = swapped(slab, 1)
     inverse = pl.pallas_call(
         invert,
-        out_shape=jax.ShapeDtypeStruct((n, n), F32),
-        in_specs=[SMEM, VMEM, VMEM, VMEM],
+        out_shape=jax.ShapeDtypeStruct((n // BASE, n, BASE), F32),
+        in_specs=[SMEM, VMEM, VMEM],
         out_specs=VMEM,
-        scratch_shapes=[pltpu.VMEM((n // 128, n, 128), F32)],
+        scratch_shapes=[pltpu.VMEM((8, BASE), F32)],
         name="invert",
-    )(at, jnp.zeros((8, BASE), F32), slab, slab_twin)
-    twin_far = swapped(far_rows, 1)
-    steps = 8
-    block = rows_w // steps
-    whole = lambda shape: pl.BlockSpec(shape, lambda i: (0,) * len(shape), pipeline_mode=pl.Buffered(1))
-    strip = pl.BlockSpec((tile_cols, block), lambda i: (0, i))
+    )(at, slab, slab_twin)
+    rows_twin = swapped(rows, 1)
+    anywhere = pl.BlockSpec(memory_space=pl.ANY)
     h_new, w_new = pl.pallas_call(
         update,
-        grid=(steps,),
         out_shape=(
             jax.ShapeDtypeStruct(hessian_inverse.shape, F32),
             jax.ShapeDtypeStruct(weights.shape, F32),
         ),
-        in_specs=[SMEM, SMEM] + [whole(a.shape) for a in (listed, inverse, rows, far_rows, twin_rows, twin_far, *cols, hessian_inverse)] + [strip],
-        out_specs=(whole(hessian_inverse.shape), strip),
+        in_specs=[SMEM, SMEM] + [VMEM] * (6 + len(cols)),
+        out_specs=(anywhere, anywhere),
         scratch_shapes=[
             pltpu.VMEM((-(-tile_cols // 128), n + cap, 128), F32),
-            pltpu.VMEM((tile_cols, n), BF16),
-            pltpu.VMEM((tile_cols, n), BF16),
-            pltpu.VMEM((tile_cols, 128), F32),
+            pltpu.VMEM(weights.shape, F32),
+            pltpu.VMEM(hessian_inverse.shape, F32),
+            pltpu.SemaphoreType.DMA((rows_w // BLOCK + 1,)),
         ],
         name="update",
-    )(
-        first, at, listed, inverse, rows, far_rows, twin_rows, twin_far, *cols, hessian_inverse, weights
-    )
+    )(first, at, listed, inverse, rows, rows_twin, *cols, hessian_inverse, weights)
     return h_new, w_new.T
 
 

time: 138 us -> 144 us (1.043)
  waiting for transfers between devices: 31.8 us -> 42.4 us
  Pallas kernels: 46.6 us -> 41.9 us
  starting transfers between devices: 36.8 us -> 39.9 us
  other arithmetic: 3.86 us -> 1.43 us
    ppermute x7 -> x2, waiting for transfers between devices: 24.1 us -> 0.01 us  [swapped(): return lax.ppermute(value, 'row', [(i, i ^ mask) for i in range(tiles)])]
    all_to_all x2 -> x3, waiting for transfers between devices: 4.91 us -> 25.9 us  [sent_to_all(): return lax.all_to_all(copies, axis, split_axis=0, concat_axis=0, tiled=True)]
    ppermute x6, waiting for transfers between devices: 2.83 us -> 16 us  [along_y(): lax.ppermute(value, 'col', [(c, (c + d * side) % tiles) for c in range(ti...]
    pallas_call x3, Pallas kernels: 36 us -> 31.3 us  [the longest x1 18.9 us: on_device(): pl.pallas_call(invert, out_shape=jax.ShapeDtypeStruct((n // BASE, n, BASE...]
    all_to_all x2 -> x3, starting transfers between devices: 15.4 us -> 19.1 us  [sent_to_all(): return lax.all_to_all(copies, axis, split_axis=0, concat_axis=0, tiled=True)]
    concatenate x2 -> x0, other arithmetic: 1.72 us -> none  [the longest x1 0.9 us: on_device(): rows = jnp.concatenate([rows, swapped(rows, 4)], axis=0)]
    ppermute x7 -> x2, starting transfers between devices: 3 us -> 2.69 us  [swapped(): return lax.ppermute(value, 'row', [(i, i ^ mask) for i in range(tiles)])]
  transfers between devices with their start and end apart: 21 -> 17, of which waited for: 6 -> 7; matrix products, arithmetic and copies ran while one was open for 3% -> 1% of each run, Pallas kernels for 19% -> 17%
where the time goes in v2:
time: 144 us
  waiting for transfers between devices  42.4 us (29%)
  Pallas kernels  41.9 us (29%)
  starting transfers between devices  39.9 us (28%)
  blocking collectives  14.1 us (10%)
  local copies, waits for them, and re-layouts  2.86 us (2%)
    all_to_all x3, waiting for transfers between devices, sent_to_all(): return lax.all_to_all(copies, axis, split_axis=0, concat_axis=0, tiled=True)  25.9 us
    all_to_all x3, starting transfers between devices, sent_to_all(): return lax.all_to_all(copies, axis, split_axis=0, concat_axis=0, tiled=True)  19.1 us
    pallas_call x1, Pallas kernels, on_device(): pl.pallas_call(invert, out_shape=jax.ShapeDtypeStruct((n // BASE, n, BASE...  18.9 us
    ppermute x6, waiting for transfers between devices, along_y(): lax.ppermute(value, 'col', [(c, (c + d * side) % tiles) for c in range(ti...  16 us
    all_to_all x1, blocking collectives, sent_to_all(): return lax.all_to_all(copies, axis, split_axis=0, concat_axis=0, tiled=True)  14.1 us
    ppermute x6, starting transfers between devices, along_y(): lax.ppermute(value, 'col', [(c, (c + d * side) % tiles) for c in range(ti...  9.64 us
    pallas_call x1, Pallas kernels, on_device(): pl.pallas_call(update, out_shape=(jax.ShapeDtypeStruct(hessian_inverse.sh...  9.53 us
    ppermute x6, starting transfers between devices, along_x(): lax.ppermute(value, 'col', [(c, c // side * side + (c + d) % side) for c...  8.48 us
  transfers between devices with their start and end apart: 17, of which 7 were waited for; matrix products, arithmetic and copies ran while one was open for 1% of the time, Pallas kernels for 17%

profile of v2, /device:TPU:26, one launch (start us, length us, event | category | flops | bytes accessed | tf_op | source)
XLA Modules:
  0.0 143.6 jit_solution(15983670239962579372)
XLA Ops:
  0.6 0.0 copy-start.15
  0.6 0.7 pad_add_fusion.at_ref
  1.3 3.9 %pack_cols.1 = bf16[128,1536]{1,0:T(8,128)(2,1)} custom-call(s32[2]{0:T(128)} %pad_add_fusion.at_ref, s32[1,512]{1,0:T(1,128)} %bitcast.11, f32[416,416]{1,0:T(8,128)} %refs_8_.1, bf16[416,2048]{1,0:T(8,128)(2,1)} %bitcast.7), custom_call_target="tpu_custom_call" | custom-call | tf_op jit(solution)/shard_map/pack_cols/pallas_call | solution.py:329
  5.2 14.1 %all_to_all.26 = bf16[16,8,1536]{2,1,0:T(8,128)(2,1)} all-to-all(bf16[16,8,1536]{2,1,0:T(8,128)(2,1)} %bitcast.10), channel_id=1, replica_groups=mesh['row'=16,'col'=16] {'col'}, dimensions={0} | all-to-all | bytes 786432 | tf_op jit(solution)/shard_map/all_to_all | solution.py:313
  19.3 2.6 %gather_hand.1 = (bf16[16,3072]{1,0:T(8,128)(2,1)}, bf16[16,3072]{1,0:T(8,128)(2,1)}, f32[16,16,128]{2,1,0:T(8,128)}) custom-call(s32[2]{0:T(128)} %pad_add_fusion.at_ref, s32[1,512]{1,0:T(1,128)} %bitcast.12, bf16[128,1536]{1,0:T(8,128)(2,1)} %bitcast.9), custom_call_target="tpu_custom_call" | custom-call | tf_op jit(solution)/shard_map/gather_hand/pallas_call | solution.py:349
  21.9 8.7 %all-to-all-start.1 = ((f32[16,16,128]{2,1,0:T(8,128)}), f32[16,16,128]{2,1,0:T(8,128)S(1)}, u32[]{:S(2)}, u32[]{:S(2)}) async-start(f32[16,16,128]{2,1,0:T(8,128)} %get-tuple-element.9), calls=%async_computation.1 | async-start | bytes 262144 | tf_op jit(solution)/shard_map/all_to_all | solution.py:313
  30.7 0.8 convert_reduce_fusion.first_ref
  31.5 7.9 %all-to-all-done.1.got_ref = f32[16,16,128]{2,1,0:T(8,128)S(1)} async-done(((f32[16,16,128]{2,1,0:T(8,128)}), f32[16,16,128]{2,1,0:T(8,128)S(1)}, u32[]{:S(2)}, u32[]{:S(2)}) %all-to-all-start.1) | async-done | bytes 131104 | tf_op jit(solution)/shard_map/all_to_all | solution.py:313
  39.3 0.7 copy-done.4
  40.0 2.0 %pack_slab.1 = f32[16,16,512]{2,1,0:T(8,128)} custom-call(s32[16]{0:T(128)} %convert_reduce_fusion.first_ref, s32[2]{0:T(128)} %pad_add_fusion.at_ref, f32[16,16,128]{2,1,0:T(8,128)} %copy-done.4), custom_call_target="tpu_custom_call" | custom-call | tf_op jit(solution)/shard_map/pack_slab/pallas_call | solution.py:371
  42.0 6.7 %all-to-all-start.2 = ((f32[16,16,512]{2,1,0:T(8,128)}), f32[16,16,512]{2,1,0:T(8,128)S(1)}, u32[]{:S(2)}, u32[]{:S(2)}) async-start(f32[16,16,512]{2,1,0:T(8,128)} %pack_slab.1), calls=%async_computation.2 | async-start | bytes 1048576 | tf_op jit(solution)/shard_map/all_to_all | solution.py:313
  48.7 2.9 %pack_rows.1 = f32[16,104,128]{2,1,0:T(8,128)} custom-call(s32[2]{0:T(128)} %pad_add_fusion.at_ref, s32[1,512]{1,0:T(1,128)} %bitcast.13, f32[416,416]{1,0:T(8,128)} %refs_8_.1), custom_call_target="tpu_custom_call" | custom-call | tf_op jit(solution)/shard_map/pack_rows/pallas_call | solution.py:338
  51.6 6.6 %all-to-all-done.2.own_ref = f32[16,16,512]{2,1,0:T(8,128)S(1)} async-done(((f32[16,16,512]{2,1,0:T(8,128)}), f32[16,16,512]{2,1,0:T(8,128)S(1)}, u32[]{:S(2)}, u32[]{:S(2)}) %all-to-all-start.2) | async-done | bytes 524320 | tf_op jit(solution)/shard_map/all_to_all | solution.py:313
  58.1 3.6 %all-to-all-start.3 = ((f32[16,104,128]{2,1,0:T(8,128)}), f32[16,104,128]{2,1,0:T(8,128)S(1)}, u32[]{:S(2)}, u32[]{:S(2)}) async-start(f32[16,104,128]{2,1,0:T(8,128)} %pack_rows.1), calls=%async_computation.3 | async-start | bytes 1703936 | tf_op jit(solution)/shard_map/all_to_all | solution.py:313
  61.8 1.5 %collective-permute-start.4 = (bf16[16,3072]{1,0:T(8,128)(2,1)S(1)}, bf16[16,3072]{1,0:T(8,128)(2,1)S(1)}, u32[]{:S(2)}, u32[]{:S(2)}) collective-permute-start(bf16[16,3072]{1,0:T(8,128)(2,1)S(1)} %copy-done.7), channel_id=1, source_target_pairs={{0,3},{1,0},{2,1},{3,2},{4,7},{5,4},{6,5},{7,6},{8,11},{9,8},{10,9... | collective-permute-start | bytes 294920 | tf_op jit(solution)/shard_map/ppermute | solution.py:364
  63.3 0.8 collective-permute-start.3
  64.1 1.8 %collective-permute-start.2 = (bf16[16,3072]{1,0:T(8,128)(2,1)S(1)}, bf16[16,3072]{1,0:T(8,128)(2,1)S(1)}, u32[]{:S(2)}, u32[]{:S(2)}) collective-permute-start(bf16[16,3072]{1,0:T(8,128)(2,1)S(1)} %copy-done.7), channel_id=1, source_target_pairs={{0,1},{1,2},{2,3},{3,0},{4,5},{5,6},{6,7},{7,4},{8,9},{9,10},{10,1... | collective-permute-start | bytes 294920 | tf_op jit(solution)/shard_map/ppermute | solution.py:364
  65.9 0.0 collective-permute-start
  65.9 0.9 collective-permute-start.7
  66.8 0.1 collective-permute-done.4.refs_3_
  66.8 2.3 %collective-permute-start.6 = (bf16[16,3072]{1,0:T(8,128)(2,1)S(1)}, bf16[16,3072]{1,0:T(8,128)(2,1)S(1)}, u32[]{:S(2)}, u32[]{:S(2)}) collective-permute-start(bf16[16,3072]{1,0:T(8,128)(2,1)S(1)} %copy-done.8), channel_id=1, source_target_pairs={{0,8},{1,9},{2,10},{3,11},{4,12},{5,13},{6,14},{7,15},{8,0},{9,1},... | collective-permute-start | bytes 294920 | tf_op jit(solution)/shard_map/ppermute | solution.py:367
  69.2 0.4 collective-permute-done.3.refs_2_
  69.5 2.4 %collective-permute-start.5 = (bf16[16,3072]{1,0:T(8,128)(2,1)S(1)}, bf16[16,3072]{1,0:T(8,128)(2,1)S(1)}, u32[]{:S(2)}, u32[]{:S(2)}) collective-permute-start(bf16[16,3072]{1,0:T(8,128)(2,1)S(1)} %copy-done.8), channel_id=1, source_target_pairs={{0,4},{1,5},{2,6},{3,7},{4,8},{5,9},{6,10},{7,11},{8,12},{9,13},{1... | collective-permute-start | bytes 294920 | tf_op jit(solution)/shard_map/ppermute | solution.py:367
  71.9 0.0 collective-permute-done.2.refs_1_
  71.9 11.5 %all-to-all-done.3.own_ref = f32[16,104,128]{2,1,0:T(8,128)S(1)} async-done(((f32[16,104,128]{2,1,0:T(8,128)}), f32[16,104,128]{2,1,0:T(8,128)S(1)}, u32[]{:S(2)}, u32[]{:S(2)}) %all-to-all-start.3) | async-done | bytes 852000 | tf_op jit(solution)/shard_map/all_to_all | solution.py:313
  83.5 2.7 %collective-permute-start.1 = (f32[16,104,128]{2,1,0:T(8,128)S(1)}, f32[16,104,128]{2,1,0:T(8,128)S(1)}, u32[]{:S(2)}, u32[]{:S(2)}) collective-permute-start(f32[16,104,128]{2,1,0:T(8,128)S(1)} %all-to-all-done.3.own_ref), channel_id=1, source_target_pairs={{0,16},{16,0},{32,48},{48,32},{64,80},{80,64},{96,112},{112,96},{1... | collective-permute-start | bytes 2555912 | tf_op jit(solution)/shard_map/ppermute | solution.py:347
  86.2 0.0 collective-permute-done.7.refs_7_
  86.2 0.0 collective-permute-done.6.refs_6_
  86.2 0.6 copy-done.12
  86.8 0.0 copy-done.13
  86.8 0.6 copy-done.14
  87.5 2.1 %join.1 = (bf16[64,3072]{1,0:T(8,128)(2,1)}, bf16[64,3072]{1,0:T(8,128)(2,1)}) custom-call(bf16[16,3072]{1,0:T(8,128)(2,1)} %get-tuple-element.10.refs_0_, bf16[16,3072]{1,0:T(8,128)(2,1)} %copy-done.11, bf16[16,3072]{1,0:T(8,128)(2,1)} %copy-done.10, bf16[16,3072]{1,0:T(8,128)(2,1)} %copy-done.9, bf16[16,3072]{1,0:T(8,128)(2,1)} %get-tuple-element.11.refs_4_, ...), custom_call_target="tpu_custom_call" | custom-call | tf_op jit(solution)/shard_map/join/pallas_call | solution.py:380
  89.6 0.5 collective-permute-start.10
  90.2 3.3 %collective-permute-start.9 = (bf16[64,3072]{1,0:T(8,128)(2,1)}, bf16[64,3072]{1,0:T(8,128)(2,1)S(1)}, u32[]{:S(2)}, u32[]{:S(2)}) collective-permute-start(bf16[64,3072]{1,0:T(8,128)(2,1)} %get-tuple-element.12.refs_0_), channel_id=1, source_target_pairs={{0,8},{1,9},{2,10},{3,11},{4,12},{5,13},{6,14},{7,15},{8,0},{9,1},... | collective-permute-start | bytes 1179656 | tf_op jit(solution)/shard_map/ppermute | solution.py:367
  93.5 0.2 collective-permute-start.8
  93.7 8.7 %collective-permute-done.10.refs_3_ = bf16[64,3072]{1,0:T(8,128)(2,1)S(1)} collective-permute-done((bf16[64,3072]{1,0:T(8,128)(2,1)}, bf16[64,3072]{1,0:T(8,128)(2,1)S(1)}, u32[]{:S(2)}, u32[]{:S(2)}) %collective-permute-start.10) | collective-permute-done | bytes 393248 | tf_op jit(solution)/shard_map/ppermute | solution.py:367
  102.4 1.5 %collective-permute-start.13 = (bf16[64,3072]{1,0:T(8,128)(2,1)}, bf16[64,3072]{1,0:T(8,128)(2,1)}, u32[]{:S(2)}, u32[]{:S(2)}) collective-permute-start(bf16[64,3072]{1,0:T(8,128)(2,1)} %get-tuple-element.13.refs_4_), channel_id=1, source_target_pairs={{0,3},{1,0},{2,1},{3,2},{4,7},{5,4},{6,5},{7,6},{8,11},{9,8},{10,9... | collective-permute-start | bytes 1179656 | tf_op jit(solution)/shard_map/ppermute | solution.py:364
  103.8 7.3 %collective-permute-done.9.refs_2_ = bf16[64,3072]{1,0:T(8,128)(2,1)S(1)} collective-permute-done((bf16[64,3072]{1,0:T(8,128)(2,1)}, bf16[64,3072]{1,0:T(8,128)(2,1)S(1)}, u32[]{:S(2)}, u32[]{:S(2)}) %collective-permute-start.9) | collective-permute-done | bytes 393248 | tf_op jit(solution)/shard_map/ppermute | solution.py:367
  111.2 0.8 collective-permute-start.12
  111.9 0.0 collective-permute-done.other_ref
  112.0 2.1 %collective-permute-start.11 = (bf16[64,3072]{1,0:T(8,128)(2,1)}, bf16[64,3072]{1,0:T(8,128)(2,1)}, u32[]{:S(2)}, u32[]{:S(2)}) collective-permute-start(bf16[64,3072]{1,0:T(8,128)(2,1)} %get-tuple-element.13.refs_4_), channel_id=1, source_target_pairs={{0,1},{1,2},{2,3},{3,0},{4,5},{5,6},{6,7},{7,4},{8,9},{9,10},{10,1... | collective-permute-start | bytes 1179656 | tf_op jit(solution)/shard_map/ppermute | solution.py:364
  114.1 18.9 %invert.1.inv_ref = f32[4,512,128]{2,1,0:T(8,128)} custom-call(s32[2]{0:T(128)} %pad_add_fusion.at_ref, f32[16,16,512]{2,1,0:T(8,128)} %copy-done.1, f32[16,16,512]{2,1,0:T(8,128)} %copy-done.3), custom_call_target="tpu_custom_call" | custom-call | tf_op jit(solution)/shard_map/invert/pallas_call | solution.py:391
  133.0 0.0 collective-permute-done.8.refs_1_
  133.0 0.0 collective-permute-done.13.refs_7_
  133.0 0.0 collective-permute-done.12.refs_6_
  133.0 0.0 collective-permute-done.11.refs_5_
  133.0 0.9 copy-done.2
  133.9 9.5 %update.1 = (f32[416,416]{1,0:T(8,128)}, f32[416,2048]{1,0:T(8,128)}) custom-call(s32[16]{0:T(128)} %convert_reduce_fusion.first_ref, s32[2]{0:T(128)} %pad_add_fusion.at_ref, s32[1,512]{1,0:T(1,128)} %bitcast.14, f32[4,512,128]{2,1,0:T(8,128)} %invert.1.inv_ref, f32[16,104,128]{2,1,0:T(8,128)} %copy-done, f32[16,104,128]{2,1,0:T(8,128)} %copy-done.2, ...), custom_call_target="tpu_custom_call" | custom-call | tf_op jit(solution)/shard_map/update/pallas_call | solution.py:401
  (29 shorter events, 0.1 us)
Async XLA Ops:
  0.6 30.0 %copy-start.15 = (s32[512]{0:T(512)S(1)}, s32[512]{0:T(512)}, u32[]{:S(2)}) copy-start(s32[512]{0:T(512)} %param.5) | copy-start | bytes 6148
  21.9 39.8 %copy-start.7 = (bf16[16,3072]{1,0:T(8,128)(2,1)S(1)}, bf16[16,3072]{1,0:T(8,128)(2,1)}, u32[]{:S(2)}) copy-start(bf16[16,3072]{1,0:T(8,128)(2,1)} %get-tuple-element.10.refs_0_) | copy-start | bytes 294916
  21.9 44.0 %copy-start.8 = (bf16[16,3072]{1,0:T(8,128)(2,1)S(1)}, bf16[16,3072]{1,0:T(8,128)(2,1)}, u32[]{:S(2)}) copy-start(bf16[16,3072]{1,0:T(8,128)(2,1)} %get-tuple-element.11.refs_4_) | copy-start | bytes 294916
  21.9 17.4 %all-to-all-start.1 = ((f32[16,16,128]{2,1,0:T(8,128)}), f32[16,16,128]{2,1,0:T(8,128)S(1)}, u32[]{:S(2)}, u32[]{:S(2)}) async-start(f32[16,16,128]{2,1,0:T(8,128)} %get-tuple-element.9), calls=%async_computation.1 | async-start | bytes 262144 | tf_op jit(solution)/shard_map/all_to_all | solution.py:313
  39.3 0.7 copy-start.4
  42.0 16.2 %all-to-all-start.2 = ((f32[16,16,512]{2,1,0:T(8,128)}), f32[16,16,512]{2,1,0:T(8,128)S(1)}, u32[]{:S(2)}, u32[]{:S(2)}) async-start(f32[16,16,512]{2,1,0:T(8,128)} %pack_slab.1), calls=%async_computation.2 | async-start | bytes 1048576 | tf_op jit(solution)/shard_map/all_to_all | solution.py:313
  58.1 56.0 %copy-start.1 = (f32[16,16,512]{2,1,0:T(8,128)}, f32[16,16,512]{2,1,0:T(8,128)S(1)}, u32[]{:S(2)}) copy-start(f32[16,16,512]{2,1,0:T(8,128)S(1)} %all-to-all-done.2.own_ref) | copy-start | bytes 1572868
  58.1 25.3 %all-to-all-start.3 = ((f32[16,104,128]{2,1,0:T(8,128)}), f32[16,104,128]{2,1,0:T(8,128)S(1)}, u32[]{:S(2)}, u32[]{:S(2)}) async-start(f32[16,104,128]{2,1,0:T(8,128)} %pack_rows.1), calls=%async_computation.3 | async-start | bytes 1703936 | tf_op jit(solution)/shard_map/all_to_all | solution.py:313
  61.8 5.1 %collective-permute-start.4 = (bf16[16,3072]{1,0:T(8,128)(2,1)S(1)}, bf16[16,3072]{1,0:T(8,128)(2,1)S(1)}, u32[]{:S(2)}, u32[]{:S(2)}) collective-permute-start(bf16[16,3072]{1,0:T(8,128)(2,1)S(1)} %copy-done.7), channel_id=1, source_target_pairs={{0,3},{1,0},{2,1},{3,2},{4,7},{5,4},{6,5},{7,6},{8,11},{9,8},{10,9... | collective-permute-start | bytes 294920 | tf_op jit(solution)/shard_map/ppermute | solution.py:364
  63.3 6.2 %collective-permute-start.3 = (bf16[16,3072]{1,0:T(8,128)(2,1)S(1)}, bf16[16,3072]{1,0:T(8,128)(2,1)S(1)}, u32[]{:S(2)}, u32[]{:S(2)}) collective-permute-start(bf16[16,3072]{1,0:T(8,128)(2,1)S(1)} %copy-done.7), channel_id=1, source_target_pairs={{0,2},{1,3},{2,0},{3,1},{4,6},{5,7},{6,4},{7,5},{8,10},{9,11},{10,... | collective-permute-start | bytes 294920 | tf_op jit(solution)/shard_map/ppermute | solution.py:364
  64.1 7.9 %collective-permute-start.2 = (bf16[16,3072]{1,0:T(8,128)(2,1)S(1)}, bf16[16,3072]{1,0:T(8,128)(2,1)S(1)}, u32[]{:S(2)}, u32[]{:S(2)}) collective-permute-start(bf16[16,3072]{1,0:T(8,128)(2,1)S(1)} %copy-done.7), channel_id=1, source_target_pairs={{0,1},{1,2},{2,3},{3,0},{4,5},{5,6},{6,7},{7,4},{8,9},{9,10},{10,1... | collective-permute-start | bytes 294920 | tf_op jit(solution)/shard_map/ppermute | solution.py:364
  65.9 46.1 %collective-permute-start = (f32[16,16,512]{2,1,0:T(8,128)S(1)}, f32[16,16,512]{2,1,0:T(8,128)S(1)}, u32[]{:S(2)}, u32[]{:S(2)}) collective-permute-start(f32[16,16,512]{2,1,0:T(8,128)S(1)} %all-to-all-done.2.own_ref), channel_id=1, source_target_pairs={{0,16},{16,0},{32,48},{48,32},{64,80},{80,64},{96,112},{112,96},{1... | collective-permute-start | bytes 1572872 | tf_op jit(solution)/shard_map/ppermute | solution.py:347
  65.9 20.3 %collective-permute-start.7 = (bf16[16,3072]{1,0:T(8,128)(2,1)S(1)}, bf16[16,3072]{1,0:T(8,128)(2,1)S(1)}, u32[]{:S(2)}, u32[]{:S(2)}) collective-permute-start(bf16[16,3072]{1,0:T(8,128)(2,1)S(1)} %copy-done.8), channel_id=1, source_target_pairs={{0,12},{1,13},{2,14},{3,15},{4,0},{5,1},{6,2},{7,3},{8,4},{9,5},{1... | collective-permute-start | bytes 294920 | tf_op jit(solution)/shard_map/ppermute | solution.py:367
  66.8 19.3 %copy-start.9 = (bf16[16,3072]{1,0:T(8,128)(2,1)}, bf16[16,3072]{1,0:T(8,128)(2,1)S(1)}, u32[]{:S(2)}) copy-start(bf16[16,3072]{1,0:T(8,128)(2,1)S(1)} %collective-permute-done.4.refs_3_) | copy-start | bytes 294916
  66.8 19.3 %collective-permute-start.6 = (bf16[16,3072]{1,0:T(8,128)(2,1)S(1)}, bf16[16,3072]{1,0:T(8,128)(2,1)S(1)}, u32[]{:S(2)}, u32[]{:S(2)}) collective-permute-start(bf16[16,3072]{1,0:T(8,128)(2,1)S(1)} %copy-done.8), channel_id=1, source_target_pairs={{0,8},{1,9},{2,10},{3,11},{4,12},{5,13},{6,14},{7,15},{8,0},{9,1},... | collective-permute-start | bytes 294920 | tf_op jit(solution)/shard_map/ppermute | solution.py:367
  69.5 16.7 %copy-start.10 = (bf16[16,3072]{1,0:T(8,128)(2,1)}, bf16[16,3072]{1,0:T(8,128)(2,1)S(1)}, u32[]{:S(2)}) copy-start(bf16[16,3072]{1,0:T(8,128)(2,1)S(1)} %collective-permute-done.3.refs_2_) | copy-start | bytes 294916
  69.5 16.7 %collective-permute-start.5 = (bf16[16,3072]{1,0:T(8,128)(2,1)S(1)}, bf16[16,3072]{1,0:T(8,128)(2,1)S(1)}, u32[]{:S(2)}, u32[]{:S(2)}) collective-permute-start(bf16[16,3072]{1,0:T(8,128)(2,1)S(1)} %copy-done.8), channel_id=1, source_target_pairs={{0,4},{1,5},{2,6},{3,7},{4,8},{5,9},{6,10},{7,11},{8,12},{9,13},{1... | collective-permute-start | bytes 294920 | tf_op jit(solution)/shard_map/ppermute | solution.py:367
  71.9 14.3 %copy-start.11 = (bf16[16,3072]{1,0:T(8,128)(2,1)}, bf16[16,3072]{1,0:T(8,128)(2,1)S(1)}, u32[]{:S(2)}) copy-start(bf16[16,3072]{1,0:T(8,128)(2,1)S(1)} %collective-permute-done.2.refs_1_) | copy-start | bytes 294916
  83.5 49.5 %copy-start = (f32[16,104,128]{2,1,0:T(8,128)}, f32[16,104,128]{2,1,0:T(8,128)S(1)}, u32[]{:S(2)}) copy-start(f32[16,104,128]{2,1,0:T(8,128)S(1)} %all-to-all-done.3.own_ref) | copy-start | bytes 2555908
  83.5 49.5 %collective-permute-start.1 = (f32[16,104,128]{2,1,0:T(8,128)S(1)}, f32[16,104,128]{2,1,0:T(8,128)S(1)}, u32[]{:S(2)}, u32[]{:S(2)}) collective-permute-start(f32[16,104,128]{2,1,0:T(8,128)S(1)} %all-to-all-done.3.own_ref), channel_id=1, source_target_pairs={{0,16},{16,0},{32,48},{48,32},{64,80},{80,64},{96,112},{112,96},{1... | collective-permute-start | bytes 2555912 | tf_op jit(solution)/shard_map/ppermute | solution.py:347
  86.2 0.6 copy-start.12
  86.2 0.7 copy-start.13
  86.8 0.6 copy-start.14
  89.6 12.8 %collective-permute-start.10 = (bf16[64,3072]{1,0:T(8,128)(2,1)}, bf16[64,3072]{1,0:T(8,128)(2,1)S(1)}, u32[]{:S(2)}, u32[]{:S(2)}) collective-permute-start(bf16[64,3072]{1,0:T(8,128)(2,1)} %get-tuple-element.12.refs_0_), channel_id=1, source_target_pairs={{0,12},{1,13},{2,14},{3,15},{4,0},{5,1},{6,2},{7,3},{8,4},{9,5},{1... | collective-permute-start | bytes 1179656 | tf_op jit(solution)/shard_map/ppermute | solution.py:367
  90.2 21.0 %collective-permute-start.9 = (bf16[64,3072]{1,0:T(8,128)(2,1)}, bf16[64,3072]{1,0:T(8,128)(2,1)S(1)}, u32[]{:S(2)}, u32[]{:S(2)}) collective-permute-start(bf16[64,3072]{1,0:T(8,128)(2,1)} %get-tuple-element.12.refs_0_), channel_id=1, source_target_pairs={{0,8},{1,9},{2,10},{3,11},{4,12},{5,13},{6,14},{7,15},{8,0},{9,1},... | collective-permute-start | bytes 1179656 | tf_op jit(solution)/shard_map/ppermute | solution.py:367
  93.5 39.5 %collective-permute-start.8 = (bf16[64,3072]{1,0:T(8,128)(2,1)}, bf16[64,3072]{1,0:T(8,128)(2,1)}, u32[]{:S(2)}, u32[]{:S(2)}) collective-permute-start(bf16[64,3072]{1,0:T(8,128)(2,1)} %get-tuple-element.12.refs_0_), channel_id=1, source_target_pairs={{0,4},{1,5},{2,6},{3,7},{4,8},{5,9},{6,10},{7,11},{8,12},{9,13},{1... | collective-permute-start | bytes 1179656 | tf_op jit(solution)/shard_map/ppermute | solution.py:367
  102.4 30.6 %copy-start.5 = (bf16[64,3072]{1,0:T(8,128)(2,1)}, bf16[64,3072]{1,0:T(8,128)(2,1)S(1)}, u32[]{:S(2)}) copy-start(bf16[64,3072]{1,0:T(8,128)(2,1)S(1)} %collective-permute-done.10.refs_3_) | copy-start | bytes 1179652
  102.4 30.6 %collective-permute-start.13 = (bf16[64,3072]{1,0:T(8,128)(2,1)}, bf16[64,3072]{1,0:T(8,128)(2,1)}, u32[]{:S(2)}, u32[]{:S(2)}) collective-permute-start(bf16[64,3072]{1,0:T(8,128)(2,1)} %get-tuple-element.13.refs_4_), channel_id=1, source_target_pairs={{0,3},{1,0},{2,1},{3,2},{4,7},{5,4},{6,5},{7,6},{8,11},{9,8},{10,9... | collective-permute-start | bytes 1179656 | tf_op jit(solution)/shard_map/ppermute | solution.py:364
  111.2 21.9 %copy-start.6 = (bf16[64,3072]{1,0:T(8,128)(2,1)}, bf16[64,3072]{1,0:T(8,128)(2,1)S(1)}, u32[]{:S(2)}) copy-start(bf16[64,3072]{1,0:T(8,128)(2,1)S(1)} %collective-permute-done.9.refs_2_) | copy-start | bytes 1179652
  111.2 21.8 %collective-permute-start.12 = (bf16[64,3072]{1,0:T(8,128)(2,1)}, bf16[64,3072]{1,0:T(8,128)(2,1)}, u32[]{:S(2)}, u32[]{:S(2)}) collective-permute-start(bf16[64,3072]{1,0:T(8,128)(2,1)} %get-tuple-element.13.refs_4_), channel_id=1, source_target_pairs={{0,2},{1,3},{2,0},{3,1},{4,6},{5,7},{6,4},{7,5},{8,10},{9,11},{10,... | collective-permute-start | bytes 1179656 | tf_op jit(solution)/shard_map/ppermute | solution.py:364
  111.9 2.1 %copy-start.3 = (f32[16,16,512]{2,1,0:T(8,128)}, f32[16,16,512]{2,1,0:T(8,128)S(1)}, u32[]{:S(2)}) copy-start(f32[16,16,512]{2,1,0:T(8,128)S(1)} %collective-permute-done.other_ref) | copy-start | bytes 1572868
  112.0 21.0 %collective-permute-start.11 = (bf16[64,3072]{1,0:T(8,128)(2,1)}, bf16[64,3072]{1,0:T(8,128)(2,1)}, u32[]{:S(2)}, u32[]{:S(2)}) collective-permute-start(bf16[64,3072]{1,0:T(8,128)(2,1)} %get-tuple-element.13.refs_4_), channel_id=1, source_target_pairs={{0,1},{1,2},{2,3},{3,0},{4,5},{5,6},{6,7},{7,4},{8,9},{9,10},{10,1... | collective-permute-start | bytes 1179656 | tf_op jit(solution)/shard_map/ppermute | solution.py:364
  133.0 0.9 copy-start.2

commit v3 on v2

--- a/solution.py
+++ b/solution.py
@@ -52,15 +52,10 @@
 
 
 def pack_rows(at_ref, pruned_ref, h_ref, rows_ref):
-    height = h_ref.shape[0]
-    tiles = rows_ref.shape[0]
-    cap = 2 * pruned_ref.shape[1] // tiles
+    height, width = h_ref.shape
+    cap = rows_ref.shape[0] * 128 // width
     pick = one_hot(held(pruned_ref[...], at_ref[0], height, in_turn(cap)), height)
-    rows = across(pick, h_ref[...], ((1,), (0,)), HIGH)
-    for core in range(2):
-        part = strips_of(rows[cap // 2 * core : cap // 2 * (core + 1)])
-        for d in range(core, tiles, 2):
-            rows_ref[d] = part
+    rows_ref[...] = strips_of(across(pick, h_ref[...], ((1,), (0,)), HIGH))
 
 
 def strips_of(rows):
@@ -130,10 +125,11 @@
     cap = 2 * mine
     pick = one_hot(held(pruned, at_ref[0], height, in_turn(cap)), height)
     piece = across(pick, c, ((1,), (1,)), HIGH)
-    quarter = cap // 4
-    piece = jnp.concatenate([piece[quarter * i : quarter * i + quarter] for i in range(4)], axis=1)
-    for d in range(tiles):
-        piece_ref[d] = piece
+    for core in range(2):
+        part = piece[:, mine // 2 * core : mine // 2 * (core + 1)]
+        part = jnp.concatenate([part[8 * i : 8 * i + 8] for i in range(cap // 8)], axis=1)
+        for d in range(core, tiles, 2):
+            piece_ref[d] = part
     for part in range(2):
         lanes = slice(half * part, half * part + half)
         low_ref[:, lanes] = parts[part][: mine // 2].astype(BF16)
@@ -149,16 +145,14 @@
             out[rows * d : rows * d + rows, :] = refs[count * path + d][...]
 
 
-def pack_slab(first_ref, at_ref, got_ref, out_ref, slab_ref, turned_ref):
-    tiles, quarter, four = got_ref.shape
-    mine = four // 4
+def pack_slab(first_ref, got_ref, out_ref, slab_ref):
+    tiles, mine, n = out_ref.shape
+    groups = got_ref.shape[2] // mine
     for t in range(tiles):
         got = got_ref[t]
-        for i in range(4):
-            slab_ref[pl.ds(first_ref[t] + quarter * i, quarter), 0:mine] = got[:, mine * i : mine * i + mine]
-    turned_ref[...] = slab_ref[0 : turned_ref.shape[1], :].T[0:mine, :]
-    half = mine // 2
-    slab = turned_ref[pl.ds(pl.multiple_of(at_ref[0] % 2 * half, half), half), :]
+        for i in range(groups):
+            slab_ref[pl.ds(first_ref[t] + 8 * i, 8), 0:mine] = got[:, mine * i : mine * i + mine]
+    slab = slab_ref[0:n, :].T[0:mine, :]
     for d in range(tiles):
         out_ref[d] = slab
 
@@ -200,7 +194,7 @@
             panel = swept(panel)
         scaled.append(jnp.where(known, panel, 0.0))
         rows = [spread(panel, j) for j in range(8)]
-        if work and t % 2:
+        if work:
             work.pop(0)()
         for s in range(t + 1, count):
             v = tiles[s]
@@ -231,41 +225,51 @@
         while work:
             work.pop(0)()
         base = across(lower, scaled, ((0,), (0,)), HIGH)
-        rows = [base if c == k else across(base, out_ref[c, own, :], ((1,), (0,)), HIGH) for c in range(blocks)]
+        rows = {k: base}
         cols = [out_ref[k, BASE * r : BASE * r + BASE, :] for r in range(blocks)]
+        out_ref[k, own, :] = base
+
+        def row(c, own=own, rows=rows, base=base):
+            rows[c] = across(base, out_ref[c, own, :], ((1,), (0,)), HIGH)
+            out_ref[c, own, :] = rows[c]
 
         def product(r, c, k=k, rows=rows, cols=cols):
             at = (c, slice(BASE * r, BASE * r + BASE))
             total = across(cols[r], rows[c], ((1,), (0,)), HIGH)
             out_ref[at] = -total if c == k else out_ref[at] - total
 
-        for i in range(1, blocks):
-            r = (k + i) % blocks
-            for c in range(blocks):
-                if r == c == k + 1:
-                    product(r, c)
-                else:
+        following = (k + 1) % blocks
+        if k + 1 < blocks:
+            row(following)
+            product(following, following)
+        for c in [(k + i) % blocks for i in range(1, blocks)]:
+            if c != following or k + 1 == blocks:
+                work.append(functools.partial(row, c))
+        for c in [(k + i) % blocks for i in range(1, blocks + 1)]:
+            for r in [(k + i) % blocks for i in range(1, blocks)]:
+                if not r == c == k + 1:
                     work.append(functools.partial(product, r, c))
-        for c in range(blocks):
-            out_ref[c, own, :] = rows[c]
     while work:
         work.pop(0)()
 
 
-def update(first_ref, at_ref, pruned_ref, inv_ref, own_ref, other_ref, *refs):
+def update(first_ref, at_ref, pruned_ref, inv_ref, near_ref, far_ref, twin_near_ref, twin_far_ref, *refs):
     blocks, (h_ref, w_ref, h_out, w_out, panel_ref, w_new_ref, h_new_ref, sems) = refs[:-8], refs[-8:]
     strips, n, _ = inv_ref.shape
     width = h_ref.shape[1]
     tiles = first_ref.shape[0]
-    half = n // tiles
+    cap = 2 * n // tiles
     side = len(blocks) // 2
     rows_w = w_ref.shape[1]
     steps = rows_w // BLOCK
-    low_is_own = at_ref[0] % 2 == 0
+    core, z = at_ref[0] % 2, at_ref[0] // 2
+    near = near_ref.shape[0]
     for t in range(tiles):
-        own, other = own_ref[t], other_ref[t]
-        place_strips(panel_ref, first_ref[t], jnp.where(low_is_own, own, other), half, width)
-        place_strips(panel_ref, first_ref[t] + half, jnp.where(low_is_own, other, own), half, width)
+        apart = (t // 2) ^ z
+        of = apart % near
+        own = jnp.where(apart < near, near_ref[of], far_ref[of])
+        twin = jnp.where(apart < near, twin_near_ref[of], twin_far_ref[of])
+        place_strips(panel_ref, first_ref[t], jnp.where(core == t % 2, own, twin), cap, width)
     panel = jnp.concatenate([panel_ref[j, 0:n, :] for j in range(panel_ref.shape[0])], axis=1).T[:width, :]
     x, y = at_ref[1] % side, at_ref[1] // side
     hands = []
@@ -319,7 +323,6 @@
     n = pruned.shape[0]
     tiles = lax.axis_size("row")
     cap = 2 * n // tiles
-    half = cap // 2
     at = jnp.stack([lax.axis_index("row"), lax.axis_index("col")]).astype(jnp.int32)
     weights = weights.T
     listed = pruned.reshape(1, n)
@@ -337,7 +340,7 @@
     mine = n // tiles
     rows = pl.pallas_call(
         pack_rows,
-        out_shape=jax.ShapeDtypeStruct((tiles, half * tile_cols // 128, 128), F32),
+        out_shape=jax.ShapeDtypeStruct((cap * tile_cols // 128, 128), F32),
         in_specs=[SMEM, VMEM, VMEM],
         out_specs=VMEM,
         name="pack_rows",
@@ -346,12 +349,14 @@
     def swapped(value, mask):
         return lax.ppermute(value, "row", [(i, i ^ mask) for i in range(tiles)])
 
+    near_rows = [rows] + [swapped(rows, 2 * m) for m in range(1, 4)]
+    near_rows = jnp.stack(near_rows)
     low, high, pieces = pl.pallas_call(
         functools.partial(gather_hand, height=tile_rows, width=tile_cols),
         out_shape=(
             jax.ShapeDtypeStruct((mine // 2, length), BF16),
             jax.ShapeDtypeStruct((mine // 2, length), BF16),
-            jax.ShapeDtypeStruct((tiles, cap // 4, 4 * mine), F32),
+            jax.ShapeDtypeStruct((tiles, 8, cap // 8 * (mine // 2)), F32),
         ),
         in_specs=[SMEM, VMEM, VMEM],
         out_specs=(VMEM, VMEM, VMEM),
@@ -371,11 +376,11 @@
     slab = pl.pallas_call(
         pack_slab,
         out_shape=jax.ShapeDtypeStruct((tiles, mine // 2, n), F32),
-        in_specs=[SMEM, SMEM, VMEM],
+        in_specs=[SMEM, VMEM],
         out_specs=VMEM,
-        scratch_shapes=[pltpu.VMEM((n + cap, 128), F32), pltpu.VMEM((mine, n), F32)],
+        scratch_shapes=[pltpu.VMEM((n + cap, 128), F32)],
         name="pack_slab",
-    )(first, at, pieces)
+    )(first, pieces)
     slab = sent_to_all(slab, "col")
     low, high = pl.pallas_call(
         join,
@@ -386,7 +391,8 @@
     )(*lows, *highs)
     cols = [low] + [along_y(low, d) for d in range(1, side)]
     cols += [high] + [along_x(high, d) for d in range(1, side)]
-    rows = sent_to_all(rows, "row")
+    far_rows = swapped(near_rows, 8)
+    twin_near = swapped(near_rows, 1)
     slab_twin = swapped(slab, 1)
     inverse = pl.pallas_call(
         invert,
@@ -396,7 +402,7 @@
         scratch_shapes=[pltpu.VMEM((8, BASE), F32)],
         name="invert",
     )(at, slab, slab_twin)
-    rows_twin = swapped(rows, 1)
+    twin_far = swapped(far_rows, 1)
     anywhere = pl.BlockSpec(memory_space=pl.ANY)
     h_new, w_new = pl.pallas_call(
         update,
@@ -404,7 +410,7 @@
             jax.ShapeDtypeStruct(hessian_inverse.shape, F32),
             jax.ShapeDtypeStruct(weights.shape, F32),
         ),
-        in_specs=[SMEM, SMEM] + [VMEM] * (6 + len(cols)),
+        in_specs=[SMEM, SMEM] + [VMEM] * (8 + len(cols)),
         out_specs=(anywhere, anywhere),
         scratch_shapes=[
             pltpu.VMEM((-(-tile_cols // 128), n + cap, 128), F32),
@@ -413,7 +419,9 @@
             pltpu.SemaphoreType.DMA((rows_w // BLOCK + 1,)),
         ],
         name="update",
-    )(first, at, listed, inverse, rows, rows_twin, *cols, hessian_inverse, weights)
+    )(
+        first, at, listed, inverse, near_rows, far_rows, twin_near, twin_far, *cols, hessian_inverse, weights
+    )
     return h_new, w_new.T
 
 

time: 144 us -> 131 us (0.910)
  the two profiles are of different devices: /device:TPU:26 before, /device:TPU:1 now
where the time goes in v3:
time: 131 us; the launch traced here: 130 us
  Pallas kernels  41.6 us (32%)
  starting transfers between devices  37.6 us (29%)
  waiting for transfers between devices  27.4 us (21%)
  blocking collectives  16.9 us (13%)
  local copies, waits for them, and re-layouts  3.12 us (2%)
  other arithmetic  2.29 us (2%)
    ppermute x7, waiting for transfers between devices, swapped(): return lax.ppermute(value, 'row', [(i, i ^ mask) for i in range(tiles)])  20.1 us
    pallas_call x1, Pallas kernels, on_device(): pl.pallas_call(invert, out_shape=jax.ShapeDtypeStruct((n // BASE, n, BASE...  18.7 us
    all_to_all x1, blocking collectives, sent_to_all(): return lax.all_to_all(copies, axis, split_axis=0, concat_axis=0, tiled=True)  16.9 us
    all_to_all x2, starting transfers between devices, sent_to_all(): return lax.all_to_all(copies, axis, split_axis=0, concat_axis=0, tiled=True)  13.9 us
    pallas_call x1, Pallas kernels, on_device(): pl.pallas_call(update, out_shape=(jax.ShapeDtypeStruct(hessian_inverse.sh...  9.67 us
    ppermute x6, starting transfers between devices, along_y(): lax.ppermute(value, 'col', [(c, (c + d * side) % tiles) for c in range(ti...  8.26 us
    ppermute x7, starting transfers between devices, swapped(): return lax.ppermute(value, 'row', [(i, i ^ mask) for i in range(tiles)])  8.25 us
    ppermute x6, starting transfers between devices, along_x(): lax.ppermute(value, 'col', [(c, c // side * side + (c + d) % side) for c...  7.22 us
  transfers between devices with their start and end apart: 21, of which 4 were waited for; matrix products, arithmetic and copies ran while one was open for 1% of the time, Pallas kernels for 18%

profile of v3, /device:TPU:1, one launch (start us, length us, event | category | flops | bytes accessed | tf_op | source)
XLA Modules:
  0.0 129.9 jit_solution(10675445099926297988)
XLA Ops:
  0.6 0.0 copy-start.15
  0.6 0.6 pad_add_fusion.at_ref
  1.3 3.9 %pack_cols.1 = bf16[128,1536]{1,0:T(8,128)(2,1)} custom-call(s32[2]{0:T(128)} %pad_add_fusion.at_ref, s32[1,512]{1,0:T(1,128)} %bitcast.19, f32[416,416]{1,0:T(8,128)} %refs_8_.1, bf16[416,2048]{1,0:T(8,128)(2,1)} %bitcast.11), custom_call_target="tpu_custom_call" | custom-call | tf_op jit(solution)/shard_map/pack_cols/pallas_call | solution.py:332
  5.2 16.9 %all_to_all.21 = bf16[16,8,1536]{2,1,0:T(8,128)(2,1)} all-to-all(bf16[16,8,1536]{2,1,0:T(8,128)(2,1)} %bitcast.14), channel_id=1, replica_groups=mesh['row'=16,'col'=16] {'col'}, dimensions={0} | all-to-all | bytes 786432 | tf_op jit(solution)/shard_map/all_to_all | solution.py:317
  22.1 2.6 %gather_hand.1 = (bf16[16,3072]{1,0:T(8,128)(2,1)}, bf16[16,3072]{1,0:T(8,128)(2,1)}, f32[16,8,128]{2,1,0:T(8,128)}) custom-call(s32[2]{0:T(128)} %pad_add_fusion.at_ref, s32[1,512]{1,0:T(1,128)} %bitcast.20, bf16[128,1536]{1,0:T(8,128)(2,1)} %bitcast.13), custom_call_target="tpu_custom_call" | custom-call | tf_op jit(solution)/shard_map/gather_hand/pallas_call | solution.py:354
  24.6 10.3 %all-to-all-start.1 = ((f32[16,8,128]{2,1,0:T(8,128)}), f32[16,8,128]{2,1,0:T(8,128)S(1)}, u32[]{:S(2)}, u32[]{:S(2)}) async-start(f32[16,8,128]{2,1,0:T(8,128)} %get-tuple-element.9), calls=%async_computation.1 | async-start | bytes 131072 | tf_op jit(solution)/shard_map/all_to_all | solution.py:317
  34.9 0.8 convert_reduce_fusion.first_ref
  35.7 7.0 %all-to-all-done.1.got_ref = f32[16,8,128]{2,1,0:T(8,128)S(1)} async-done(((f32[16,8,128]{2,1,0:T(8,128)}), f32[16,8,128]{2,1,0:T(8,128)S(1)}, u32[]{:S(2)}, u32[]{:S(2)}) %all-to-all-start.1) | async-done | bytes 65568 | tf_op jit(solution)/shard_map/all_to_all | solution.py:317
  42.7 0.6 copy-done.8
  43.3 2.0 %pack_slab.1 = f32[16,16,512]{2,1,0:T(8,128)} custom-call(s32[16]{0:T(128)} %convert_reduce_fusion.first_ref, f32[16,8,128]{2,1,0:T(8,128)} %copy-done.8), custom_call_target="tpu_custom_call" | custom-call | tf_op jit(solution)/shard_map/pack_slab/pallas_call | solution.py:376
  45.3 3.6 %all-to-all-start.2 = ((f32[16,16,512]{2,1,0:T(8,128)}), f32[16,16,512]{2,1,0:T(8,128)S(1)}, u32[]{:S(2)}, u32[]{:S(2)}) async-start(f32[16,16,512]{2,1,0:T(8,128)} %pack_slab.1), calls=%async_computation.2 | async-start | bytes 1048576 | tf_op jit(solution)/shard_map/all_to_all | solution.py:317
  48.9 2.6 %pack_rows.1 = f32[208,128]{1,0:T(8,128)} custom-call(s32[2]{0:T(128)} %pad_add_fusion.at_ref, s32[1,512]{1,0:T(1,128)} %bitcast.21, f32[416,416]{1,0:T(8,128)} %refs_8_.1), custom_call_target="tpu_custom_call" | custom-call | tf_op jit(solution)/shard_map/pack_rows/pallas_call | solution.py:341
  51.5 0.3 collective-permute-start.3
  51.8 1.1 collective-permute-start.2
  52.9 2.2 %collective-permute-start.1 = (f32[208,128]{1,0:T(8,128)}, f32[208,128]{1,0:T(8,128)S(1)}, u32[]{:S(2)}, u32[]{:S(2)}) collective-permute-start(f32[208,128]{1,0:T(8,128)} %pack_rows.1), channel_id=1, source_target_pairs={{0,32},{16,48},{32,0},{48,16},{64,96},{80,112},{96,64},{112,80},{1... | collective-permute-start | bytes 319496 | tf_op jit(solution)/shard_map/ppermute | solution.py:350
  55.0 2.5 %collective-permute-start.9 = (bf16[16,3072]{1,0:T(8,128)(2,1)}, bf16[16,3072]{1,0:T(8,128)(2,1)S(1)}, u32[]{:S(2)}, u32[]{:S(2)}) collective-permute-start(bf16[16,3072]{1,0:T(8,128)(2,1)} %get-tuple-element.10.refs_0_), channel_id=1, source_target_pairs={{0,3},{1,0},{2,1},{3,2},{4,7},{5,4},{6,5},{7,6},{8,11},{9,8},{10,9... | collective-permute-start | bytes 294920 | tf_op jit(solution)/shard_map/ppermute | solution.py:369
  57.5 0.6 collective-permute-start.8
  58.1 0.0 collective-permute-done.3
  58.1 0.8 collective-permute-start.7
  58.9 3.8 %collective-permute-done.2 = f32[208,128]{1,0:T(8,128)S(1)} collective-permute-done((f32[208,128]{1,0:T(8,128)}, f32[208,128]{1,0:T(8,128)S(1)}, u32[]{:S(2)}, u32[]{:S(2)}) %collective-permute-start.2) | collective-permute-done | bytes 106528 | tf_op jit(solution)/shard_map/ppermute | solution.py:350
  62.7 2.3 %collective-permute-start.12 = (bf16[16,3072]{1,0:T(8,128)(2,1)}, bf16[16,3072]{1,0:T(8,128)(2,1)S(1)}, u32[]{:S(2)}, u32[]{:S(2)}) collective-permute-start(bf16[16,3072]{1,0:T(8,128)(2,1)} %get-tuple-element.11.refs_4_), channel_id=1, source_target_pairs={{0,12},{1,13},{2,14},{3,15},{4,0},{5,1},{6,2},{7,3},{8,4},{9,5},{1... | collective-permute-start | bytes 294920 | tf_op jit(solution)/shard_map/ppermute | solution.py:372
  65.0 0.0 collective-permute-done.1
  65.0 0.5 collective-permute-start.11
  65.5 0.6 collective-permute-start.10
  66.2 0.0 all-to-all-done.2.own_ref
  66.2 0.0 copy-start
  66.2 2.3 %collective-permute-start = (f32[16,16,512]{2,1,0:T(8,128)S(1)}, f32[16,16,512]{2,1,0:T(8,128)S(1)}, u32[]{:S(2)}, u32[]{:S(2)}) collective-permute-start(f32[16,16,512]{2,1,0:T(8,128)S(1)} %all-to-all-done.2.own_ref), channel_id=1, source_target_pairs={{0,16},{16,0},{32,48},{48,32},{64,80},{80,64},{96,112},{112,96},{1... | collective-permute-start | bytes 1572872 | tf_op jit(solution)/shard_map/ppermute | solution.py:350
  68.5 0.9 pad_maximum_fusion.near_ref
  69.4 0.0 copy-start.11
  69.4 1.4 %collective-permute-start.4 = (f32[4,208,128]{2,1,0:T(8,128)S(1)}, f32[4,208,128]{2,1,0:T(8,128)S(1)}, u32[]{:S(2)}, u32[]{:S(2)}) collective-permute-start(f32[4,208,128]{2,1,0:T(8,128)S(1)} %pad_maximum_fusion.near_ref), channel_id=1, source_target_pairs={{0,128},{16,144},{32,160},{48,176},{64,192},{80,208},{96,224},{112... | collective-permute-start | bytes 1277960 | tf_op jit(solution)/shard_map/ppermute | solution.py:350
  70.8 0.4 collective-permute-start.5
  71.3 0.2 copy-done.12
  71.5 0.4 copy-done.13
  71.9 0.6 copy-done.14
  72.5 2.1 %join.1 = (bf16[64,3072]{1,0:T(8,128)(2,1)}, bf16[64,3072]{1,0:T(8,128)(2,1)}) custom-call(bf16[16,3072]{1,0:T(8,128)(2,1)} %get-tuple-element.10.refs_0_, bf16[16,3072]{1,0:T(8,128)(2,1)} %copy-done.11, bf16[16,3072]{1,0:T(8,128)(2,1)} %copy-done.10, bf16[16,3072]{1,0:T(8,128)(2,1)} %copy-done.9, bf16[16,3072]{1,0:T(8,128)(2,1)} %get-tuple-element.11.refs_4_, ...), custom_call_target="tpu_custom_call" | custom-call | tf_op jit(solution)/shard_map/join/pallas_call | solution.py:385
  74.7 2.8 %collective-permute-start.15 = (bf16[64,3072]{1,0:T(8,128)(2,1)}, bf16[64,3072]{1,0:T(8,128)(2,1)S(1)}, u32[]{:S(2)}, u32[]{:S(2)}) collective-permute-start(bf16[64,3072]{1,0:T(8,128)(2,1)} %get-tuple-element.12.refs_0_), channel_id=1, source_target_pairs={{0,12},{1,13},{2,14},{3,15},{4,0},{5,1},{6,2},{7,3},{8,4},{9,5},{1... | collective-permute-start | bytes 1179656 | tf_op jit(solution)/shard_map/ppermute | solution.py:372
  77.5 0.5 collective-permute-start.14
  78.0 16.3 %collective-permute-done.4.far_ref = f32[4,208,128]{2,1,0:T(8,128)S(1)} collective-permute-done((f32[4,208,128]{2,1,0:T(8,128)S(1)}, f32[4,208,128]{2,1,0:T(8,128)S(1)}, u32[]{:S(2)}, u32[]{:S(2)}) %collective-permute-start.4) | collective-permute-done | bytes 426016 | tf_op jit(solution)/shard_map/ppermute | solution.py:350
  94.3 0.6 collective-permute-start.6
  94.9 1.5 %collective-permute-start.13 = (bf16[64,3072]{1,0:T(8,128)(2,1)}, bf16[64,3072]{1,0:T(8,128)(2,1)}, u32[]{:S(2)}, u32[]{:S(2)}) collective-permute-start(bf16[64,3072]{1,0:T(8,128)(2,1)} %get-tuple-element.12.refs_0_), channel_id=1, source_target_pairs={{0,4},{1,5},{2,6},{3,7},{4,8},{5,9},{6,10},{7,11},{8,12},{9,13},{1... | collective-permute-start | bytes 1179656 | tf_op jit(solution)/shard_map/ppermute | solution.py:372
  96.4 1.5 %collective-permute-start.18 = (bf16[64,3072]{1,0:T(8,128)(2,1)}, bf16[64,3072]{1,0:T(8,128)(2,1)}, u32[]{:S(2)}, u32[]{:S(2)}) collective-permute-start(bf16[64,3072]{1,0:T(8,128)(2,1)} %get-tuple-element.13.refs_4_), channel_id=1, source_target_pairs={{0,3},{1,0},{2,1},{3,2},{4,7},{5,4},{6,5},{7,6},{8,11},{9,8},{10,9... | collective-permute-start | bytes 1179656 | tf_op jit(solution)/shard_map/ppermute | solution.py:369
  97.9 1.5 %collective-permute-start.17 = (bf16[64,3072]{1,0:T(8,128)(2,1)}, bf16[64,3072]{1,0:T(8,128)(2,1)}, u32[]{:S(2)}, u32[]{:S(2)}) collective-permute-start(bf16[64,3072]{1,0:T(8,128)(2,1)} %get-tuple-element.13.refs_4_), channel_id=1, source_target_pairs={{0,2},{1,3},{2,0},{3,1},{4,6},{5,7},{6,4},{7,5},{8,10},{9,11},{10,... | collective-permute-start | bytes 1179656 | tf_op jit(solution)/shard_map/ppermute | solution.py:369
  99.4 0.4 collective-permute-start.16
  99.8 0.4 copy-done.2
  100.2 18.7 %invert.1.inv_ref = f32[4,512,128]{2,1,0:T(8,128)} custom-call(s32[2]{0:T(128)} %pad_add_fusion.at_ref, f32[16,16,512]{2,1,0:T(8,128)} %copy-done, f32[16,16,512]{2,1,0:T(8,128)} %copy-done.2), custom_call_target="tpu_custom_call" | custom-call | tf_op jit(solution)/shard_map/invert/pallas_call | solution.py:397
  118.9 0.3 collective-permute-done.16.refs_5_
  119.3 0.8 copy-done.5
  120.1 9.7 %update.1 = (f32[416,416]{1,0:T(8,128)}, f32[416,2048]{1,0:T(8,128)}) custom-call(s32[16]{0:T(128)} %convert_reduce_fusion.first_ref, s32[2]{0:T(128)} %pad_add_fusion.at_ref, s32[1,512]{1,0:T(1,128)} %bitcast.22, f32[4,512,128]{2,1,0:T(8,128)} %invert.1.inv_ref, f32[4,208,128]{2,1,0:T(8,128)} %copy-done.1, f32[4,208,128]{2,1,0:T(8,128)} %copy-done.3, ...), custom_call_target="tpu_custom_call" | custom-call | tf_op jit(solution)/shard_map/update/pallas_call | solution.py:407
  (38 shorter events, 0.1 us)
Async XLA Ops:
  0.6 34.3 %copy-start.15 = (s32[512]{0:T(512)S(1)}, s32[512]{0:T(512)}, u32[]{:S(2)}) copy-start(s32[512]{0:T(512)} %param.5) | copy-start | bytes 6148
  24.6 18.1 %all-to-all-start.1 = ((f32[16,8,128]{2,1,0:T(8,128)}), f32[16,8,128]{2,1,0:T(8,128)S(1)}, u32[]{:S(2)}, u32[]{:S(2)}) async-start(f32[16,8,128]{2,1,0:T(8,128)} %get-tuple-element.9), calls=%async_computation.1 | async-start | bytes 131072 | tf_op jit(solution)/shard_map/all_to_all | solution.py:317
  42.7 0.6 copy-start.8
  45.3 20.9 %all-to-all-start.2 = ((f32[16,16,512]{2,1,0:T(8,128)}), f32[16,16,512]{2,1,0:T(8,128)S(1)}, u32[]{:S(2)}, u32[]{:S(2)}) async-start(f32[16,16,512]{2,1,0:T(8,128)} %pack_slab.1), calls=%async_computation.2 | async-start | bytes 1048576 | tf_op jit(solution)/shard_map/all_to_all | solution.py:317
  51.5 6.6 %collective-permute-start.3 = (f32[208,128]{1,0:T(8,128)}, f32[208,128]{1,0:T(8,128)S(1)}, u32[]{:S(2)}, u32[]{:S(2)}) collective-permute-start(f32[208,128]{1,0:T(8,128)} %pack_rows.1), channel_id=1, source_target_pairs={{0,96},{16,112},{32,64},{48,80},{64,32},{80,48},{96,0},{112,16},{1... | collective-permute-start | bytes 319496 | tf_op jit(solution)/shard_map/ppermute | solution.py:350
  51.8 10.9 %collective-permute-start.2 = (f32[208,128]{1,0:T(8,128)}, f32[208,128]{1,0:T(8,128)S(1)}, u32[]{:S(2)}, u32[]{:S(2)}) collective-permute-start(f32[208,128]{1,0:T(8,128)} %pack_rows.1), channel_id=1, source_target_pairs={{0,64},{16,80},{32,96},{48,112},{64,0},{80,16},{96,32},{112,48},{1... | collective-permute-start | bytes 319496 | tf_op jit(solution)/shard_map/ppermute | solution.py:350
  52.9 12.1 %collective-permute-start.1 = (f32[208,128]{1,0:T(8,128)}, f32[208,128]{1,0:T(8,128)S(1)}, u32[]{:S(2)}, u32[]{:S(2)}) collective-permute-start(f32[208,128]{1,0:T(8,128)} %pack_rows.1), channel_id=1, source_target_pairs={{0,32},{16,48},{32,0},{48,16},{64,96},{80,112},{96,64},{112,80},{1... | collective-permute-start | bytes 319496 | tf_op jit(solution)/shard_map/ppermute | solution.py:350
  55.0 10.5 %collective-permute-start.9 = (bf16[16,3072]{1,0:T(8,128)(2,1)}, bf16[16,3072]{1,0:T(8,128)(2,1)S(1)}, u32[]{:S(2)}, u32[]{:S(2)}) collective-permute-start(bf16[16,3072]{1,0:T(8,128)(2,1)} %get-tuple-element.10.refs_0_), channel_id=1, source_target_pairs={{0,3},{1,0},{2,1},{3,2},{4,7},{5,4},{6,5},{7,6},{8,11},{9,8},{10,9... | collective-permute-start | bytes 294920 | tf_op jit(solution)/shard_map/ppermute | solution.py:369
  57.5 8.7 %collective-permute-start.8 = (bf16[16,3072]{1,0:T(8,128)(2,1)}, bf16[16,3072]{1,0:T(8,128)(2,1)S(1)}, u32[]{:S(2)}, u32[]{:S(2)}) collective-permute-start(bf16[16,3072]{1,0:T(8,128)(2,1)} %get-tuple-element.10.refs_0_), channel_id=1, source_target_pairs={{0,2},{1,3},{2,0},{3,1},{4,6},{5,7},{6,4},{7,5},{8,10},{9,11},{10,... | collective-permute-start | bytes 294920 | tf_op jit(solution)/shard_map/ppermute | solution.py:369
  58.1 11.3 %collective-permute-start.7 = (bf16[16,3072]{1,0:T(8,128)(2,1)}, bf16[16,3072]{1,0:T(8,128)(2,1)S(1)}, u32[]{:S(2)}, u32[]{:S(2)}) collective-permute-start(bf16[16,3072]{1,0:T(8,128)(2,1)} %get-tuple-element.10.refs_0_), channel_id=1, source_target_pairs={{0,1},{1,2},{2,3},{3,0},{4,5},{5,6},{6,7},{7,4},{8,9},{9,10},{10,1... | collective-permute-start | bytes 294920 | tf_op jit(solution)/shard_map/ppermute | solution.py:369
  62.7 8.1 %collective-permute-start.12 = (bf16[16,3072]{1,0:T(8,128)(2,1)}, bf16[16,3072]{1,0:T(8,128)(2,1)S(1)}, u32[]{:S(2)}, u32[]{:S(2)}) collective-permute-start(bf16[16,3072]{1,0:T(8,128)(2,1)} %get-tuple-element.11.refs_4_), channel_id=1, source_target_pairs={{0,12},{1,13},{2,14},{3,15},{4,0},{5,1},{6,2},{7,3},{8,4},{9,5},{1... | collective-permute-start | bytes 294920 | tf_op jit(solution)/shard_map/ppermute | solution.py:372
  65.0 6.2 %collective-permute-start.11 = (bf16[16,3072]{1,0:T(8,128)(2,1)}, bf16[16,3072]{1,0:T(8,128)(2,1)S(1)}, u32[]{:S(2)}, u32[]{:S(2)}) collective-permute-start(bf16[16,3072]{1,0:T(8,128)(2,1)} %get-tuple-element.11.refs_4_), channel_id=1, source_target_pairs={{0,8},{1,9},{2,10},{3,11},{4,12},{5,13},{6,14},{7,15},{8,0},{9,1},... | collective-permute-start | bytes 294920 | tf_op jit(solution)/shard_map/ppermute | solution.py:372
  65.5 5.7 %copy-start.9 = (bf16[16,3072]{1,0:T(8,128)(2,1)}, bf16[16,3072]{1,0:T(8,128)(2,1)S(1)}, u32[]{:S(2)}) copy-start(bf16[16,3072]{1,0:T(8,128)(2,1)S(1)} %collective-permute-done.9.refs_3_) | copy-start | bytes 294916
  65.5 5.7 %collective-permute-start.10 = (bf16[16,3072]{1,0:T(8,128)(2,1)}, bf16[16,3072]{1,0:T(8,128)(2,1)S(1)}, u32[]{:S(2)}, u32[]{:S(2)}) collective-permute-start(bf16[16,3072]{1,0:T(8,128)(2,1)} %get-tuple-element.11.refs_4_), channel_id=1, source_target_pairs={{0,4},{1,5},{2,6},{3,7},{4,8},{5,9},{6,10},{7,11},{8,12},{9,13},{1... | collective-permute-start | bytes 294920 | tf_op jit(solution)/shard_map/ppermute | solution.py:372
  66.1 5.1 %copy-start.10 = (bf16[16,3072]{1,0:T(8,128)(2,1)}, bf16[16,3072]{1,0:T(8,128)(2,1)S(1)}, u32[]{:S(2)}) copy-start(bf16[16,3072]{1,0:T(8,128)(2,1)S(1)} %collective-permute-done.8.refs_2_) | copy-start | bytes 294916
  66.2 33.6 %copy-start = (f32[16,16,512]{2,1,0:T(8,128)}, f32[16,16,512]{2,1,0:T(8,128)S(1)}, u32[]{:S(2)}) copy-start(f32[16,16,512]{2,1,0:T(8,128)S(1)} %all-to-all-done.2.own_ref) | copy-start | bytes 1572868
  66.2 33.2 %collective-permute-start = (f32[16,16,512]{2,1,0:T(8,128)S(1)}, f32[16,16,512]{2,1,0:T(8,128)S(1)}, u32[]{:S(2)}, u32[]{:S(2)}) collective-permute-start(f32[16,16,512]{2,1,0:T(8,128)S(1)} %all-to-all-done.2.own_ref), channel_id=1, source_target_pairs={{0,16},{16,0},{32,48},{48,32},{64,80},{80,64},{96,112},{112,96},{1... | collective-permute-start | bytes 1572872 | tf_op jit(solution)/shard_map/ppermute | solution.py:350
  69.4 49.8 %copy-start.1 = (f32[4,208,128]{2,1,0:T(8,128)}, f32[4,208,128]{2,1,0:T(8,128)S(1)}, u32[]{:S(2)}) copy-start(f32[4,208,128]{2,1,0:T(8,128)S(1)} %pad_maximum_fusion.near_ref) | copy-start | bytes 1277956
  69.4 1.9 %copy-start.11 = (bf16[16,3072]{1,0:T(8,128)(2,1)}, bf16[16,3072]{1,0:T(8,128)(2,1)S(1)}, u32[]{:S(2)}) copy-start(bf16[16,3072]{1,0:T(8,128)(2,1)S(1)} %collective-permute-done.7.refs_1_) | copy-start | bytes 294916
  69.4 24.9 %collective-permute-start.4 = (f32[4,208,128]{2,1,0:T(8,128)S(1)}, f32[4,208,128]{2,1,0:T(8,128)S(1)}, u32[]{:S(2)}, u32[]{:S(2)}) collective-permute-start(f32[4,208,128]{2,1,0:T(8,128)S(1)} %pad_maximum_fusion.near_ref), channel_id=1, source_target_pairs={{0,128},{16,144},{32,160},{48,176},{64,192},{80,208},{96,224},{112... | collective-permute-start | bytes 1277960 | tf_op jit(solution)/shard_map/ppermute | solution.py:350
  70.8 0.6 copy-start.12
  70.8 24.0 %collective-permute-start.5 = (f32[4,208,128]{2,1,0:T(8,128)S(1)}, f32[4,208,128]{2,1,0:T(8,128)S(1)}, u32[]{:S(2)}, u32[]{:S(2)}) collective-permute-start(f32[4,208,128]{2,1,0:T(8,128)S(1)} %pad_maximum_fusion.near_ref), channel_id=1, source_target_pairs={{0,16},{16,0},{32,48},{48,32},{64,80},{80,64},{96,112},{112,96},{1... | collective-permute-start | bytes 1277960 | tf_op jit(solution)/shard_map/ppermute | solution.py:350
  71.2 0.7 copy-start.13
  71.9 0.6 copy-start.14
  74.7 21.7 %collective-permute-start.15 = (bf16[64,3072]{1,0:T(8,128)(2,1)}, bf16[64,3072]{1,0:T(8,128)(2,1)S(1)}, u32[]{:S(2)}, u32[]{:S(2)}) collective-permute-start(bf16[64,3072]{1,0:T(8,128)(2,1)} %get-tuple-element.12.refs_0_), channel_id=1, source_target_pairs={{0,12},{1,13},{2,14},{3,15},{4,0},{5,1},{6,2},{7,3},{8,4},{9,5},{1... | collective-permute-start | bytes 1179656 | tf_op jit(solution)/shard_map/ppermute | solution.py:372
  77.5 20.5 %collective-permute-start.14 = (bf16[64,3072]{1,0:T(8,128)(2,1)}, bf16[64,3072]{1,0:T(8,128)(2,1)S(1)}, u32[]{:S(2)}, u32[]{:S(2)}) collective-permute-start(bf16[64,3072]{1,0:T(8,128)(2,1)} %get-tuple-element.12.refs_0_), channel_id=1, source_target_pairs={{0,8},{1,9},{2,10},{3,11},{4,12},{5,13},{6,14},{7,15},{8,0},{9,1},... | collective-permute-start | bytes 1179656 | tf_op jit(solution)/shard_map/ppermute | solution.py:372
  94.3 25.0 %copy-start.3 = (f32[4,208,128]{2,1,0:T(8,128)}, f32[4,208,128]{2,1,0:T(8,128)S(1)}, u32[]{:S(2)}) copy-start(f32[4,208,128]{2,1,0:T(8,128)S(1)} %collective-permute-done.4.far_ref) | copy-start | bytes 1277956
  94.3 25.0 %collective-permute-start.6 = (f32[4,208,128]{2,1,0:T(8,128)S(1)}, f32[4,208,128]{2,1,0:T(8,128)S(1)}, u32[]{:S(2)}, u32[]{:S(2)}) collective-permute-start(f32[4,208,128]{2,1,0:T(8,128)S(1)} %collective-permute-done.4.far_ref), channel_id=1, source_target_pairs={{0,16},{16,0},{32,48},{48,32},{64,80},{80,64},{96,112},{112,96},{1... | collective-permute-start | bytes 1277960 | tf_op jit(solution)/shard_map/ppermute | solution.py:350
  94.9 24.4 %copy-start.4 = (f32[4,208,128]{2,1,0:T(8,128)}, f32[4,208,128]{2,1,0:T(8,128)S(1)}, u32[]{:S(2)}) copy-start(f32[4,208,128]{2,1,0:T(8,128)S(1)} %collective-permute-done.5.twin_near_ref) | copy-start | bytes 1277956
  94.9 24.1 %collective-permute-start.13 = (bf16[64,3072]{1,0:T(8,128)(2,1)}, bf16[64,3072]{1,0:T(8,128)(2,1)}, u32[]{:S(2)}, u32[]{:S(2)}) collective-permute-start(bf16[64,3072]{1,0:T(8,128)(2,1)} %get-tuple-element.12.refs_0_), channel_id=1, source_target_pairs={{0,4},{1,5},{2,6},{3,7},{4,8},{5,9},{6,10},{7,11},{8,12},{9,13},{1... | collective-permute-start | bytes 1179656 | tf_op jit(solution)/shard_map/ppermute | solution.py:372
  96.4 22.8 %copy-start.6 = (bf16[64,3072]{1,0:T(8,128)(2,1)}, bf16[64,3072]{1,0:T(8,128)(2,1)S(1)}, u32[]{:S(2)}) copy-start(bf16[64,3072]{1,0:T(8,128)(2,1)S(1)} %collective-permute-done.15.refs_3_) | copy-start | bytes 1179652
  96.4 22.5 %collective-permute-start.18 = (bf16[64,3072]{1,0:T(8,128)(2,1)}, bf16[64,3072]{1,0:T(8,128)(2,1)}, u32[]{:S(2)}, u32[]{:S(2)}) collective-permute-start(bf16[64,3072]{1,0:T(8,128)(2,1)} %get-tuple-element.13.refs_4_), channel_id=1, source_target_pairs={{0,3},{1,0},{2,1},{3,2},{4,7},{5,4},{6,5},{7,6},{8,11},{9,8},{10,9... | collective-permute-start | bytes 1179656 | tf_op jit(solution)/shard_map/ppermute | solution.py:369
  97.9 21.3 %copy-start.7 = (bf16[64,3072]{1,0:T(8,128)(2,1)}, bf16[64,3072]{1,0:T(8,128)(2,1)S(1)}, u32[]{:S(2)}) copy-start(bf16[64,3072]{1,0:T(8,128)(2,1)S(1)} %collective-permute-done.14.refs_2_) | copy-start | bytes 1179652
  97.9 21.0 %collective-permute-start.17 = (bf16[64,3072]{1,0:T(8,128)(2,1)}, bf16[64,3072]{1,0:T(8,128)(2,1)}, u32[]{:S(2)}, u32[]{:S(2)}) collective-permute-start(bf16[64,3072]{1,0:T(8,128)(2,1)} %get-tuple-element.13.refs_4_), channel_id=1, source_target_pairs={{0,2},{1,3},{2,0},{3,1},{4,6},{5,7},{6,4},{7,5},{8,10},{9,11},{10,... | collective-permute-start | bytes 1179656 | tf_op jit(solution)/shard_map/ppermute | solution.py:369
  99.4 0.8 copy-start.2
  99.4 19.8 %collective-permute-start.16 = (bf16[64,3072]{1,0:T(8,128)(2,1)}, bf16[64,3072]{1,0:T(8,128)(2,1)}, u32[]{:S(2)}, u32[]{:S(2)}) collective-permute-start(bf16[64,3072]{1,0:T(8,128)(2,1)} %get-tuple-element.13.refs_4_), channel_id=1, source_target_pairs={{0,1},{1,2},{2,3},{3,0},{4,5},{5,6},{6,7},{7,4},{8,9},{9,10},{10,1... | collective-permute-start | bytes 1179656 | tf_op jit(solution)/shard_map/ppermute | solution.py:369
  119.3 0.8 copy-start.5

commit v4 on v3

--- a/solution.py
+++ b/solution.py
@@ -14,6 +14,7 @@
 BF16 = jnp.bfloat16
 VMEM = pl.BlockSpec(memory_space=pltpu.VMEM)
 SMEM = pl.BlockSpec(memory_space=pltpu.SMEM)
+ANY = pl.BlockSpec(memory_space=pl.ANY)
 BASE = 128
 BLOCK = 256
 
@@ -80,21 +81,30 @@
         ref[full, pl.ds(start + each * i, each), 0:rest] = last[:, rest * i : rest * i + rest]
 
 
-def pack_cols(at_ref, pruned_ref, h_ref, w_ref, out_ref):
+def pack_cols(pruned_ref, h_hbm, w_hbm, out_ref, h_ref, w_ref, sems):
+    slots, half = out_ref.shape
+    copies = [
+        pltpu.make_async_copy(h_hbm, h_ref, sems.at[0]),
+        pltpu.make_async_copy(w_hbm.at[:, half:], w_ref.at[:, half:], sems.at[1]),
+        pltpu.make_async_copy(w_hbm.at[:, :half], w_ref.at[:, :half], sems.at[2]),
+    ]
+    for copy in copies:
+        copy.start()
     pruned = pruned_ref[...]
-    slots, half = out_ref.shape
     width = h_ref.shape[1]
     tiles = slots // 8
-    pick = one_hot(held(pruned, at_ref[1], width, lambda before: dealt_places(before, tiles, 4)), width)
-    w = w_ref[...]
+    pick = one_hot(held(pruned, lax.axis_index("col"), width, lambda before: dealt_places(before, tiles, 4)), width)
     picked = pick.astype(BF16)
-    first = across(picked, w[:, :half], ((1,), (0,)))
-    last = across(picked, w[:, half:], ((1,), (0,)))
+    copies[0].wait()
     c = across(pick, h_ref[...], ((1,), (1,)), HIGH)
     c_high = c.astype(BF16).astype(F32)
+    copies[1].wait()
+    last = across(picked, w_ref[:, half:], ((1,), (0,)))
     spare = jnp.zeros((slots, lanes_for(width) - width), F32)
     last = jnp.concatenate([last, c_high, spare, c - c_high, spare], axis=1)
     second = lax.broadcasted_iota(jnp.int32, (slots, 1), 0) // 4 % 2
+    copies[2].wait()
+    first = across(picked, w_ref[:, :half], ((1,), (0,)))
     out_ref[...] = jnp.where(second == 1, last, first).astype(BF16)
 
 
@@ -103,7 +113,9 @@
     return hand + tiles * turn
 
 
-def gather_hand(at_ref, pruned_ref, got_ref, low_ref, high_ref, piece_ref, *, height, width):
+def gather_hand(at_ref, pruned_ref, sent_ref, low_ref, high_ref, piece_ref, got_ref, sem, *, height, width):
+    copy = pltpu.make_async_copy(sent_ref, got_ref, sem)
+    copy.start()
     pruned = pruned_ref[...]
     slots, half = got_ref.shape
     tiles = piece_ref.shape[0]
@@ -115,15 +127,14 @@
     hand = at_ref[1]
     turn = (before - hand + tiles - 1) // tiles + turn
     turn = jnp.where(hand + tiles * turn < after, turn, -1)
+    cap = 2 * mine
+    pick = one_hot(held(pruned, at_ref[0], height, in_turn(cap)), height)
+    deal = [one_hot(jnp.where(second == part, turn, -1), mine).astype(BF16) for part in range(2)]
+    copy.wait()
     got = got_ref[...]
-    parts = [
-        across(one_hot(jnp.where(second == part, turn, -1), mine).astype(BF16), got, ((0,), (0,)))
-        for part in range(2)
-    ]
+    parts = [across(d, got, ((0,), (0,))) for d in deal]
     wide = lanes_for(height)
     c = parts[1][:, half - 2 * wide : half - 2 * wide + height] + parts[1][:, half - wide : half - wide + height]
-    cap = 2 * mine
-    pick = one_hot(held(pruned, at_ref[0], height, in_turn(cap)), height)
     piece = across(pick, c, ((1,), (1,)), HIGH)
     for core in range(2):
         part = piece[:, mine // 2 * core : mine // 2 * (core + 1)]
@@ -137,24 +148,35 @@
 
 
 def join(*refs):
-    count = (len(refs) - 2) // 2
+    count = (len(refs) - 3) // 2
+    sems = refs[-1]
+    copies = []
     for path in range(2):
         out = refs[2 * count + path]
         rows = out.shape[0] // count
         for d in range(count):
-            out[rows * d : rows * d + rows, :] = refs[count * path + d][...]
-
-
-def pack_slab(first_ref, got_ref, out_ref, slab_ref):
+            i = count * path + d
+            copies.append(pltpu.make_async_copy(refs[i], out.at[rows * d : rows * d + rows, :], sems.at[i]))
+            copies[-1].start()
+    for copy in copies:
+        copy.wait()
+
+
+def pack_slab(pruned_ref, got_ref, out_ref, slab_ref, *, width):
     tiles, mine, n = out_ref.shape
     groups = got_ref.shape[2] // mine
+    first = first_places(pruned_ref[...], tiles, width)
     for t in range(tiles):
         got = got_ref[t]
         for i in range(groups):
-            slab_ref[pl.ds(first_ref[t] + 8 * i, 8), 0:mine] = got[:, mine * i : mine * i + mine]
+            slab_ref[pl.ds(first[t] + 8 * i, 8), 0:mine] = got[:, mine * i : mine * i + mine]
     slab = slab_ref[0:n, :].T[0:mine, :]
     for d in range(tiles):
         out_ref[d] = slab
+
+
+def first_places(pruned, tiles, width):
+    return [jnp.sum(jnp.where(pruned < t * width, 1, 0)) for t in range(tiles)]
 
 
 def spread(v, i):
@@ -253,11 +275,12 @@
         work.pop(0)()
 
 
-def update(first_ref, at_ref, pruned_ref, inv_ref, near_ref, far_ref, twin_near_ref, twin_far_ref, *refs):
+def update(at_ref, pruned_ref, inv_ref, near_ref, far_ref, twin_near_ref, twin_far_ref, *refs):
     blocks, (h_ref, w_ref, h_out, w_out, panel_ref, w_new_ref, h_new_ref, sems) = refs[:-8], refs[-8:]
     strips, n, _ = inv_ref.shape
     width = h_ref.shape[1]
-    tiles = first_ref.shape[0]
+    tiles = 4 * near_ref.shape[0]
+    first = first_places(pruned_ref[...], tiles, h_ref.shape[0])
     cap = 2 * n // tiles
     side = len(blocks) // 2
     rows_w = w_ref.shape[1]
@@ -269,7 +292,7 @@
         of = apart % near
         own = jnp.where(apart < near, near_ref[of], far_ref[of])
         twin = jnp.where(apart < near, twin_near_ref[of], twin_far_ref[of])
-        place_strips(panel_ref, first_ref[t], jnp.where(core == t % 2, own, twin), cap, width)
+        place_strips(panel_ref, first[t], jnp.where(core == t % 2, own, twin), cap, width)
     panel = jnp.concatenate([panel_ref[j, 0:n, :] for j in range(panel_ref.shape[0])], axis=1).T[:width, :]
     x, y = at_ref[1] % side, at_ref[1] // side
     hands = []
@@ -326,16 +349,19 @@
     at = jnp.stack([lax.axis_index("row"), lax.axis_index("col")]).astype(jnp.int32)
     weights = weights.T
     listed = pruned.reshape(1, n)
-    edges = jnp.arange(tiles, dtype=jnp.int32) * tile_cols
-    first = jnp.sum((listed < edges[:, None]).astype(jnp.int32), axis=1)
     length = rows_w + 2 * lanes_for(tile_rows)
     hands = pl.pallas_call(
         pack_cols,
         out_shape=jax.ShapeDtypeStruct((8 * tiles, length // 2), BF16),
-        in_specs=[SMEM, VMEM, VMEM, VMEM],
+        in_specs=[VMEM, ANY, ANY],
         out_specs=VMEM,
+        scratch_shapes=[
+            pltpu.VMEM(hessian_inverse.shape, F32),
+            pltpu.VMEM(weights.shape, BF16),
+            pltpu.SemaphoreType.DMA((3,)),
+        ],
         name="pack_cols",
-    )(at, listed, hessian_inverse, weights)
+    )(listed, hessian_inverse, weights)
     hands = sent_to_all(hands, "col")
     mine = n // tiles
     rows = pl.pallas_call(
@@ -358,8 +384,9 @@
             jax.ShapeDtypeStruct((mine // 2, length), BF16),
             jax.ShapeDtypeStruct((tiles, 8, cap // 8 * (mine // 2)), F32),
         ),
-        in_specs=[SMEM, VMEM, VMEM],
+        in_specs=[SMEM, VMEM, ANY],
         out_specs=(VMEM, VMEM, VMEM),
+        scratch_shapes=[pltpu.VMEM(hands.shape, BF16), pltpu.SemaphoreType.DMA(())],
         name="gather_hand",
     )(at, listed, hands)
     pieces = sent_to_all(pieces, "row")
@@ -374,19 +401,20 @@
     lows = [low] + [along_x(low, d) for d in range(1, side)]
     highs = [high] + [along_y(high, d) for d in range(1, side)]
     slab = pl.pallas_call(
-        pack_slab,
+        functools.partial(pack_slab, width=tile_rows),
         out_shape=jax.ShapeDtypeStruct((tiles, mine // 2, n), F32),
-        in_specs=[SMEM, VMEM],
+        in_specs=[VMEM, VMEM],
         out_specs=VMEM,
         scratch_shapes=[pltpu.VMEM((n + cap, 128), F32)],
         name="pack_slab",
-    )(first, pieces)
+    )(listed, pieces)
     slab = sent_to_all(slab, "col")
     low, high = pl.pallas_call(
         join,
         out_shape=(jax.ShapeDtypeStruct((side * mine // 2, length), BF16),) * 2,
-        in_specs=[VMEM] * (2 * side),
-        out_specs=(VMEM, VMEM),
+        in_specs=[ANY] * (2 * side),
+        out_specs=(ANY, ANY),
+        scratch_shapes=[pltpu.SemaphoreType.DMA((2 * side,))],
         name="join",
     )(*lows, *highs)
     cols = [low] + [along_y(low, d) for d in range(1, side)]
@@ -403,15 +431,14 @@
         name="invert",
     )(at, slab, slab_twin)
     twin_far = swapped(far_rows, 1)
-    anywhere = pl.BlockSpec(memory_space=pl.ANY)
     h_new, w_new = pl.pallas_call(
         update,
         out_shape=(
             jax.ShapeDtypeStruct(hessian_inverse.shape, F32),
             jax.ShapeDtypeStruct(weights.shape, F32),
         ),
-        in_specs=[SMEM, SMEM] + [VMEM] * (8 + len(cols)),
-        out_specs=(anywhere, anywhere),
+        in_specs=[SMEM] + [VMEM] * (8 + len(cols)),
+        out_specs=(ANY, ANY),
         scratch_shapes=[
             pltpu.VMEM((-(-tile_cols // 128), n + cap, 128), F32),
             pltpu.VMEM(weights.shape, F32),
@@ -420,7 +447,7 @@
         ],
         name="update",
     )(
-        first, at, listed, inverse, near_rows, far_rows, twin_near, twin_far, *cols, hessian_inverse, weights
+        at, listed, inverse, near_rows, far_rows, twin_near, twin_far, *cols, hessian_inverse, weights
     )
     return h_new, w_new.T
 

time: 131 us -> 153 us (1.17)
  Pallas kernels: 41.6 us -> 65.5 us
  starting transfers between devices: 37.6 us -> 34.2 us
  waiting for transfers between devices: 27.4 us -> 29.1 us
    pallas_call x1, Pallas kernels: 2.14 us -> 25 us  [on_device(): pl.pallas_call(join, out_shape=(jax.ShapeDtypeStruct((side * mine // 2, l...]
    ppermute x7, waiting for transfers between devices: 20.1 us -> 3.82 us  [swapped(): return lax.ppermute(value, 'row', [(i, i ^ mask) for i in range(tiles)])]
    ppermute x6, waiting for transfers between devices: 0.02 us -> 15.5 us  [along_y(): lax.ppermute(value, 'col', [(c, (c + d * side) % tiles) for c in range(ti...]
    all_to_all x2, starting transfers between devices: 13.9 us -> 11.2 us  [sent_to_all(): return lax.all_to_all(copies, axis, split_axis=0, concat_axis=0, tiled=True)]
    all_to_all x2, waiting for transfers between devices: 7 us -> 8.58 us  [sent_to_all(): return lax.all_to_all(copies, axis, split_axis=0, concat_axis=0, tiled=True)]
    unnamed x32 -> x30, local copies, waits for them, and re-layouts: 3.12 us -> 3 us
  transfers between devices with their start and end apart: 21 -> 21, of which waited for: 4 -> 4; matrix products, arithmetic and copies ran while one was open for 1% -> 1% of each run, Pallas kernels for 18% -> 30%
where the time goes in v4:
time: 153 us
  Pallas kernels  65.5 us (43%)
  starting transfers between devices  34.2 us (22%)
  waiting for transfers between devices  29.1 us (19%)
  blocking collectives  18.2 us (12%)
  local copies, waits for them, and re-layouts  3 us (2%)
  other arithmetic  1.57 us (1%)
    pallas_call x1, Pallas kernels, on_device(): pl.pallas_call(join, out_shape=(jax.ShapeDtypeStruct((side * mine // 2, l...  25 us
    pallas_call x1, Pallas kernels, on_device(): pl.pallas_call(invert, out_shape=jax.ShapeDtypeStruct((n // BASE, n, BASE...  18.7 us
    all_to_all x1, blocking collectives, sent_to_all(): return lax.all_to_all(copies, axis, split_axis=0, concat_axis=0, tiled=True)  18.2 us
    ppermute x6, waiting for transfers between devices, along_y(): lax.ppermute(value, 'col', [(c, (c + d * side) % tiles) for c in range(ti...  15.5 us
    all_to_all x2, starting transfers between devices, sent_to_all(): return lax.all_to_all(copies, axis, split_axis=0, concat_axis=0, tiled=True)  11.2 us
    pallas_call x1, Pallas kernels, on_device(): pl.pallas_call(update, out_shape=(jax.ShapeDtypeStruct(hessian_inverse.sh...  9.76 us
    all_to_all x2, waiting for transfers between devices, sent_to_all(): return lax.all_to_all(copies, axis, split_axis=0, concat_axis=0, tiled=True)  8.58 us
    ppermute x7, starting transfers between devices, swapped(): return lax.ppermute(value, 'row', [(i, i ^ mask) for i in range(tiles)])  8.32 us
  transfers between devices with their start and end apart: 21, of which 4 were waited for; matrix products, arithmetic and copies ran while one was open for 1% of the time, Pallas kernels for 30%

profile of v4, /device:TPU:1, one launch (start us, length us, event | category | flops | bytes accessed | tf_op | source)
XLA Modules:
  0.0 152.6 jit_solution(9098225645092724354)
XLA Ops:
  0.6 4.4 %pack_cols.1 = bf16[128,1536]{1,0:T(8,128)(2,1)} custom-call(s32[1,512]{1,0:T(1,128)} %bitcast.19, f32[416,416]{1,0:T(8,128)} %refs_8_.1, bf16[416,2048]{1,0:T(8,128)(2,1)} %bitcast.11), custom_call_target="tpu_custom_call" | custom-call | tf_op jit(solution)/shard_map/pack_cols/pallas_call | solution.py:353
  5.0 7.6 %all-to-all-start = ((bf16[16,8,1536]{2,1,0:T(8,128)(2,1)}), bf16[16,8,1536]{2,1,0:T(8,128)(2,1)S(1)}, u32[]{:S(2)}, u32[]{:S(2)}) async-start(bf16[16,8,1536]{2,1,0:T(8,128)(2,1)} %bitcast.14), calls=%async_computation | async-start | bytes 786432 | tf_op jit(solution)/shard_map/all_to_all | solution.py:340
  12.6 0.6 pad_add_fusion.at_ref
  13.2 8.6 %all-to-all-done = bf16[16,8,1536]{2,1,0:T(8,128)(2,1)S(1)} async-done(((bf16[16,8,1536]{2,1,0:T(8,128)(2,1)}), bf16[16,8,1536]{2,1,0:T(8,128)(2,1)S(1)}, u32[]{:S(2)}, u32[]{:S(2)}) %all-to-all-start) | async-done | bytes 393248 | tf_op jit(solution)/shard_map/all_to_all | solution.py:340
  21.8 0.7 copy-done.2
  22.6 3.1 %gather_hand.1 = (bf16[16,3072]{1,0:T(8,128)(2,1)}, bf16[16,3072]{1,0:T(8,128)(2,1)}, f32[16,8,128]{2,1,0:T(8,128)}) custom-call(s32[2]{0:T(128)} %pad_add_fusion.at_ref, s32[1,512]{1,0:T(1,128)} %bitcast.20, bf16[128,1536]{1,0:T(8,128)(2,1)} %bitcast.13), custom_call_target="tpu_custom_call" | custom-call | tf_op jit(solution)/shard_map/gather_hand/pallas_call | solution.py:380
  25.6 18.2 %all_to_all.21.got_ref = f32[16,8,128]{2,1,0:T(8,128)} all-to-all(f32[16,8,128]{2,1,0:T(8,128)} %get-tuple-element.9), channel_id=1, replica_groups=mesh['row'=16,'col'=16] {'row'}, dimensions={0} | all-to-all | bytes 131072 | tf_op jit(solution)/shard_map/all_to_all | solution.py:340
  43.8 2.0 %pack_slab.1 = f32[16,16,512]{2,1,0:T(8,128)} custom-call(s32[1,512]{1,0:T(1,128)} %bitcast.21, f32[16,8,128]{2,1,0:T(8,128)} %all_to_all.21.got_ref), custom_call_target="tpu_custom_call" | custom-call | tf_op jit(solution)/shard_map/pack_slab/pallas_call | solution.py:403
  45.8 3.6 %all-to-all-start.2 = ((f32[16,16,512]{2,1,0:T(8,128)}), f32[16,16,512]{2,1,0:T(8,128)S(1)}, u32[]{:S(2)}, u32[]{:S(2)}) async-start(f32[16,16,512]{2,1,0:T(8,128)} %pack_slab.1), calls=%async_computation.2 | async-start | bytes 1048576 | tf_op jit(solution)/shard_map/all_to_all | solution.py:340
  49.4 2.6 %pack_rows.1 = f32[208,128]{1,0:T(8,128)} custom-call(s32[2]{0:T(128)} %pad_add_fusion.at_ref, s32[1,512]{1,0:T(1,128)} %bitcast.22, f32[416,416]{1,0:T(8,128)} %refs_8_.1), custom_call_target="tpu_custom_call" | custom-call | tf_op jit(solution)/shard_map/pack_rows/pallas_call | solution.py:367
  52.0 0.3 collective-permute-start.3
  52.4 1.1 collective-permute-start.2
  53.4 2.2 %collective-permute-start.1 = (f32[208,128]{1,0:T(8,128)}, f32[208,128]{1,0:T(8,128)S(1)}, u32[]{:S(2)}, u32[]{:S(2)}) collective-permute-start(f32[208,128]{1,0:T(8,128)} %pack_rows.1), channel_id=1, source_target_pairs={{0,32},{16,48},{32,0},{48,16},{64,96},{80,112},{96,64},{112,80},{1... | collective-permute-start | bytes 319496 | tf_op jit(solution)/shard_map/ppermute | solution.py:376
  55.6 2.5 %collective-permute-start.9 = (bf16[16,3072]{1,0:T(8,128)(2,1)}, bf16[16,3072]{1,0:T(8,128)(2,1)S(1)}, u32[]{:S(2)}, u32[]{:S(2)}) collective-permute-start(bf16[16,3072]{1,0:T(8,128)(2,1)} %get-tuple-element.10.refs_0_), channel_id=1, source_target_pairs={{0,3},{1,0},{2,1},{3,2},{4,7},{5,4},{6,5},{7,6},{8,11},{9,8},{10,9... | collective-permute-start | bytes 294920 | tf_op jit(solution)/shard_map/ppermute | solution.py:396
  58.0 0.6 collective-permute-start.8
  58.6 0.0 collective-permute-done.3
  58.6 0.8 collective-permute-start.7
  59.4 3.8 %collective-permute-done.2 = f32[208,128]{1,0:T(8,128)S(1)} collective-permute-done((f32[208,128]{1,0:T(8,128)}, f32[208,128]{1,0:T(8,128)S(1)}, u32[]{:S(2)}, u32[]{:S(2)}) %collective-permute-start.2) | collective-permute-done | bytes 106528 | tf_op jit(solution)/shard_map/ppermute | solution.py:376
  63.3 2.3 %collective-permute-start.12 = (bf16[16,3072]{1,0:T(8,128)(2,1)}, bf16[16,3072]{1,0:T(8,128)(2,1)S(1)}, u32[]{:S(2)}, u32[]{:S(2)}) collective-permute-start(bf16[16,3072]{1,0:T(8,128)(2,1)} %get-tuple-element.11.refs_4_), channel_id=1, source_target_pairs={{0,12},{1,13},{2,14},{3,15},{4,0},{5,1},{6,2},{7,3},{8,4},{9,5},{1... | collective-permute-start | bytes 294920 | tf_op jit(solution)/shard_map/ppermute | solution.py:399
  65.5 0.0 collective-permute-done.1
  65.5 0.5 collective-permute-start.11
  66.1 0.6 collective-permute-start.10
  66.7 0.0 collective-permute-done.8.refs_2_
  66.7 0.0 copy-start
  66.7 2.3 %collective-permute-start = (f32[16,16,512]{2,1,0:T(8,128)S(1)}, f32[16,16,512]{2,1,0:T(8,128)S(1)}, u32[]{:S(2)}, u32[]{:S(2)}) collective-permute-start(f32[16,16,512]{2,1,0:T(8,128)S(1)} %all-to-all-done.2.own_ref), channel_id=1, source_target_pairs={{0,16},{16,0},{32,48},{48,32},{64,80},{80,64},{96,112},{112,96},{1... | collective-permute-start | bytes 1572872 | tf_op jit(solution)/shard_map/ppermute | solution.py:376
  69.0 0.9 pad_maximum_fusion.near_ref
  69.9 0.0 collective-permute-done.7.refs_1_
  69.9 0.0 copy-start.11
  70.0 1.4 collective-permute-start.4
  71.4 0.0 collective-permute-done.12.refs_7_
  71.4 0.4 collective-permute-start.5
  71.8 0.2 copy-done.12
  72.0 0.4 copy-done.13
  72.4 0.6 copy-done.14
  73.1 25.0 %join.1 = (bf16[64,3072]{1,0:T(8,128)(2,1)}, bf16[64,3072]{1,0:T(8,128)(2,1)}) custom-call(bf16[16,3072]{1,0:T(8,128)(2,1)} %get-tuple-element.10.refs_0_, bf16[16,3072]{1,0:T(8,128)(2,1)} %copy-done.11, bf16[16,3072]{1,0:T(8,128)(2,1)} %copy-done.10, bf16[16,3072]{1,0:T(8,128)(2,1)} %copy-done.9, bf16[16,3072]{1,0:T(8,128)(2,1)} %get-tuple-element.11.refs_4_, ...), custom_call_target="tpu_custom_call" | custom-call | tf_op jit(solution)/shard_map/join/pallas_call | solution.py:412
  98.1 3.0 %collective-permute-start.15 = (bf16[64,3072]{1,0:T(8,128)(2,1)}, bf16[64,3072]{1,0:T(8,128)(2,1)S(1)}, u32[]{:S(2)}, u32[]{:S(2)}) collective-permute-start(bf16[64,3072]{1,0:T(8,128)(2,1)} %get-tuple-element.12.refs_0_), channel_id=1, source_target_pairs={{0,12},{1,13},{2,14},{3,15},{4,0},{5,1},{6,2},{7,3},{8,4},{9,5},{1... | collective-permute-start | bytes 1179656 | tf_op jit(solution)/shard_map/ppermute | solution.py:399
  101.1 0.5 collective-permute-start.14
  101.6 0.7 collective-permute-start.6
  102.3 0.3 collective-permute-start.13
  102.6 15.5 %collective-permute-done.15.refs_3_ = bf16[64,3072]{1,0:T(8,128)(2,1)S(1)} collective-permute-done((bf16[64,3072]{1,0:T(8,128)(2,1)}, bf16[64,3072]{1,0:T(8,128)(2,1)S(1)}, u32[]{:S(2)}, u32[]{:S(2)}) %collective-permute-start.15) | collective-permute-done | bytes 393248 | tf_op jit(solution)/shard_map/ppermute | solution.py:399
  118.1 2.4 %collective-permute-start.18 = (bf16[64,3072]{1,0:T(8,128)(2,1)}, bf16[64,3072]{1,0:T(8,128)(2,1)}, u32[]{:S(2)}, u32[]{:S(2)}) collective-permute-start(bf16[64,3072]{1,0:T(8,128)(2,1)} %get-tuple-element.13.refs_4_), channel_id=1, source_target_pairs={{0,3},{1,0},{2,1},{3,2},{4,7},{5,4},{6,5},{7,6},{8,11},{9,8},{10,9... | collective-permute-start | bytes 1179656 | tf_op jit(solution)/shard_map/ppermute | solution.py:396
  120.6 0.6 collective-permute-start.17
  121.1 0.6 collective-permute-start.16
  121.7 0.2 copy-done.3
  121.9 18.7 %invert.1.inv_ref = f32[4,512,128]{2,1,0:T(8,128)} custom-call(s32[2]{0:T(128)} %pad_add_fusion.at_ref, f32[16,16,512]{2,1,0:T(8,128)} %copy-done, f32[16,16,512]{2,1,0:T(8,128)} %copy-done.3), custom_call_target="tpu_custom_call" | custom-call | tf_op jit(solution)/shard_map/invert/pallas_call | solution.py:425
  140.7 1.2 collective-permute-done.16.refs_5_
  141.9 0.8 copy-done.6
  142.7 9.8 %update.1 = (f32[416,416]{1,0:T(8,128)}, f32[416,2048]{1,0:T(8,128)}) custom-call(s32[2]{0:T(128)} %pad_add_fusion.at_ref, s32[1,512]{1,0:T(1,128)} %bitcast.23, f32[4,512,128]{2,1,0:T(8,128)} %invert.1.inv_ref, f32[4,208,128]{2,1,0:T(8,128)} %copy-done.1, f32[4,208,128]{2,1,0:T(8,128)} %copy-done.4, f32[4,208,128]{2,1,0:T(8,128)} %copy-done.5, ...), custom_call_target="tpu_custom_call" | custom-call | tf_op jit(solution)/shard_map/update/pallas_call | solution.py:434
  (34 shorter events, 0.1 us)
Async XLA Ops:
  5.0 16.8 %all-to-all-start = ((bf16[16,8,1536]{2,1,0:T(8,128)(2,1)}), bf16[16,8,1536]{2,1,0:T(8,128)(2,1)S(1)}, u32[]{:S(2)}, u32[]{:S(2)}) async-start(bf16[16,8,1536]{2,1,0:T(8,128)(2,1)} %bitcast.14), calls=%async_computation | async-start | bytes 786432 | tf_op jit(solution)/shard_map/all_to_all | solution.py:340
  21.8 0.7 copy-start.2
  45.8 20.9 %all-to-all-start.2 = ((f32[16,16,512]{2,1,0:T(8,128)}), f32[16,16,512]{2,1,0:T(8,128)S(1)}, u32[]{:S(2)}, u32[]{:S(2)}) async-start(f32[16,16,512]{2,1,0:T(8,128)} %pack_slab.1), calls=%async_computation.2 | async-start | bytes 1048576 | tf_op jit(solution)/shard_map/all_to_all | solution.py:340
  52.0 6.6 %collective-permute-start.3 = (f32[208,128]{1,0:T(8,128)}, f32[208,128]{1,0:T(8,128)S(1)}, u32[]{:S(2)}, u32[]{:S(2)}) collective-permute-start(f32[208,128]{1,0:T(8,128)} %pack_rows.1), channel_id=1, source_target_pairs={{0,96},{16,112},{32,64},{48,80},{64,32},{80,48},{96,0},{112,16},{1... | collective-permute-start | bytes 319496 | tf_op jit(solution)/shard_map/ppermute | solution.py:376
  52.4 10.9 %collective-permute-start.2 = (f32[208,128]{1,0:T(8,128)}, f32[208,128]{1,0:T(8,128)S(1)}, u32[]{:S(2)}, u32[]{:S(2)}) collective-permute-start(f32[208,128]{1,0:T(8,128)} %pack_rows.1), channel_id=1, source_target_pairs={{0,64},{16,80},{32,96},{48,112},{64,0},{80,16},{96,32},{112,48},{1... | collective-permute-start | bytes 319496 | tf_op jit(solution)/shard_map/ppermute | solution.py:376
  53.4 12.1 %collective-permute-start.1 = (f32[208,128]{1,0:T(8,128)}, f32[208,128]{1,0:T(8,128)S(1)}, u32[]{:S(2)}, u32[]{:S(2)}) collective-permute-start(f32[208,128]{1,0:T(8,128)} %pack_rows.1), channel_id=1, source_target_pairs={{0,32},{16,48},{32,0},{48,16},{64,96},{80,112},{96,64},{112,80},{1... | collective-permute-start | bytes 319496 | tf_op jit(solution)/shard_map/ppermute | solution.py:376
  55.6 10.5 %collective-permute-start.9 = (bf16[16,3072]{1,0:T(8,128)(2,1)}, bf16[16,3072]{1,0:T(8,128)(2,1)S(1)}, u32[]{:S(2)}, u32[]{:S(2)}) collective-permute-start(bf16[16,3072]{1,0:T(8,128)(2,1)} %get-tuple-element.10.refs_0_), channel_id=1, source_target_pairs={{0,3},{1,0},{2,1},{3,2},{4,7},{5,4},{6,5},{7,6},{8,11},{9,8},{10,9... | collective-permute-start | bytes 294920 | tf_op jit(solution)/shard_map/ppermute | solution.py:396
  58.0 8.6 %collective-permute-start.8 = (bf16[16,3072]{1,0:T(8,128)(2,1)}, bf16[16,3072]{1,0:T(8,128)(2,1)S(1)}, u32[]{:S(2)}, u32[]{:S(2)}) collective-permute-start(bf16[16,3072]{1,0:T(8,128)(2,1)} %get-tuple-element.10.refs_0_), channel_id=1, source_target_pairs={{0,2},{1,3},{2,0},{3,1},{4,6},{5,7},{6,4},{7,5},{8,10},{9,11},{10,... | collective-permute-start | bytes 294920 | tf_op jit(solution)/shard_map/ppermute | solution.py:396
  58.6 11.3 %collective-permute-start.7 = (bf16[16,3072]{1,0:T(8,128)(2,1)}, bf16[16,3072]{1,0:T(8,128)(2,1)S(1)}, u32[]{:S(2)}, u32[]{:S(2)}) collective-permute-start(bf16[16,3072]{1,0:T(8,128)(2,1)} %get-tuple-element.10.refs_0_), channel_id=1, source_target_pairs={{0,1},{1,2},{2,3},{3,0},{4,5},{5,6},{6,7},{7,4},{8,9},{9,10},{10,1... | collective-permute-start | bytes 294920 | tf_op jit(solution)/shard_map/ppermute | solution.py:396
  63.3 8.1 %collective-permute-start.12 = (bf16[16,3072]{1,0:T(8,128)(2,1)}, bf16[16,3072]{1,0:T(8,128)(2,1)S(1)}, u32[]{:S(2)}, u32[]{:S(2)}) collective-permute-start(bf16[16,3072]{1,0:T(8,128)(2,1)} %get-tuple-element.11.refs_4_), channel_id=1, source_target_pairs={{0,12},{1,13},{2,14},{3,15},{4,0},{5,1},{6,2},{7,3},{8,4},{9,5},{1... | collective-permute-start | bytes 294920 | tf_op jit(solution)/shard_map/ppermute | solution.py:399
  65.5 6.2 %collective-permute-start.11 = (bf16[16,3072]{1,0:T(8,128)(2,1)}, bf16[16,3072]{1,0:T(8,128)(2,1)S(1)}, u32[]{:S(2)}, u32[]{:S(2)}) collective-permute-start(bf16[16,3072]{1,0:T(8,128)(2,1)} %get-tuple-element.11.refs_4_), channel_id=1, source_target_pairs={{0,8},{1,9},{2,10},{3,11},{4,12},{5,13},{6,14},{7,15},{8,0},{9,1},... | collective-permute-start | bytes 294920 | tf_op jit(solution)/shard_map/ppermute | solution.py:399
  66.1 5.7 %copy-start.9 = (bf16[16,3072]{1,0:T(8,128)(2,1)}, bf16[16,3072]{1,0:T(8,128)(2,1)S(1)}, u32[]{:S(2)}) copy-start(bf16[16,3072]{1,0:T(8,128)(2,1)S(1)} %collective-permute-done.9.refs_3_) | copy-start | bytes 294916
  66.1 5.7 %collective-permute-start.10 = (bf16[16,3072]{1,0:T(8,128)(2,1)}, bf16[16,3072]{1,0:T(8,128)(2,1)S(1)}, u32[]{:S(2)}, u32[]{:S(2)}) collective-permute-start(bf16[16,3072]{1,0:T(8,128)(2,1)} %get-tuple-element.11.refs_4_), channel_id=1, source_target_pairs={{0,4},{1,5},{2,6},{3,7},{4,8},{5,9},{6,10},{7,11},{8,12},{9,13},{1... | collective-permute-start | bytes 294920 | tf_op jit(solution)/shard_map/ppermute | solution.py:399
  66.7 5.1 %copy-start.10 = (bf16[16,3072]{1,0:T(8,128)(2,1)}, bf16[16,3072]{1,0:T(8,128)(2,1)S(1)}, u32[]{:S(2)}) copy-start(bf16[16,3072]{1,0:T(8,128)(2,1)S(1)} %collective-permute-done.8.refs_2_) | copy-start | bytes 294916
  66.7 55.0 %copy-start = (f32[16,16,512]{2,1,0:T(8,128)}, f32[16,16,512]{2,1,0:T(8,128)S(1)}, u32[]{:S(2)}) copy-start(f32[16,16,512]{2,1,0:T(8,128)S(1)} %all-to-all-done.2.own_ref) | copy-start | bytes 1572868
  66.7 54.4 %collective-permute-start = (f32[16,16,512]{2,1,0:T(8,128)S(1)}, f32[16,16,512]{2,1,0:T(8,128)S(1)}, u32[]{:S(2)}, u32[]{:S(2)}) collective-permute-start(f32[16,16,512]{2,1,0:T(8,128)S(1)} %all-to-all-done.2.own_ref), channel_id=1, source_target_pairs={{0,16},{16,0},{32,48},{48,32},{64,80},{80,64},{96,112},{112,96},{1... | collective-permute-start | bytes 1572872 | tf_op jit(solution)/shard_map/ppermute | solution.py:376
  69.9 71.9 %copy-start.1 = (f32[4,208,128]{2,1,0:T(8,128)}, f32[4,208,128]{2,1,0:T(8,128)S(1)}, u32[]{:S(2)}) copy-start(f32[4,208,128]{2,1,0:T(8,128)S(1)} %pad_maximum_fusion.near_ref) | copy-start | bytes 1277956
  69.9 1.9 %copy-start.11 = (bf16[16,3072]{1,0:T(8,128)(2,1)}, bf16[16,3072]{1,0:T(8,128)(2,1)S(1)}, u32[]{:S(2)}) copy-start(bf16[16,3072]{1,0:T(8,128)(2,1)S(1)} %collective-permute-done.7.refs_1_) | copy-start | bytes 294916
  70.0 31.7 %collective-permute-start.4 = (f32[4,208,128]{2,1,0:T(8,128)S(1)}, f32[4,208,128]{2,1,0:T(8,128)S(1)}, u32[]{:S(2)}, u32[]{:S(2)}) collective-permute-start(f32[4,208,128]{2,1,0:T(8,128)S(1)} %pad_maximum_fusion.near_ref), channel_id=1, source_target_pairs={{0,128},{16,144},{32,160},{48,176},{64,192},{80,208},{96,224},{112... | collective-permute-start | bytes 1277960 | tf_op jit(solution)/shard_map/ppermute | solution.py:376
  71.4 0.6 copy-start.12
  71.4 30.9 %collective-permute-start.5 = (f32[4,208,128]{2,1,0:T(8,128)S(1)}, f32[4,208,128]{2,1,0:T(8,128)S(1)}, u32[]{:S(2)}, u32[]{:S(2)}) collective-permute-start(f32[4,208,128]{2,1,0:T(8,128)S(1)} %pad_maximum_fusion.near_ref), channel_id=1, source_target_pairs={{0,16},{16,0},{32,48},{48,32},{64,80},{80,64},{96,112},{112,96},{1... | collective-permute-start | bytes 1277960 | tf_op jit(solution)/shard_map/ppermute | solution.py:376
  71.8 0.6 copy-start.13
  72.4 0.6 copy-start.14
  98.1 20.1 %collective-permute-start.15 = (bf16[64,3072]{1,0:T(8,128)(2,1)}, bf16[64,3072]{1,0:T(8,128)(2,1)S(1)}, u32[]{:S(2)}, u32[]{:S(2)}) collective-permute-start(bf16[64,3072]{1,0:T(8,128)(2,1)} %get-tuple-element.12.refs_0_), channel_id=1, source_target_pairs={{0,12},{1,13},{2,14},{3,15},{4,0},{5,1},{6,2},{7,3},{8,4},{9,5},{1... | collective-permute-start | bytes 1179656 | tf_op jit(solution)/shard_map/ppermute | solution.py:399
  101.1 19.5 %collective-permute-start.14 = (bf16[64,3072]{1,0:T(8,128)(2,1)}, bf16[64,3072]{1,0:T(8,128)(2,1)S(1)}, u32[]{:S(2)}, u32[]{:S(2)}) collective-permute-start(bf16[64,3072]{1,0:T(8,128)(2,1)} %get-tuple-element.12.refs_0_), channel_id=1, source_target_pairs={{0,8},{1,9},{2,10},{3,11},{4,12},{5,13},{6,14},{7,15},{8,0},{9,1},... | collective-permute-start | bytes 1179656 | tf_op jit(solution)/shard_map/ppermute | solution.py:399
  101.6 40.2 %copy-start.4 = (f32[4,208,128]{2,1,0:T(8,128)}, f32[4,208,128]{2,1,0:T(8,128)S(1)}, u32[]{:S(2)}) copy-start(f32[4,208,128]{2,1,0:T(8,128)S(1)} %collective-permute-done.4.far_ref) | copy-start | bytes 1277956
  101.6 40.2 %collective-permute-start.6 = (f32[4,208,128]{2,1,0:T(8,128)S(1)}, f32[4,208,128]{2,1,0:T(8,128)S(1)}, u32[]{:S(2)}, u32[]{:S(2)}) collective-permute-start(f32[4,208,128]{2,1,0:T(8,128)S(1)} %collective-permute-done.4.far_ref), channel_id=1, source_target_pairs={{0,16},{16,0},{32,48},{48,32},{64,80},{80,64},{96,112},{112,96},{1... | collective-permute-start | bytes 1277960 | tf_op jit(solution)/shard_map/ppermute | solution.py:376
  102.3 39.6 %copy-start.5 = (f32[4,208,128]{2,1,0:T(8,128)}, f32[4,208,128]{2,1,0:T(8,128)S(1)}, u32[]{:S(2)}) copy-start(f32[4,208,128]{2,1,0:T(8,128)S(1)} %collective-permute-done.5.twin_near_ref) | copy-start | bytes 1277956
  102.3 38.4 %collective-permute-start.13 = (bf16[64,3072]{1,0:T(8,128)(2,1)}, bf16[64,3072]{1,0:T(8,128)(2,1)}, u32[]{:S(2)}, u32[]{:S(2)}) collective-permute-start(bf16[64,3072]{1,0:T(8,128)(2,1)} %get-tuple-element.12.refs_0_), channel_id=1, source_target_pairs={{0,4},{1,5},{2,6},{3,7},{4,8},{5,9},{6,10},{7,11},{8,12},{9,13},{1... | collective-permute-start | bytes 1179656 | tf_op jit(solution)/shard_map/ppermute | solution.py:399
  118.1 23.7 %copy-start.7 = (bf16[64,3072]{1,0:T(8,128)(2,1)}, bf16[64,3072]{1,0:T(8,128)(2,1)S(1)}, u32[]{:S(2)}) copy-start(bf16[64,3072]{1,0:T(8,128)(2,1)S(1)} %collective-permute-done.15.refs_3_) | copy-start | bytes 1179652
  118.1 22.5 %collective-permute-start.18 = (bf16[64,3072]{1,0:T(8,128)(2,1)}, bf16[64,3072]{1,0:T(8,128)(2,1)}, u32[]{:S(2)}, u32[]{:S(2)}) collective-permute-start(bf16[64,3072]{1,0:T(8,128)(2,1)} %get-tuple-element.13.refs_4_), channel_id=1, source_target_pairs={{0,3},{1,0},{2,1},{3,2},{4,7},{5,4},{6,5},{7,6},{8,11},{9,8},{10,9... | collective-permute-start | bytes 1179656 | tf_op jit(solution)/shard_map/ppermute | solution.py:396
  120.6 21.3 %copy-start.8 = (bf16[64,3072]{1,0:T(8,128)(2,1)}, bf16[64,3072]{1,0:T(8,128)(2,1)S(1)}, u32[]{:S(2)}) copy-start(bf16[64,3072]{1,0:T(8,128)(2,1)S(1)} %collective-permute-done.14.refs_2_) | copy-start | bytes 1179652
  120.6 20.1 %collective-permute-start.17 = (bf16[64,3072]{1,0:T(8,128)(2,1)}, bf16[64,3072]{1,0:T(8,128)(2,1)}, u32[]{:S(2)}, u32[]{:S(2)}) collective-permute-start(bf16[64,3072]{1,0:T(8,128)(2,1)} %get-tuple-element.13.refs_4_), channel_id=1, source_target_pairs={{0,2},{1,3},{2,0},{3,1},{4,6},{5,7},{6,4},{7,5},{8,10},{9,11},{10,... | collective-permute-start | bytes 1179656 | tf_op jit(solution)/shard_map/ppermute | solution.py:396
  121.1 0.8 copy-start.3
  121.1 20.7 %collective-permute-start.16 = (bf16[64,3072]{1,0:T(8,128)(2,1)}, bf16[64,3072]{1,0:T(8,128)(2,1)}, u32[]{:S(2)}, u32[]{:S(2)}) collective-permute-start(bf16[64,3072]{1,0:T(8,128)(2,1)} %get-tuple-element.13.refs_4_), channel_id=1, source_target_pairs={{0,1},{1,2},{2,3},{3,0},{4,5},{5,6},{6,7},{7,4},{8,9},{9,10},{10,1... | collective-permute-start | bytes 1179656 | tf_op jit(solution)/shard_map/ppermute | solution.py:396
  141.9 0.8 copy-start.6

commit v5 on v4

--- a/solution.py
+++ b/solution.py
@@ -113,9 +113,7 @@
     return hand + tiles * turn
 
 
-def gather_hand(at_ref, pruned_ref, sent_ref, low_ref, high_ref, piece_ref, got_ref, sem, *, height, width):
-    copy = pltpu.make_async_copy(sent_ref, got_ref, sem)
-    copy.start()
+def gather_hand(at_ref, pruned_ref, got_ref, low_ref, high_ref, piece_ref, *, height, width):
     pruned = pruned_ref[...]
     slots, half = got_ref.shape
     tiles = piece_ref.shape[0]
@@ -127,14 +125,15 @@
     hand = at_ref[1]
     turn = (before - hand + tiles - 1) // tiles + turn
     turn = jnp.where(hand + tiles * turn < after, turn, -1)
+    got = got_ref[...]
+    parts = [
+        across(one_hot(jnp.where(second == part, turn, -1), mine).astype(BF16), got, ((0,), (0,)))
+        for part in range(2)
+    ]
+    wide = lanes_for(height)
+    c = parts[1][:, half - 2 * wide : half - 2 * wide + height] + parts[1][:, half - wide : half - wide + height]
     cap = 2 * mine
     pick = one_hot(held(pruned, at_ref[0], height, in_turn(cap)), height)
-    deal = [one_hot(jnp.where(second == part, turn, -1), mine).astype(BF16) for part in range(2)]
-    copy.wait()
-    got = got_ref[...]
-    parts = [across(d, got, ((0,), (0,))) for d in deal]
-    wide = lanes_for(height)
-    c = parts[1][:, half - 2 * wide : half - 2 * wide + height] + parts[1][:, half - wide : half - wide + height]
     piece = across(pick, c, ((1,), (1,)), HIGH)
     for core in range(2):
         part = piece[:, mine // 2 * core : mine // 2 * (core + 1)]
@@ -148,18 +147,12 @@
 
 
 def join(*refs):
-    count = (len(refs) - 3) // 2
-    sems = refs[-1]
-    copies = []
+    count = (len(refs) - 2) // 2
     for path in range(2):
         out = refs[2 * count + path]
         rows = out.shape[0] // count
         for d in range(count):
-            i = count * path + d
-            copies.append(pltpu.make_async_copy(refs[i], out.at[rows * d : rows * d + rows, :], sems.at[i]))
-            copies[-1].start()
-    for copy in copies:
-        copy.wait()
+            out[rows * d : rows * d + rows, :] = refs[count * path + d][...]
 
 
 def pack_slab(pruned_ref, got_ref, out_ref, slab_ref, *, width):
@@ -384,9 +377,8 @@
             jax.ShapeDtypeStruct((mine // 2, length), BF16),
             jax.ShapeDtypeStruct((tiles, 8, cap // 8 * (mine // 2)), F32),
         ),
-        in_specs=[SMEM, VMEM, ANY],
+        in_specs=[SMEM, VMEM, VMEM],
         out_specs=(VMEM, VMEM, VMEM),
-        scratch_shapes=[pltpu.VMEM(hands.shape, BF16), pltpu.SemaphoreType.DMA(())],
         name="gather_hand",
     )(at, listed, hands)
     pieces = sent_to_all(pieces, "row")
@@ -412,9 +404,8 @@
     low, high = pl.pallas_call(
         join,
         out_shape=(jax.ShapeDtypeStruct((side * mine // 2, length), BF16),) * 2,
-        in_specs=[ANY] * (2 * side),
-        out_specs=(ANY, ANY),
-        scratch_shapes=[pltpu.SemaphoreType.DMA((2 * side,))],
+        in_specs=[VMEM] * (2 * side),
+        out_specs=(VMEM, VMEM),
         name="join",
     )(*lows, *highs)
     cols = [low] + [along_y(low, d) for d in range(1, side)]

time: 153 us -> 131 us (0.86)
  Pallas kernels: 65.5 us -> 42.2 us
    pallas_call x1, Pallas kernels: 25 us -> 2.14 us  [on_device(): pl.pallas_call(join, out_shape=(jax.ShapeDtypeStruct((side * mine // 2, l...]
    ppermute x7, waiting for transfers between devices: 3.82 us -> 20.1 us  [swapped(): return lax.ppermute(value, 'row', [(i, i ^ mask) for i in range(tiles)])]
    ppermute x6, waiting for transfers between devices: 15.5 us -> 0.02 us  [along_y(): lax.ppermute(value, 'col', [(c, (c + d * side) % tiles) for c in range(ti...]
  transfers between devices with their start and end apart: 21 -> 21, of which waited for: 4 -> 4; matrix products, arithmetic and copies ran while one was open for 1% -> 1% of each run, Pallas kernels for 30% -> 18%
where the time goes in v5:
time: 131 us; the launch traced here: 130 us
  Pallas kernels  42.2 us (32%)
  starting transfers between devices  34.9 us (27%)
  waiting for transfers between devices  29 us (22%)
  blocking collectives  18.2 us (14%)
  local copies, waits for them, and re-layouts  3.21 us (2%)
  other arithmetic  1.57 us (1%)
    ppermute x7, waiting for transfers between devices, swapped(): return lax.ppermute(value, 'row', [(i, i ^ mask) for i in range(tiles)])  20.1 us
    pallas_call x1, Pallas kernels, on_device(): pl.pallas_call(invert, out_shape=jax.ShapeDtypeStruct((n // BASE, n, BASE...  18.7 us
    all_to_all x1, blocking collectives, sent_to_all(): return lax.all_to_all(copies, axis, split_axis=0, concat_axis=0, tiled=True)  18.2 us
    all_to_all x2, starting transfers between devices, sent_to_all(): return lax.all_to_all(copies, axis, split_axis=0, concat_axis=0, tiled=True)  11.2 us
    pallas_call x1, Pallas kernels, on_device(): pl.pallas_call(update, out_shape=(jax.ShapeDtypeStruct(hessian_inverse.sh...  9.75 us
    all_to_all x2, waiting for transfers between devices, sent_to_all(): return lax.all_to_all(copies, axis, split_axis=0, concat_axis=0, tiled=True)  8.58 us
    ppermute x7, starting transfers between devices, swapped(): return lax.ppermute(value, 'row', [(i, i ^ mask) for i in range(tiles)])  8.26 us
    ppermute x6, starting transfers between devices, along_y(): lax.ppermute(value, 'col', [(c, (c + d * side) % tiles) for c in range(ti...  8.24 us
  transfers between devices with their start and end apart: 21, of which 4 were waited for; matrix products, arithmetic and copies ran while one was open for 1% of the time, Pallas kernels for 18%

profile of v5, /device:TPU:1, one launch (start us, length us, event | category | flops | bytes accessed | tf_op | source)
XLA Modules:
  0.0 130.0 jit_solution(14347297350679328692)
XLA Ops:
  0.6 4.4 %pack_cols.1 = bf16[128,1536]{1,0:T(8,128)(2,1)} custom-call(s32[1,512]{1,0:T(1,128)} %bitcast.19, f32[416,416]{1,0:T(8,128)} %refs_8_.1, bf16[416,2048]{1,0:T(8,128)(2,1)} %bitcast.11), custom_call_target="tpu_custom_call" | custom-call | tf_op jit(solution)/shard_map/pack_cols/pallas_call | solution.py:346
  5.0 7.6 %all-to-all-start = ((bf16[16,8,1536]{2,1,0:T(8,128)(2,1)}), bf16[16,8,1536]{2,1,0:T(8,128)(2,1)S(1)}, u32[]{:S(2)}, u32[]{:S(2)}) async-start(bf16[16,8,1536]{2,1,0:T(8,128)(2,1)} %bitcast.14), calls=%async_computation | async-start | bytes 786432 | tf_op jit(solution)/shard_map/all_to_all | solution.py:333
  12.6 0.6 pad_add_fusion.at_ref
  13.2 8.6 %all-to-all-done = bf16[16,8,1536]{2,1,0:T(8,128)(2,1)S(1)} async-done(((bf16[16,8,1536]{2,1,0:T(8,128)(2,1)}), bf16[16,8,1536]{2,1,0:T(8,128)(2,1)S(1)}, u32[]{:S(2)}, u32[]{:S(2)}) %all-to-all-start) | async-done | bytes 393248 | tf_op jit(solution)/shard_map/all_to_all | solution.py:333
  21.8 0.7 copy-done.2
  22.6 2.6 %gather_hand.1 = (bf16[16,3072]{1,0:T(8,128)(2,1)}, bf16[16,3072]{1,0:T(8,128)(2,1)}, f32[16,8,128]{2,1,0:T(8,128)}) custom-call(s32[2]{0:T(128)} %pad_add_fusion.at_ref, s32[1,512]{1,0:T(1,128)} %bitcast.20, bf16[128,1536]{1,0:T(8,128)(2,1)} %bitcast.13), custom_call_target="tpu_custom_call" | custom-call | tf_op jit(solution)/shard_map/gather_hand/pallas_call | solution.py:373
  25.1 18.2 %all_to_all.21.got_ref = f32[16,8,128]{2,1,0:T(8,128)} all-to-all(f32[16,8,128]{2,1,0:T(8,128)} %get-tuple-element.9), channel_id=1, replica_groups=mesh['row'=16,'col'=16] {'row'}, dimensions={0} | all-to-all | bytes 131072 | tf_op jit(solution)/shard_map/all_to_all | solution.py:333
  43.3 2.0 %pack_slab.1 = f32[16,16,512]{2,1,0:T(8,128)} custom-call(s32[1,512]{1,0:T(1,128)} %bitcast.21, f32[16,8,128]{2,1,0:T(8,128)} %all_to_all.21.got_ref), custom_call_target="tpu_custom_call" | custom-call | tf_op jit(solution)/shard_map/pack_slab/pallas_call | solution.py:395
  45.3 3.6 %all-to-all-start.2 = ((f32[16,16,512]{2,1,0:T(8,128)}), f32[16,16,512]{2,1,0:T(8,128)S(1)}, u32[]{:S(2)}, u32[]{:S(2)}) async-start(f32[16,16,512]{2,1,0:T(8,128)} %pack_slab.1), calls=%async_computation.2 | async-start | bytes 1048576 | tf_op jit(solution)/shard_map/all_to_all | solution.py:333
  48.9 2.6 %pack_rows.1 = f32[208,128]{1,0:T(8,128)} custom-call(s32[2]{0:T(128)} %pad_add_fusion.at_ref, s32[1,512]{1,0:T(1,128)} %bitcast.22, f32[416,416]{1,0:T(8,128)} %refs_8_.1), custom_call_target="tpu_custom_call" | custom-call | tf_op jit(solution)/shard_map/pack_rows/pallas_call | solution.py:360
  51.5 0.3 collective-permute-start.3
  51.8 1.1 collective-permute-start.2
  52.9 2.2 %collective-permute-start.1 = (f32[208,128]{1,0:T(8,128)}, f32[208,128]{1,0:T(8,128)S(1)}, u32[]{:S(2)}, u32[]{:S(2)}) collective-permute-start(f32[208,128]{1,0:T(8,128)} %pack_rows.1), channel_id=1, source_target_pairs={{0,32},{16,48},{32,0},{48,16},{64,96},{80,112},{96,64},{112,80},{1... | collective-permute-start | bytes 319496 | tf_op jit(solution)/shard_map/ppermute | solution.py:369
  55.1 2.5 %collective-permute-start.9 = (bf16[16,3072]{1,0:T(8,128)(2,1)}, bf16[16,3072]{1,0:T(8,128)(2,1)S(1)}, u32[]{:S(2)}, u32[]{:S(2)}) collective-permute-start(bf16[16,3072]{1,0:T(8,128)(2,1)} %get-tuple-element.10.refs_0_), channel_id=1, source_target_pairs={{0,3},{1,0},{2,1},{3,2},{4,7},{5,4},{6,5},{7,6},{8,11},{9,8},{10,9... | collective-permute-start | bytes 294920 | tf_op jit(solution)/shard_map/ppermute | solution.py:388
  57.5 0.6 collective-permute-start.8
  58.1 0.9 collective-permute-start.7
  58.9 3.8 %collective-permute-done.2 = f32[208,128]{1,0:T(8,128)S(1)} collective-permute-done((f32[208,128]{1,0:T(8,128)}, f32[208,128]{1,0:T(8,128)S(1)}, u32[]{:S(2)}, u32[]{:S(2)}) %collective-permute-start.2) | collective-permute-done | bytes 106528 | tf_op jit(solution)/shard_map/ppermute | solution.py:369
  62.7 2.3 %collective-permute-start.12 = (bf16[16,3072]{1,0:T(8,128)(2,1)}, bf16[16,3072]{1,0:T(8,128)(2,1)S(1)}, u32[]{:S(2)}, u32[]{:S(2)}) collective-permute-start(bf16[16,3072]{1,0:T(8,128)(2,1)} %get-tuple-element.11.refs_4_), channel_id=1, source_target_pairs={{0,12},{1,13},{2,14},{3,15},{4,0},{5,1},{6,2},{7,3},{8,4},{9,5},{1... | collective-permute-start | bytes 294920 | tf_op jit(solution)/shard_map/ppermute | solution.py:391
  65.0 0.5 collective-permute-start.11
  65.6 0.0 collective-permute-done.9.refs_3_
  65.6 0.6 collective-permute-start.10
  66.2 0.0 collective-permute-done.8.refs_2_
  66.2 0.0 all-to-all-done.2.own_ref
  66.2 0.0 copy-start
  66.2 2.3 %collective-permute-start = (f32[16,16,512]{2,1,0:T(8,128)S(1)}, f32[16,16,512]{2,1,0:T(8,128)S(1)}, u32[]{:S(2)}, u32[]{:S(2)}) collective-permute-start(f32[16,16,512]{2,1,0:T(8,128)S(1)} %all-to-all-done.2.own_ref), channel_id=1, source_target_pairs={{0,16},{16,0},{32,48},{48,32},{64,80},{80,64},{96,112},{112,96},{1... | collective-permute-start | bytes 1572872 | tf_op jit(solution)/shard_map/ppermute | solution.py:369
  68.5 0.9 pad_maximum_fusion.near_ref
  69.4 0.0 copy-start.11
  69.4 1.4 %collective-permute-start.4 = (f32[4,208,128]{2,1,0:T(8,128)S(1)}, f32[4,208,128]{2,1,0:T(8,128)S(1)}, u32[]{:S(2)}, u32[]{:S(2)}) collective-permute-start(f32[4,208,128]{2,1,0:T(8,128)S(1)} %pad_maximum_fusion.near_ref), channel_id=1, source_target_pairs={{0,128},{16,144},{32,160},{48,176},{64,192},{80,208},{96,224},{112... | collective-permute-start | bytes 1277960 | tf_op jit(solution)/shard_map/ppermute | solution.py:369
  70.9 0.4 collective-permute-start.5
  71.3 0.0 collective-permute-done.11.refs_6_
  71.3 0.0 collective-permute-done.10.refs_5_
  71.3 0.2 copy-done.12
  71.5 0.4 copy-done.13
  71.9 0.6 copy-done.14
  72.5 2.1 %join.1 = (bf16[64,3072]{1,0:T(8,128)(2,1)}, bf16[64,3072]{1,0:T(8,128)(2,1)}) custom-call(bf16[16,3072]{1,0:T(8,128)(2,1)} %get-tuple-element.10.refs_0_, bf16[16,3072]{1,0:T(8,128)(2,1)} %copy-done.11, bf16[16,3072]{1,0:T(8,128)(2,1)} %copy-done.10, bf16[16,3072]{1,0:T(8,128)(2,1)} %copy-done.9, bf16[16,3072]{1,0:T(8,128)(2,1)} %get-tuple-element.11.refs_4_, ...), custom_call_target="tpu_custom_call" | custom-call | tf_op jit(solution)/shard_map/join/pallas_call | solution.py:404
  74.7 2.8 %collective-permute-start.15 = (bf16[64,3072]{1,0:T(8,128)(2,1)}, bf16[64,3072]{1,0:T(8,128)(2,1)S(1)}, u32[]{:S(2)}, u32[]{:S(2)}) collective-permute-start(bf16[64,3072]{1,0:T(8,128)(2,1)} %get-tuple-element.12.refs_0_), channel_id=1, source_target_pairs={{0,12},{1,13},{2,14},{3,15},{4,0},{5,1},{6,2},{7,3},{8,4},{9,5},{1... | collective-permute-start | bytes 1179656 | tf_op jit(solution)/shard_map/ppermute | solution.py:391
  77.5 0.5 collective-permute-start.14
  78.0 16.3 %collective-permute-done.4.far_ref = f32[4,208,128]{2,1,0:T(8,128)S(1)} collective-permute-done((f32[4,208,128]{2,1,0:T(8,128)S(1)}, f32[4,208,128]{2,1,0:T(8,128)S(1)}, u32[]{:S(2)}, u32[]{:S(2)}) %collective-permute-start.4) | collective-permute-done | bytes 426016 | tf_op jit(solution)/shard_map/ppermute | solution.py:369
  94.3 0.6 collective-permute-start.6
  94.9 1.5 %collective-permute-start.13 = (bf16[64,3072]{1,0:T(8,128)(2,1)}, bf16[64,3072]{1,0:T(8,128)(2,1)}, u32[]{:S(2)}, u32[]{:S(2)}) collective-permute-start(bf16[64,3072]{1,0:T(8,128)(2,1)} %get-tuple-element.12.refs_0_), channel_id=1, source_target_pairs={{0,4},{1,5},{2,6},{3,7},{4,8},{5,9},{6,10},{7,11},{8,12},{9,13},{1... | collective-permute-start | bytes 1179656 | tf_op jit(solution)/shard_map/ppermute | solution.py:391
  96.4 1.5 %collective-permute-start.18 = (bf16[64,3072]{1,0:T(8,128)(2,1)}, bf16[64,3072]{1,0:T(8,128)(2,1)}, u32[]{:S(2)}, u32[]{:S(2)}) collective-permute-start(bf16[64,3072]{1,0:T(8,128)(2,1)} %get-tuple-element.13.refs_4_), channel_id=1, source_target_pairs={{0,3},{1,0},{2,1},{3,2},{4,7},{5,4},{6,5},{7,6},{8,11},{9,8},{10,9... | collective-permute-start | bytes 1179656 | tf_op jit(solution)/shard_map/ppermute | solution.py:388
  98.0 1.4 %collective-permute-start.17 = (bf16[64,3072]{1,0:T(8,128)(2,1)}, bf16[64,3072]{1,0:T(8,128)(2,1)}, u32[]{:S(2)}, u32[]{:S(2)}) collective-permute-start(bf16[64,3072]{1,0:T(8,128)(2,1)} %get-tuple-element.13.refs_4_), channel_id=1, source_target_pairs={{0,2},{1,3},{2,0},{3,1},{4,6},{5,7},{6,4},{7,5},{8,10},{9,11},{10,... | collective-permute-start | bytes 1179656 | tf_op jit(solution)/shard_map/ppermute | solution.py:388
  99.4 0.4 collective-permute-start.16
  99.8 0.4 copy-done.3
  100.2 18.7 %invert.1.inv_ref = f32[4,512,128]{2,1,0:T(8,128)} custom-call(s32[2]{0:T(128)} %pad_add_fusion.at_ref, f32[16,16,512]{2,1,0:T(8,128)} %copy-done, f32[16,16,512]{2,1,0:T(8,128)} %copy-done.3), custom_call_target="tpu_custom_call" | custom-call | tf_op jit(solution)/shard_map/invert/pallas_call | solution.py:416
  119.0 0.3 collective-permute-done.16.refs_5_
  119.3 0.8 copy-done.6
  120.1 9.8 %update.1 = (f32[416,416]{1,0:T(8,128)}, f32[416,2048]{1,0:T(8,128)}) custom-call(s32[2]{0:T(128)} %pad_add_fusion.at_ref, s32[1,512]{1,0:T(1,128)} %bitcast.23, f32[4,512,128]{2,1,0:T(8,128)} %invert.1.inv_ref, f32[4,208,128]{2,1,0:T(8,128)} %copy-done.1, f32[4,208,128]{2,1,0:T(8,128)} %copy-done.4, f32[4,208,128]{2,1,0:T(8,128)} %copy-done.5, ...), custom_call_target="tpu_custom_call" | custom-call | tf_op jit(solution)/shard_map/update/pallas_call | solution.py:425
  (34 shorter events, 0.1 us)
Async XLA Ops:
  5.0 16.8 %all-to-all-start = ((bf16[16,8,1536]{2,1,0:T(8,128)(2,1)}), bf16[16,8,1536]{2,1,0:T(8,128)(2,1)S(1)}, u32[]{:S(2)}, u32[]{:S(2)}) async-start(bf16[16,8,1536]{2,1,0:T(8,128)(2,1)} %bitcast.14), calls=%async_computation | async-start | bytes 786432 | tf_op jit(solution)/shard_map/all_to_all | solution.py:333
  21.8 0.7 copy-start.2
  45.3 20.9 %all-to-all-start.2 = ((f32[16,16,512]{2,1,0:T(8,128)}), f32[16,16,512]{2,1,0:T(8,128)S(1)}, u32[]{:S(2)}, u32[]{:S(2)}) async-start(f32[16,16,512]{2,1,0:T(8,128)} %pack_slab.1), calls=%async_computation.2 | async-start | bytes 1048576 | tf_op jit(solution)/shard_map/all_to_all | solution.py:333
  51.5 6.6 %collective-permute-start.3 = (f32[208,128]{1,0:T(8,128)}, f32[208,128]{1,0:T(8,128)S(1)}, u32[]{:S(2)}, u32[]{:S(2)}) collective-permute-start(f32[208,128]{1,0:T(8,128)} %pack_rows.1), channel_id=1, source_target_pairs={{0,96},{16,112},{32,64},{48,80},{64,32},{80,48},{96,0},{112,16},{1... | collective-permute-start | bytes 319496 | tf_op jit(solution)/shard_map/ppermute | solution.py:369
  51.8 10.9 %collective-permute-start.2 = (f32[208,128]{1,0:T(8,128)}, f32[208,128]{1,0:T(8,128)S(1)}, u32[]{:S(2)}, u32[]{:S(2)}) collective-permute-start(f32[208,128]{1,0:T(8,128)} %pack_rows.1), channel_id=1, source_target_pairs={{0,64},{16,80},{32,96},{48,112},{64,0},{80,16},{96,32},{112,48},{1... | collective-permute-start | bytes 319496 | tf_op jit(solution)/shard_map/ppermute | solution.py:369
  52.9 12.1 %collective-permute-start.1 = (f32[208,128]{1,0:T(8,128)}, f32[208,128]{1,0:T(8,128)S(1)}, u32[]{:S(2)}, u32[]{:S(2)}) collective-permute-start(f32[208,128]{1,0:T(8,128)} %pack_rows.1), channel_id=1, source_target_pairs={{0,32},{16,48},{32,0},{48,16},{64,96},{80,112},{96,64},{112,80},{1... | collective-permute-start | bytes 319496 | tf_op jit(solution)/shard_map/ppermute | solution.py:369
  55.1 10.5 %collective-permute-start.9 = (bf16[16,3072]{1,0:T(8,128)(2,1)}, bf16[16,3072]{1,0:T(8,128)(2,1)S(1)}, u32[]{:S(2)}, u32[]{:S(2)}) collective-permute-start(bf16[16,3072]{1,0:T(8,128)(2,1)} %get-tuple-element.10.refs_0_), channel_id=1, source_target_pairs={{0,3},{1,0},{2,1},{3,2},{4,7},{5,4},{6,5},{7,6},{8,11},{9,8},{10,9... | collective-permute-start | bytes 294920 | tf_op jit(solution)/shard_map/ppermute | solution.py:388
  57.5 8.6 %collective-permute-start.8 = (bf16[16,3072]{1,0:T(8,128)(2,1)}, bf16[16,3072]{1,0:T(8,128)(2,1)S(1)}, u32[]{:S(2)}, u32[]{:S(2)}) collective-permute-start(bf16[16,3072]{1,0:T(8,128)(2,1)} %get-tuple-element.10.refs_0_), channel_id=1, source_target_pairs={{0,2},{1,3},{2,0},{3,1},{4,6},{5,7},{6,4},{7,5},{8,10},{9,11},{10,... | collective-permute-start | bytes 294920 | tf_op jit(solution)/shard_map/ppermute | solution.py:388
  58.1 11.3 %collective-permute-start.7 = (bf16[16,3072]{1,0:T(8,128)(2,1)}, bf16[16,3072]{1,0:T(8,128)(2,1)S(1)}, u32[]{:S(2)}, u32[]{:S(2)}) collective-permute-start(bf16[16,3072]{1,0:T(8,128)(2,1)} %get-tuple-element.10.refs_0_), channel_id=1, source_target_pairs={{0,1},{1,2},{2,3},{3,0},{4,5},{5,6},{6,7},{7,4},{8,9},{9,10},{10,1... | collective-permute-start | bytes 294920 | tf_op jit(solution)/shard_map/ppermute | solution.py:388
  62.7 8.1 %collective-permute-start.12 = (bf16[16,3072]{1,0:T(8,128)(2,1)}, bf16[16,3072]{1,0:T(8,128)(2,1)S(1)}, u32[]{:S(2)}, u32[]{:S(2)}) collective-permute-start(bf16[16,3072]{1,0:T(8,128)(2,1)} %get-tuple-element.11.refs_4_), channel_id=1, source_target_pairs={{0,12},{1,13},{2,14},{3,15},{4,0},{5,1},{6,2},{7,3},{8,4},{9,5},{1... | collective-permute-start | bytes 294920 | tf_op jit(solution)/shard_map/ppermute | solution.py:391
  65.0 6.2 %collective-permute-start.11 = (bf16[16,3072]{1,0:T(8,128)(2,1)}, bf16[16,3072]{1,0:T(8,128)(2,1)S(1)}, u32[]{:S(2)}, u32[]{:S(2)}) collective-permute-start(bf16[16,3072]{1,0:T(8,128)(2,1)} %get-tuple-element.11.refs_4_), channel_id=1, source_target_pairs={{0,8},{1,9},{2,10},{3,11},{4,12},{5,13},{6,14},{7,15},{8,0},{9,1},... | collective-permute-start | bytes 294920 | tf_op jit(solution)/shard_map/ppermute | solution.py:391
  65.6 5.7 %copy-start.9 = (bf16[16,3072]{1,0:T(8,128)(2,1)}, bf16[16,3072]{1,0:T(8,128)(2,1)S(1)}, u32[]{:S(2)}) copy-start(bf16[16,3072]{1,0:T(8,128)(2,1)S(1)} %collective-permute-done.9.refs_3_) | copy-start | bytes 294916
  65.6 5.7 %collective-permute-start.10 = (bf16[16,3072]{1,0:T(8,128)(2,1)}, bf16[16,3072]{1,0:T(8,128)(2,1)S(1)}, u32[]{:S(2)}, u32[]{:S(2)}) collective-permute-start(bf16[16,3072]{1,0:T(8,128)(2,1)} %get-tuple-element.11.refs_4_), channel_id=1, source_target_pairs={{0,4},{1,5},{2,6},{3,7},{4,8},{5,9},{6,10},{7,11},{8,12},{9,13},{1... | collective-permute-start | bytes 294920 | tf_op jit(solution)/shard_map/ppermute | solution.py:391
  66.2 5.1 %copy-start.10 = (bf16[16,3072]{1,0:T(8,128)(2,1)}, bf16[16,3072]{1,0:T(8,128)(2,1)S(1)}, u32[]{:S(2)}) copy-start(bf16[16,3072]{1,0:T(8,128)(2,1)S(1)} %collective-permute-done.8.refs_2_) | copy-start | bytes 294916
  66.2 33.6 %copy-start = (f32[16,16,512]{2,1,0:T(8,128)}, f32[16,16,512]{2,1,0:T(8,128)S(1)}, u32[]{:S(2)}) copy-start(f32[16,16,512]{2,1,0:T(8,128)S(1)} %all-to-all-done.2.own_ref) | copy-start | bytes 1572868
  66.2 33.2 %collective-permute-start = (f32[16,16,512]{2,1,0:T(8,128)S(1)}, f32[16,16,512]{2,1,0:T(8,128)S(1)}, u32[]{:S(2)}, u32[]{:S(2)}) collective-permute-start(f32[16,16,512]{2,1,0:T(8,128)S(1)} %all-to-all-done.2.own_ref), channel_id=1, source_target_pairs={{0,16},{16,0},{32,48},{48,32},{64,80},{80,64},{96,112},{112,96},{1... | collective-permute-start | bytes 1572872 | tf_op jit(solution)/shard_map/ppermute | solution.py:369
  69.4 49.8 %copy-start.1 = (f32[4,208,128]{2,1,0:T(8,128)}, f32[4,208,128]{2,1,0:T(8,128)S(1)}, u32[]{:S(2)}) copy-start(f32[4,208,128]{2,1,0:T(8,128)S(1)} %pad_maximum_fusion.near_ref) | copy-start | bytes 1277956
  69.4 1.9 %copy-start.11 = (bf16[16,3072]{1,0:T(8,128)(2,1)}, bf16[16,3072]{1,0:T(8,128)(2,1)S(1)}, u32[]{:S(2)}) copy-start(bf16[16,3072]{1,0:T(8,128)(2,1)S(1)} %collective-permute-done.7.refs_1_) | copy-start | bytes 294916
  69.4 24.8 %collective-permute-start.4 = (f32[4,208,128]{2,1,0:T(8,128)S(1)}, f32[4,208,128]{2,1,0:T(8,128)S(1)}, u32[]{:S(2)}, u32[]{:S(2)}) collective-permute-start(f32[4,208,128]{2,1,0:T(8,128)S(1)} %pad_maximum_fusion.near_ref), channel_id=1, source_target_pairs={{0,128},{16,144},{32,160},{48,176},{64,192},{80,208},{96,224},{112... | collective-permute-start | bytes 1277960 | tf_op jit(solution)/shard_map/ppermute | solution.py:369
  70.9 0.6 copy-start.12
  70.9 24.0 %collective-permute-start.5 = (f32[4,208,128]{2,1,0:T(8,128)S(1)}, f32[4,208,128]{2,1,0:T(8,128)S(1)}, u32[]{:S(2)}, u32[]{:S(2)}) collective-permute-start(f32[4,208,128]{2,1,0:T(8,128)S(1)} %pad_maximum_fusion.near_ref), channel_id=1, source_target_pairs={{0,16},{16,0},{32,48},{48,32},{64,80},{80,64},{96,112},{112,96},{1... | collective-permute-start | bytes 1277960 | tf_op jit(solution)/shard_map/ppermute | solution.py:369
  71.3 0.6 copy-start.13
  71.9 0.6 copy-start.14
  74.7 21.7 %collective-permute-start.15 = (bf16[64,3072]{1,0:T(8,128)(2,1)}, bf16[64,3072]{1,0:T(8,128)(2,1)S(1)}, u32[]{:S(2)}, u32[]{:S(2)}) collective-permute-start(bf16[64,3072]{1,0:T(8,128)(2,1)} %get-tuple-element.12.refs_0_), channel_id=1, source_target_pairs={{0,12},{1,13},{2,14},{3,15},{4,0},{5,1},{6,2},{7,3},{8,4},{9,5},{1... | collective-permute-start | bytes 1179656 | tf_op jit(solution)/shard_map/ppermute | solution.py:391
  77.5 20.5 %collective-permute-start.14 = (bf16[64,3072]{1,0:T(8,128)(2,1)}, bf16[64,3072]{1,0:T(8,128)(2,1)S(1)}, u32[]{:S(2)}, u32[]{:S(2)}) collective-permute-start(bf16[64,3072]{1,0:T(8,128)(2,1)} %get-tuple-element.12.refs_0_), channel_id=1, source_target_pairs={{0,8},{1,9},{2,10},{3,11},{4,12},{5,13},{6,14},{7,15},{8,0},{9,1},... | collective-permute-start | bytes 1179656 | tf_op jit(solution)/shard_map/ppermute | solution.py:391
  94.3 25.0 %copy-start.4 = (f32[4,208,128]{2,1,0:T(8,128)}, f32[4,208,128]{2,1,0:T(8,128)S(1)}, u32[]{:S(2)}) copy-start(f32[4,208,128]{2,1,0:T(8,128)S(1)} %collective-permute-done.4.far_ref) | copy-start | bytes 1277956
  94.3 25.0 %collective-permute-start.6 = (f32[4,208,128]{2,1,0:T(8,128)S(1)}, f32[4,208,128]{2,1,0:T(8,128)S(1)}, u32[]{:S(2)}, u32[]{:S(2)}) collective-permute-start(f32[4,208,128]{2,1,0:T(8,128)S(1)} %collective-permute-done.4.far_ref), channel_id=1, source_target_pairs={{0,16},{16,0},{32,48},{48,32},{64,80},{80,64},{96,112},{112,96},{1... | collective-permute-start | bytes 1277960 | tf_op jit(solution)/shard_map/ppermute | solution.py:369
  94.9 24.4 %copy-start.5 = (f32[4,208,128]{2,1,0:T(8,128)}, f32[4,208,128]{2,1,0:T(8,128)S(1)}, u32[]{:S(2)}) copy-start(f32[4,208,128]{2,1,0:T(8,128)S(1)} %collective-permute-done.5.twin_near_ref) | copy-start | bytes 1277956
  94.9 24.0 %collective-permute-start.13 = (bf16[64,3072]{1,0:T(8,128)(2,1)}, bf16[64,3072]{1,0:T(8,128)(2,1)}, u32[]{:S(2)}, u32[]{:S(2)}) collective-permute-start(bf16[64,3072]{1,0:T(8,128)(2,1)} %get-tuple-element.12.refs_0_), channel_id=1, source_target_pairs={{0,4},{1,5},{2,6},{3,7},{4,8},{5,9},{6,10},{7,11},{8,12},{9,13},{1... | collective-permute-start | bytes 1179656 | tf_op jit(solution)/shard_map/ppermute | solution.py:391
  96.4 22.9 %copy-start.7 = (bf16[64,3072]{1,0:T(8,128)(2,1)}, bf16[64,3072]{1,0:T(8,128)(2,1)S(1)}, u32[]{:S(2)}) copy-start(bf16[64,3072]{1,0:T(8,128)(2,1)S(1)} %collective-permute-done.15.refs_3_) | copy-start | bytes 1179652
  96.4 22.5 %collective-permute-start.18 = (bf16[64,3072]{1,0:T(8,128)(2,1)}, bf16[64,3072]{1,0:T(8,128)(2,1)}, u32[]{:S(2)}, u32[]{:S(2)}) collective-permute-start(bf16[64,3072]{1,0:T(8,128)(2,1)} %get-tuple-element.13.refs_4_), channel_id=1, source_target_pairs={{0,3},{1,0},{2,1},{3,2},{4,7},{5,4},{6,5},{7,6},{8,11},{9,8},{10,9... | collective-permute-start | bytes 1179656 | tf_op jit(solution)/shard_map/ppermute | solution.py:388
  98.0 21.3 %copy-start.8 = (bf16[64,3072]{1,0:T(8,128)(2,1)}, bf16[64,3072]{1,0:T(8,128)(2,1)S(1)}, u32[]{:S(2)}) copy-start(bf16[64,3072]{1,0:T(8,128)(2,1)S(1)} %collective-permute-done.14.refs_2_) | copy-start | bytes 1179652
  98.0 21.0 %collective-permute-start.17 = (bf16[64,3072]{1,0:T(8,128)(2,1)}, bf16[64,3072]{1,0:T(8,128)(2,1)}, u32[]{:S(2)}, u32[]{:S(2)}) collective-permute-start(bf16[64,3072]{1,0:T(8,128)(2,1)} %get-tuple-element.13.refs_4_), channel_id=1, source_target_pairs={{0,2},{1,3},{2,0},{3,1},{4,6},{5,7},{6,4},{7,5},{8,10},{9,11},{10,... | collective-permute-start | bytes 1179656 | tf_op jit(solution)/shard_map/ppermute | solution.py:388
  99.4 0.8 copy-start.3
  99.4 19.8 %collective-permute-start.16 = (bf16[64,3072]{1,0:T(8,128)(2,1)}, bf16[64,3072]{1,0:T(8,128)(2,1)}, u32[]{:S(2)}, u32[]{:S(2)}) collective-permute-start(bf16[64,3072]{1,0:T(8,128)(2,1)} %get-tuple-element.13.refs_4_), channel_id=1, source_target_pairs={{0,1},{1,2},{2,3},{3,0},{4,5},{5,6},{6,7},{7,4},{8,9},{9,10},{10,1... | collective-permute-start | bytes 1179656 | tf_op jit(solution)/shard_map/ppermute | solution.py:388
  119.3 0.8 copy-start.6

commit v6 on v5

--- a/solution.py
+++ b/solution.py
@@ -16,6 +16,7 @@
 SMEM = pl.BlockSpec(memory_space=pltpu.SMEM)
 ANY = pl.BlockSpec(memory_space=pl.ANY)
 BASE = 128
+GRANT = 24 << 20
 BLOCK = 256
 
 
@@ -81,30 +82,21 @@
         ref[full, pl.ds(start + each * i, each), 0:rest] = last[:, rest * i : rest * i + rest]
 
 
-def pack_cols(pruned_ref, h_hbm, w_hbm, out_ref, h_ref, w_ref, sems):
+def pack_cols(pruned_ref, h_ref, w_ref, out_ref):
+    pruned = pruned_ref[...]
     slots, half = out_ref.shape
-    copies = [
-        pltpu.make_async_copy(h_hbm, h_ref, sems.at[0]),
-        pltpu.make_async_copy(w_hbm.at[:, half:], w_ref.at[:, half:], sems.at[1]),
-        pltpu.make_async_copy(w_hbm.at[:, :half], w_ref.at[:, :half], sems.at[2]),
-    ]
-    for copy in copies:
-        copy.start()
-    pruned = pruned_ref[...]
     width = h_ref.shape[1]
     tiles = slots // 8
     pick = one_hot(held(pruned, lax.axis_index("col"), width, lambda before: dealt_places(before, tiles, 4)), width)
+    w = w_ref[...]
     picked = pick.astype(BF16)
-    copies[0].wait()
+    first = across(picked, w[:, :half], ((1,), (0,)))
+    last = across(picked, w[:, half:], ((1,), (0,)))
     c = across(pick, h_ref[...], ((1,), (1,)), HIGH)
     c_high = c.astype(BF16).astype(F32)
-    copies[1].wait()
-    last = across(picked, w_ref[:, half:], ((1,), (0,)))
     spare = jnp.zeros((slots, lanes_for(width) - width), F32)
     last = jnp.concatenate([last, c_high, spare, c - c_high, spare], axis=1)
     second = lax.broadcasted_iota(jnp.int32, (slots, 1), 0) // 4 % 2
-    copies[2].wait()
-    first = across(picked, w_ref[:, :half], ((1,), (0,)))
     out_ref[...] = jnp.where(second == 1, last, first).astype(BF16)
 
 
@@ -346,14 +338,10 @@
     hands = pl.pallas_call(
         pack_cols,
         out_shape=jax.ShapeDtypeStruct((8 * tiles, length // 2), BF16),
-        in_specs=[VMEM, ANY, ANY],
+        in_specs=[VMEM, VMEM, VMEM],
         out_specs=VMEM,
-        scratch_shapes=[
-            pltpu.VMEM(hessian_inverse.shape, F32),
-            pltpu.VMEM(weights.shape, BF16),
-            pltpu.SemaphoreType.DMA((3,)),
-        ],
         name="pack_cols",
+        compiler_params=pltpu.CompilerParams(vmem_limit_bytes=GRANT),
     )(listed, hessian_inverse, weights)
     hands = sent_to_all(hands, "col")
     mine = n // tiles
@@ -363,6 +351,7 @@
         in_specs=[SMEM, VMEM, VMEM],
         out_specs=VMEM,
         name="pack_rows",
+        compiler_params=pltpu.CompilerParams(vmem_limit_bytes=GRANT),
     )(at, listed, hessian_inverse)
 
     def swapped(value, mask):
@@ -380,6 +369,7 @@
         in_specs=[SMEM, VMEM, VMEM],
         out_specs=(VMEM, VMEM, VMEM),
         name="gather_hand",
+        compiler_params=pltpu.CompilerParams(vmem_limit_bytes=GRANT),
     )(at, listed, hands)
     pieces = sent_to_all(pieces, "row")
     side = math.isqrt(tiles)
@@ -399,6 +389,7 @@
         out_specs=VMEM,
         scratch_shapes=[pltpu.VMEM((n + cap, 128), F32)],
         name="pack_slab",
+        compiler_params=pltpu.CompilerParams(vmem_limit_bytes=GRANT),
     )(listed, pieces)
     slab = sent_to_all(slab, "col")
     low, high = pl.pallas_call(
@@ -407,6 +398,7 @@
         in_specs=[VMEM] * (2 * side),
         out_specs=(VMEM, VMEM),
         name="join",
+        compiler_params=pltpu.CompilerParams(vmem_limit_bytes=GRANT),
     )(*lows, *highs)
     cols = [low] + [along_y(low, d) for d in range(1, side)]
     cols += [high] + [along_x(high, d) for d in range(1, side)]
@@ -420,6 +412,7 @@
         out_specs=VMEM,
         scratch_shapes=[pltpu.VMEM((8, BASE), F32)],
         name="invert",
+        compiler_params=pltpu.CompilerParams(vmem_limit_bytes=GRANT),
     )(at, slab, slab_twin)
     twin_far = swapped(far_rows, 1)
     h_new, w_new = pl.pallas_call(
@@ -437,6 +430,7 @@
             pltpu.SemaphoreType.DMA((rows_w // BLOCK + 1,)),
         ],
         name="update",
+        compiler_params=pltpu.CompilerParams(vmem_limit_bytes=GRANT),
     )(
         at, listed, inverse, near_rows, far_rows, twin_near, twin_far, *cols, hessian_inverse, weights
     )

time: 131 us -> 125 us (0.954)
  Pallas kernels: 42.2 us -> 30.3 us
  waiting for transfers between devices: 29 us -> 32.7 us
  local copies, waits for them, and re-layouts: 3.21 us -> 6.87 us
    unnamed x30 -> x32, local copies, waits for them, and re-layouts: 3.21 us -> 6.87 us
    pallas_call x1, Pallas kernels: 9.75 us -> 6.77 us  [on_device(): pl.pallas_call(update, out_shape=(jax.ShapeDtypeStruct(hessian_inverse.sh...]
    pallas_call x1, Pallas kernels: 4.36 us -> 2.19 us  [on_device(): pl.pallas_call(pack_cols, out_shape=jax.ShapeDtypeStruct((8 * tiles, leng...]
    ppermute x6, waiting for transfers between devices: 0.31 us -> 1.98 us  [along_x(): lax.ppermute(value, 'col', [(c, c // side * side + (c + d) % side) for c...]
    pallas_call x1, Pallas kernels: 2.02 us -> 0.36 us  [on_device(): pl.pallas_call(functools.partial(pack_slab, width=tile_rows), out_shape=j...]
    pallas_call x1, Pallas kernels: 18.7 us -> 17.1 us  [on_device(): pl.pallas_call(invert, out_shape=jax.ShapeDtypeStruct((n // BASE, n, BASE...]
    ppermute x7, waiting for transfers between devices: 20.1 us -> 21.6 us  [swapped(): return lax.ppermute(value, 'row', [(i, i ^ mask) for i in range(tiles)])]
  transfers between devices with their start and end apart: 21 -> 21, of which waited for: 4 -> 4; matrix products, arithmetic and copies ran while one was open for 1% -> 1% of each run, Pallas kernels for 18% -> 16%
where the time goes in v6:
time: 125 us
  starting transfers between devices  34.6 us (28%)
  waiting for transfers between devices  32.7 us (26%)
  Pallas kernels  30.3 us (24%)
  blocking collectives  18 us (14%)
  local copies, waits for them, and re-layouts  6.87 us (5%)
    ppermute x7, waiting for transfers between devices, swapped(): return lax.ppermute(value, 'row', [(i, i ^ mask) for i in range(tiles)])  21.6 us
    all_to_all x1, blocking collectives, sent_to_all(): return lax.all_to_all(copies, axis, split_axis=0, concat_axis=0, tiled=True)  18 us
    pallas_call x1, Pallas kernels, on_device(): pl.pallas_call(invert, out_shape=jax.ShapeDtypeStruct((n // BASE, n, BASE...  17.1 us
    all_to_all x2, starting transfers between devices, sent_to_all(): return lax.all_to_all(copies, axis, split_axis=0, concat_axis=0, tiled=True)  11.1 us
    all_to_all x2, waiting for transfers between devices, sent_to_all(): return lax.all_to_all(copies, axis, split_axis=0, concat_axis=0, tiled=True)  9.15 us
    ppermute x6, starting transfers between devices, along_y(): lax.ppermute(value, 'col', [(c, (c + d * side) % tiles) for c in range(ti...  8.32 us
    ppermute x7, starting transfers between devices, swapped(): return lax.ppermute(value, 'row', [(i, i ^ mask) for i in range(tiles)])  8.08 us
    ppermute x6, starting transfers between devices, along_x(): lax.ppermute(value, 'col', [(c, c // side * side + (c + d) % side) for c...  7.04 us
  transfers between devices with their start and end apart: 21, of which 4 were waited for; matrix products, arithmetic and copies ran while one was open for 1% of the time, Pallas kernels for 16%

profile of v6, /device:TPU:1, one launch (start us, length us, event | category | flops | bytes accessed | tf_op | source)
XLA Modules:
  0.0 124.6 jit_solution(186772567698578920)
XLA Ops:
  0.6 1.2 copy-done
  1.8 1.5 %copy-done.2 = bf16[2048,416]{0,1:T(8,128)(2,1)S(1)} copy-done((bf16[2048,416]{0,1:T(8,128)(2,1)S(1)}, bf16[2048,416]{0,1:T(8,128)(2,1)}, u32[]{:S(2)}) %copy-start.2) | copy-done | bytes 1703960
  3.3 0.7 copy-done.11
  3.9 2.2 %pack_cols.1 = bf16[128,1536]{1,0:T(8,128)(2,1)} custom-call(s32[1,512]{1,0:T(1,128)S(1)} %bitcast.15, f32[416,416]{1,0:T(8,128)S(1)} %copy-done, bf16[416,2048]{1,0:T(8,128)(2,1)S(1)} %bitcast.11), custom_call_target="tpu_custom_call" | custom-call | tf_op jit(solution)/shard_map/pack_cols/pallas_call | solution.py:338
  6.1 7.6 %all-to-all-start = ((bf16[16,8,1536]{2,1,0:T(8,128)(2,1)}), bf16[16,8,1536]{2,1,0:T(8,128)(2,1)S(1)}, u32[]{:S(2)}, u32[]{:S(2)}) async-start(bf16[16,8,1536]{2,1,0:T(8,128)(2,1)} %bitcast.4), calls=%async_computation | async-start | bytes 786432 | tf_op jit(solution)/shard_map/all_to_all | solution.py:325
  13.7 0.1 pad_add_fusion.at_ref
  13.8 9.1 %all-to-all-done = bf16[16,8,1536]{2,1,0:T(8,128)(2,1)S(1)} async-done(((bf16[16,8,1536]{2,1,0:T(8,128)(2,1)}), bf16[16,8,1536]{2,1,0:T(8,128)(2,1)S(1)}, u32[]{:S(2)}, u32[]{:S(2)}) %all-to-all-start) | async-done | bytes 393248 | tf_op jit(solution)/shard_map/all_to_all | solution.py:325
  22.9 1.5 %gather_hand.1 = (bf16[16,3072]{1,0:T(8,128)(2,1)S(1)}, bf16[16,3072]{1,0:T(8,128)(2,1)S(1)}, f32[16,8,128]{2,1,0:T(8,128)S(1)}) custom-call(s32[2]{0:T(128)S(1)} %pad_add_fusion.at_ref, s32[1,512]{1,0:T(1,128)S(1)} %bitcast.16, bf16[128,1536]{1,0:T(8,128)(2,1)S(1)} %bitcast.13), custom_call_target="tpu_custom_call" | custom-call | tf_op jit(solution)/shard_map/gather_hand/pallas_call | solution.py:362
  24.4 0.6 copy-done.5
  25.0 0.6 copy-done.7
  25.7 18.0 %all_to_all.21.got_ref = f32[16,8,128]{2,1,0:T(8,128)S(1)} all-to-all(f32[16,8,128]{2,1,0:T(8,128)S(1)} %get-tuple-element.9), channel_id=1, replica_groups=mesh['row'=16,'col'=16] {'row'}, dimensions={0} | all-to-all | bytes 131072 | tf_op jit(solution)/shard_map/all_to_all | solution.py:325
  43.6 0.4 pack_slab.1
  44.0 0.0 copy-start.4
  44.0 0.8 copy-done.4
  44.8 3.6 %all-to-all-start.2 = ((f32[16,16,512]{2,1,0:T(8,128)}), f32[16,16,512]{2,1,0:T(8,128)S(1)}, u32[]{:S(2)}, u32[]{:S(2)}) async-start(f32[16,16,512]{2,1,0:T(8,128)} %copy-done.4), calls=%async_computation.2 | async-start | bytes 1048576 | tf_op jit(solution)/shard_map/all_to_all | solution.py:325
  48.4 1.3 %pack_rows.1 = f32[208,128]{1,0:T(8,128)S(1)} custom-call(s32[2]{0:T(128)S(1)} %pad_add_fusion.at_ref, s32[1,512]{1,0:T(1,128)S(1)} %bitcast.18, f32[416,416]{1,0:T(8,128)S(1)} %copy-done.1), custom_call_target="tpu_custom_call" | custom-call | tf_op jit(solution)/shard_map/pack_rows/pallas_call | solution.py:348
  49.7 0.4 collective-permute-start.3
  50.1 1.1 collective-permute-start.2
  51.2 2.2 %collective-permute-start.1 = (f32[208,128]{1,0:T(8,128)S(1)}, f32[208,128]{1,0:T(8,128)S(1)}, u32[]{:S(2)}, u32[]{:S(2)}) collective-permute-start(f32[208,128]{1,0:T(8,128)S(1)} %pack_rows.1), channel_id=1, source_target_pairs={{0,32},{16,48},{32,0},{48,16},{64,96},{80,112},{96,64},{112,80},{1... | collective-permute-start | bytes 319496 | tf_op jit(solution)/shard_map/ppermute | solution.py:358
  53.3 2.5 %collective-permute-start.9 = (bf16[16,3072]{1,0:T(8,128)(2,1)}, bf16[16,3072]{1,0:T(8,128)(2,1)S(1)}, u32[]{:S(2)}, u32[]{:S(2)}) collective-permute-start(bf16[16,3072]{1,0:T(8,128)(2,1)} %copy-done.5), channel_id=1, source_target_pairs={{0,3},{1,0},{2,1},{3,2},{4,7},{5,4},{6,5},{7,6},{8,11},{9,8},{10,9... | collective-permute-start | bytes 294920 | tf_op jit(solution)/shard_map/ppermute | solution.py:378
  55.8 0.6 collective-permute-start.8
  56.3 0.0 collective-permute-done.3
  56.4 0.6 collective-permute-start.7
  57.0 3.8 %collective-permute-done.2 = f32[208,128]{1,0:T(8,128)S(1)} collective-permute-done((f32[208,128]{1,0:T(8,128)S(1)}, f32[208,128]{1,0:T(8,128)S(1)}, u32[]{:S(2)}, u32[]{:S(2)}) %collective-permute-start.2) | collective-permute-done | bytes 106528 | tf_op jit(solution)/shard_map/ppermute | solution.py:358
  60.8 2.3 %collective-permute-start.12 = (bf16[16,3072]{1,0:T(8,128)(2,1)}, bf16[16,3072]{1,0:T(8,128)(2,1)}, u32[]{:S(2)}, u32[]{:S(2)}) collective-permute-start(bf16[16,3072]{1,0:T(8,128)(2,1)} %copy-done.7), channel_id=1, source_target_pairs={{0,12},{1,13},{2,14},{3,15},{4,0},{5,1},{6,2},{7,3},{8,4},{9,5},{1... | collective-permute-start | bytes 294920 | tf_op jit(solution)/shard_map/ppermute | solution.py:381
  63.1 0.5 collective-permute-start.11
  63.6 0.6 collective-permute-start.10
  64.2 0.0 collective-permute-done.8.refs_2_
  64.2 0.6 copy-done.9
  64.9 0.0 all-to-all-done.2.own_ref
  64.9 2.2 %collective-permute-start = (f32[16,16,512]{2,1,0:T(8,128)S(1)}, f32[16,16,512]{2,1,0:T(8,128)S(1)}, u32[]{:S(2)}, u32[]{:S(2)}) collective-permute-start(f32[16,16,512]{2,1,0:T(8,128)S(1)} %all-to-all-done.2.own_ref), channel_id=1, source_target_pairs={{0,16},{16,0},{32,48},{48,32},{64,80},{80,64},{96,112},{112,96},{1... | collective-permute-start | bytes 1572872 | tf_op jit(solution)/shard_map/ppermute | solution.py:358
  67.1 1.0 pad_maximum_fusion.near_ref
  68.1 0.0 collective-permute-done.7.refs_1_
  68.1 1.4 %collective-permute-start.4 = (f32[4,208,128]{2,1,0:T(8,128)S(1)}, f32[4,208,128]{2,1,0:T(8,128)S(1)}, u32[]{:S(2)}, u32[]{:S(2)}) collective-permute-start(f32[4,208,128]{2,1,0:T(8,128)S(1)} %pad_maximum_fusion.near_ref), channel_id=1, source_target_pairs={{0,128},{16,144},{32,160},{48,176},{64,192},{80,208},{96,224},{112... | collective-permute-start | bytes 1277960 | tf_op jit(solution)/shard_map/ppermute | solution.py:358
  69.5 0.3 collective-permute-start.5
  69.8 0.9 copy-done.10
  70.7 1.1 join.1
  71.8 2.5 %collective-permute-start.15 = (bf16[64,3072]{1,0:T(8,128)(2,1)S(1)}, bf16[64,3072]{1,0:T(8,128)(2,1)S(1)}, u32[]{:S(2)}, u32[]{:S(2)}) collective-permute-start(bf16[64,3072]{1,0:T(8,128)(2,1)S(1)} %get-tuple-element.12.refs_0_), channel_id=1, source_target_pairs={{0,12},{1,13},{2,14},{3,15},{4,0},{5,1},{6,2},{7,3},{8,4},{9,5},{1... | collective-permute-start | bytes 1179656 | tf_op jit(solution)/shard_map/ppermute | solution.py:381
  74.3 0.9 collective-permute-start.14
  75.2 17.8 %collective-permute-done.4.far_ref = f32[4,208,128]{2,1,0:T(8,128)S(1)} collective-permute-done((f32[4,208,128]{2,1,0:T(8,128)S(1)}, f32[4,208,128]{2,1,0:T(8,128)S(1)}, u32[]{:S(2)}, u32[]{:S(2)}) %collective-permute-start.4) | collective-permute-done | bytes 426016 | tf_op jit(solution)/shard_map/ppermute | solution.py:358
  93.0 0.6 collective-permute-start.6
  93.6 1.5 %collective-permute-start.13 = (bf16[64,3072]{1,0:T(8,128)(2,1)S(1)}, bf16[64,3072]{1,0:T(8,128)(2,1)S(1)}, u32[]{:S(2)}, u32[]{:S(2)}) collective-permute-start(bf16[64,3072]{1,0:T(8,128)(2,1)S(1)} %get-tuple-element.12.refs_0_), channel_id=1, source_target_pairs={{0,4},{1,5},{2,6},{3,7},{4,8},{5,9},{6,10},{7,11},{8,12},{9,13},{1... | collective-permute-start | bytes 1179656 | tf_op jit(solution)/shard_map/ppermute | solution.py:381
  95.1 1.5 %collective-permute-start.18 = (bf16[64,3072]{1,0:T(8,128)(2,1)S(1)}, bf16[64,3072]{1,0:T(8,128)(2,1)S(1)}, u32[]{:S(2)}, u32[]{:S(2)}) collective-permute-start(bf16[64,3072]{1,0:T(8,128)(2,1)S(1)} %get-tuple-element.13.refs_4_), channel_id=1, source_target_pairs={{0,3},{1,0},{2,1},{3,2},{4,7},{5,4},{6,5},{7,6},{8,11},{9,8},{10,9... | collective-permute-start | bytes 1179656 | tf_op jit(solution)/shard_map/ppermute | solution.py:378
  96.6 1.4 %collective-permute-start.17 = (bf16[64,3072]{1,0:T(8,128)(2,1)S(1)}, bf16[64,3072]{1,0:T(8,128)(2,1)S(1)}, u32[]{:S(2)}, u32[]{:S(2)}) collective-permute-start(bf16[64,3072]{1,0:T(8,128)(2,1)S(1)} %get-tuple-element.13.refs_4_), channel_id=1, source_target_pairs={{0,2},{1,3},{2,0},{3,1},{4,6},{5,7},{6,4},{7,5},{8,10},{9,11},{10,... | collective-permute-start | bytes 1179656 | tf_op jit(solution)/shard_map/ppermute | solution.py:378
  98.1 0.4 collective-permute-start.16
  98.5 17.1 %invert.1.inv_ref = f32[4,512,128]{2,1,0:T(8,128)S(1)} custom-call(s32[2]{0:T(128)S(1)} %pad_add_fusion.at_ref, f32[16,16,512]{2,1,0:T(8,128)S(1)} %all-to-all-done.2.own_ref, f32[16,16,512]{2,1,0:T(8,128)S(1)} %collective-permute-done.other_ref), custom_call_target="tpu_custom_call" | custom-call | tf_op jit(solution)/shard_map/invert/pallas_call | solution.py:408
  115.6 2.0 %collective-permute-done.16.refs_5_ = bf16[64,3072]{1,0:T(8,128)(2,1)S(1)} collective-permute-done((bf16[64,3072]{1,0:T(8,128)(2,1)S(1)}, bf16[64,3072]{1,0:T(8,128)(2,1)S(1)}, u32[]{:S(2)}, u32[]{:S(2)}) %collective-permute-start.16) | collective-permute-done | bytes 393248 | tf_op jit(solution)/shard_map/ppermute | solution.py:378
  117.6 6.8 %update.1 = (f32[416,416]{1,0:T(8,128)}, f32[416,2048]{1,0:T(8,128)}) custom-call(s32[2]{0:T(128)S(1)} %pad_add_fusion.at_ref, s32[1,512]{1,0:T(1,128)S(1)} %bitcast.19, f32[4,512,128]{2,1,0:T(8,128)S(1)} %invert.1.inv_ref, f32[4,208,128]{2,1,0:T(8,128)S(1)} %pad_maximum_fusion.near_ref, f32[4,208,128]{2,1,0:T(8,128)S(1)} %collective-permute-done.4.far_ref, ...), custom_call_target="tpu_custom_call" | custom-call | tf_op jit(solution)/shard_map/update/pallas_call | solution.py:418
  (36 shorter events, 0.1 us)
Async XLA Ops:
  0.6 43.0 %copy-start.12 = (s32[512]{0:T(512)S(1)}, s32[512]{0:T(512)}, u32[]{:S(2)}) copy-start(s32[512]{0:T(512)} %param.5) | copy-start | bytes 6148
  0.6 1.2 copy-start
  1.8 1.5 %copy-start.2 = (bf16[2048,416]{0,1:T(8,128)(2,1)S(1)}, bf16[2048,416]{0,1:T(8,128)(2,1)}, u32[]{:S(2)}) copy-start(bf16[2048,416]{0,1:T(8,128)(2,1)} %param.4) | copy-start | bytes 5111812
  3.3 0.7 copy-start.11
  3.9 44.5 %copy-start.1 = (f32[416,416]{1,0:T(8,128)S(1)}, f32[416,416]{1,0:T(8,128)}, u32[]{:S(2)}) copy-start(f32[416,416]{1,0:T(8,128)} %refs_8_.1) | copy-start | bytes 2076676
  6.1 16.8 %all-to-all-start = ((bf16[16,8,1536]{2,1,0:T(8,128)(2,1)}), bf16[16,8,1536]{2,1,0:T(8,128)(2,1)S(1)}, u32[]{:S(2)}, u32[]{:S(2)}) async-start(bf16[16,8,1536]{2,1,0:T(8,128)(2,1)} %bitcast.4), calls=%async_computation | async-start | bytes 786432 | tf_op jit(solution)/shard_map/all_to_all | solution.py:325
  22.9 94.7 %copy-start.3 = (bf16[2048,416]{0,1:T(8,128)(2,1)S(1)}, bf16[2048,416]{0,1:T(8,128)(2,1)}, u32[]{:S(2)}) copy-start(bf16[2048,416]{0,1:T(8,128)(2,1)} %param.4) | copy-start | bytes 5111812
  24.4 0.6 copy-start.5
  25.0 0.6 copy-start.7
  25.7 44.2 %copy-start.6 = (bf16[16,3072]{1,0:T(8,128)(2,1)S(1)}, bf16[16,3072]{1,0:T(8,128)(2,1)}, u32[]{:S(2)}) copy-start(bf16[16,3072]{1,0:T(8,128)(2,1)} %copy-done.5) | copy-start | bytes 294916
  25.7 44.2 %copy-start.8 = (bf16[16,3072]{1,0:T(8,128)(2,1)S(1)}, bf16[16,3072]{1,0:T(8,128)(2,1)}, u32[]{:S(2)}) copy-start(bf16[16,3072]{1,0:T(8,128)(2,1)} %copy-done.7) | copy-start | bytes 294916
  44.0 0.8 copy-start.4
  44.8 20.0 %all-to-all-start.2 = ((f32[16,16,512]{2,1,0:T(8,128)}), f32[16,16,512]{2,1,0:T(8,128)S(1)}, u32[]{:S(2)}, u32[]{:S(2)}) async-start(f32[16,16,512]{2,1,0:T(8,128)} %copy-done.4), calls=%async_computation.2 | async-start | bytes 1048576 | tf_op jit(solution)/shard_map/all_to_all | solution.py:325
  49.7 6.6 %collective-permute-start.3 = (f32[208,128]{1,0:T(8,128)S(1)}, f32[208,128]{1,0:T(8,128)S(1)}, u32[]{:S(2)}, u32[]{:S(2)}) collective-permute-start(f32[208,128]{1,0:T(8,128)S(1)} %pack_rows.1), channel_id=1, source_target_pairs={{0,96},{16,112},{32,64},{48,80},{64,32},{80,48},{96,0},{112,16},{1... | collective-permute-start | bytes 319496 | tf_op jit(solution)/shard_map/ppermute | solution.py:358
  50.1 10.7 %collective-permute-start.2 = (f32[208,128]{1,0:T(8,128)S(1)}, f32[208,128]{1,0:T(8,128)S(1)}, u32[]{:S(2)}, u32[]{:S(2)}) collective-permute-start(f32[208,128]{1,0:T(8,128)S(1)} %pack_rows.1), channel_id=1, source_target_pairs={{0,64},{16,80},{32,96},{48,112},{64,0},{80,16},{96,32},{112,48},{1... | collective-permute-start | bytes 319496 | tf_op jit(solution)/shard_map/ppermute | solution.py:358
  51.2 11.9 %collective-permute-start.1 = (f32[208,128]{1,0:T(8,128)S(1)}, f32[208,128]{1,0:T(8,128)S(1)}, u32[]{:S(2)}, u32[]{:S(2)}) collective-permute-start(f32[208,128]{1,0:T(8,128)S(1)} %pack_rows.1), channel_id=1, source_target_pairs={{0,32},{16,48},{32,0},{48,16},{64,96},{80,112},{96,64},{112,80},{1... | collective-permute-start | bytes 319496 | tf_op jit(solution)/shard_map/ppermute | solution.py:358
  53.3 10.3 %collective-permute-start.9 = (bf16[16,3072]{1,0:T(8,128)(2,1)}, bf16[16,3072]{1,0:T(8,128)(2,1)S(1)}, u32[]{:S(2)}, u32[]{:S(2)}) collective-permute-start(bf16[16,3072]{1,0:T(8,128)(2,1)} %copy-done.5), channel_id=1, source_target_pairs={{0,3},{1,0},{2,1},{3,2},{4,7},{5,4},{6,5},{7,6},{8,11},{9,8},{10,9... | collective-permute-start | bytes 294920 | tf_op jit(solution)/shard_map/ppermute | solution.py:378
  55.8 8.4 %collective-permute-start.8 = (bf16[16,3072]{1,0:T(8,128)(2,1)}, bf16[16,3072]{1,0:T(8,128)(2,1)S(1)}, u32[]{:S(2)}, u32[]{:S(2)}) collective-permute-start(bf16[16,3072]{1,0:T(8,128)(2,1)} %copy-done.5), channel_id=1, source_target_pairs={{0,2},{1,3},{2,0},{3,1},{4,6},{5,7},{6,4},{7,5},{8,10},{9,11},{10,... | collective-permute-start | bytes 294920 | tf_op jit(solution)/shard_map/ppermute | solution.py:378
  56.3 7.9 %copy-start.13 = (f32[208,128]{1,0:T(8,128)}, f32[208,128]{1,0:T(8,128)S(1)}, u32[]{:S(2)}) copy-start(f32[208,128]{1,0:T(8,128)S(1)} %collective-permute-done.3) | copy-start | bytes 319492
  56.4 11.8 %collective-permute-start.7 = (bf16[16,3072]{1,0:T(8,128)(2,1)}, bf16[16,3072]{1,0:T(8,128)(2,1)}, u32[]{:S(2)}, u32[]{:S(2)}) collective-permute-start(bf16[16,3072]{1,0:T(8,128)(2,1)} %copy-done.5), channel_id=1, source_target_pairs={{0,1},{1,2},{2,3},{3,0},{4,5},{5,6},{6,7},{7,4},{8,9},{9,10},{10,1... | collective-permute-start | bytes 294920 | tf_op jit(solution)/shard_map/ppermute | solution.py:378
  60.8 3.4 %copy-start.14 = (f32[208,128]{1,0:T(8,128)}, f32[208,128]{1,0:T(8,128)S(1)}, u32[]{:S(2)}) copy-start(f32[208,128]{1,0:T(8,128)S(1)} %collective-permute-done.2) | copy-start | bytes 319492
  60.8 8.7 %collective-permute-start.12 = (bf16[16,3072]{1,0:T(8,128)(2,1)}, bf16[16,3072]{1,0:T(8,128)(2,1)}, u32[]{:S(2)}, u32[]{:S(2)}) collective-permute-start(bf16[16,3072]{1,0:T(8,128)(2,1)} %copy-done.7), channel_id=1, source_target_pairs={{0,12},{1,13},{2,14},{3,15},{4,0},{5,1},{6,2},{7,3},{8,4},{9,5},{1... | collective-permute-start | bytes 294920 | tf_op jit(solution)/shard_map/ppermute | solution.py:381
  63.1 1.1 copy-start.15
  63.1 6.7 %collective-permute-start.11 = (bf16[16,3072]{1,0:T(8,128)(2,1)}, bf16[16,3072]{1,0:T(8,128)(2,1)}, u32[]{:S(2)}, u32[]{:S(2)}) collective-permute-start(bf16[16,3072]{1,0:T(8,128)(2,1)} %copy-done.7), channel_id=1, source_target_pairs={{0,8},{1,9},{2,10},{3,11},{4,12},{5,13},{6,14},{7,15},{8,0},{9,1},... | collective-permute-start | bytes 294920 | tf_op jit(solution)/shard_map/ppermute | solution.py:381
  63.6 6.2 %collective-permute-start.10 = (bf16[16,3072]{1,0:T(8,128)(2,1)}, bf16[16,3072]{1,0:T(8,128)(2,1)}, u32[]{:S(2)}, u32[]{:S(2)}) collective-permute-start(bf16[16,3072]{1,0:T(8,128)(2,1)} %copy-done.7), channel_id=1, source_target_pairs={{0,4},{1,5},{2,6},{3,7},{4,8},{5,9},{6,10},{7,11},{8,12},{9,13},{1... | collective-permute-start | bytes 294920 | tf_op jit(solution)/shard_map/ppermute | solution.py:381
  64.2 0.6 copy-start.9
  64.9 33.2 %collective-permute-start = (f32[16,16,512]{2,1,0:T(8,128)S(1)}, f32[16,16,512]{2,1,0:T(8,128)S(1)}, u32[]{:S(2)}, u32[]{:S(2)}) collective-permute-start(f32[16,16,512]{2,1,0:T(8,128)S(1)} %all-to-all-done.2.own_ref), channel_id=1, source_target_pairs={{0,16},{16,0},{32,48},{48,32},{64,80},{80,64},{96,112},{112,96},{1... | collective-permute-start | bytes 1572872 | tf_op jit(solution)/shard_map/ppermute | solution.py:358
  68.1 24.9 %collective-permute-start.4 = (f32[4,208,128]{2,1,0:T(8,128)S(1)}, f32[4,208,128]{2,1,0:T(8,128)S(1)}, u32[]{:S(2)}, u32[]{:S(2)}) collective-permute-start(f32[4,208,128]{2,1,0:T(8,128)S(1)} %pad_maximum_fusion.near_ref), channel_id=1, source_target_pairs={{0,128},{16,144},{32,160},{48,176},{64,192},{80,208},{96,224},{112... | collective-permute-start | bytes 1277960 | tf_op jit(solution)/shard_map/ppermute | solution.py:358
  69.5 24.0 %collective-permute-start.5 = (f32[4,208,128]{2,1,0:T(8,128)S(1)}, f32[4,208,128]{2,1,0:T(8,128)S(1)}, u32[]{:S(2)}, u32[]{:S(2)}) collective-permute-start(f32[4,208,128]{2,1,0:T(8,128)S(1)} %pad_maximum_fusion.near_ref), channel_id=1, source_target_pairs={{0,16},{16,0},{32,48},{48,32},{64,80},{80,64},{96,112},{112,96},{1... | collective-permute-start | bytes 1277960 | tf_op jit(solution)/shard_map/ppermute | solution.py:358
  69.8 0.9 copy-start.10
  71.8 23.3 %collective-permute-start.15 = (bf16[64,3072]{1,0:T(8,128)(2,1)S(1)}, bf16[64,3072]{1,0:T(8,128)(2,1)S(1)}, u32[]{:S(2)}, u32[]{:S(2)}) collective-permute-start(bf16[64,3072]{1,0:T(8,128)(2,1)S(1)} %get-tuple-element.12.refs_0_), channel_id=1, source_target_pairs={{0,12},{1,13},{2,14},{3,15},{4,0},{5,1},{6,2},{7,3},{8,4},{9,5},{1... | collective-permute-start | bytes 1179656 | tf_op jit(solution)/shard_map/ppermute | solution.py:381
  74.3 22.3 %collective-permute-start.14 = (bf16[64,3072]{1,0:T(8,128)(2,1)S(1)}, bf16[64,3072]{1,0:T(8,128)(2,1)S(1)}, u32[]{:S(2)}, u32[]{:S(2)}) collective-permute-start(bf16[64,3072]{1,0:T(8,128)(2,1)S(1)} %get-tuple-element.12.refs_0_), channel_id=1, source_target_pairs={{0,8},{1,9},{2,10},{3,11},{4,12},{5,13},{6,14},{7,15},{8,0},{9,1},... | collective-permute-start | bytes 1179656 | tf_op jit(solution)/shard_map/ppermute | solution.py:381
  93.0 24.6 %collective-permute-start.6 = (f32[4,208,128]{2,1,0:T(8,128)S(1)}, f32[4,208,128]{2,1,0:T(8,128)S(1)}, u32[]{:S(2)}, u32[]{:S(2)}) collective-permute-start(f32[4,208,128]{2,1,0:T(8,128)S(1)} %collective-permute-done.4.far_ref), channel_id=1, source_target_pairs={{0,16},{16,0},{32,48},{48,32},{64,80},{80,64},{96,112},{112,96},{1... | collective-permute-start | bytes 1277960 | tf_op jit(solution)/shard_map/ppermute | solution.py:358
  93.6 22.0 %collective-permute-start.13 = (bf16[64,3072]{1,0:T(8,128)(2,1)S(1)}, bf16[64,3072]{1,0:T(8,128)(2,1)S(1)}, u32[]{:S(2)}, u32[]{:S(2)}) collective-permute-start(bf16[64,3072]{1,0:T(8,128)(2,1)S(1)} %get-tuple-element.12.refs_0_), channel_id=1, source_target_pairs={{0,4},{1,5},{2,6},{3,7},{4,8},{5,9},{6,10},{7,11},{8,12},{9,13},{1... | collective-permute-start | bytes 1179656 | tf_op jit(solution)/shard_map/ppermute | solution.py:381
  95.1 20.5 %collective-permute-start.18 = (bf16[64,3072]{1,0:T(8,128)(2,1)S(1)}, bf16[64,3072]{1,0:T(8,128)(2,1)S(1)}, u32[]{:S(2)}, u32[]{:S(2)}) collective-permute-start(bf16[64,3072]{1,0:T(8,128)(2,1)S(1)} %get-tuple-element.13.refs_4_), channel_id=1, source_target_pairs={{0,3},{1,0},{2,1},{3,2},{4,7},{5,4},{6,5},{7,6},{8,11},{9,8},{10,9... | collective-permute-start | bytes 1179656 | tf_op jit(solution)/shard_map/ppermute | solution.py:378
  96.6 19.0 %collective-permute-start.17 = (bf16[64,3072]{1,0:T(8,128)(2,1)S(1)}, bf16[64,3072]{1,0:T(8,128)(2,1)S(1)}, u32[]{:S(2)}, u32[]{:S(2)}) collective-permute-start(bf16[64,3072]{1,0:T(8,128)(2,1)S(1)} %get-tuple-element.13.refs_4_), channel_id=1, source_target_pairs={{0,2},{1,3},{2,0},{3,1},{4,6},{5,7},{6,4},{7,5},{8,10},{9,11},{10,... | collective-permute-start | bytes 1179656 | tf_op jit(solution)/shard_map/ppermute | solution.py:378
  98.1 19.5 %collective-permute-start.16 = (bf16[64,3072]{1,0:T(8,128)(2,1)S(1)}, bf16[64,3072]{1,0:T(8,128)(2,1)S(1)}, u32[]{:S(2)}, u32[]{:S(2)}) collective-permute-start(bf16[64,3072]{1,0:T(8,128)(2,1)S(1)} %get-tuple-element.13.refs_4_), channel_id=1, source_target_pairs={{0,1},{1,2},{2,3},{3,0},{4,5},{5,6},{6,7},{7,4},{8,9},{9,10},{10,1... | collective-permute-start | bytes 1179656 | tf_op jit(solution)/shard_map/ppermute | solution.py:378

commit v7 on v5

--- a/solution.py
+++ b/solution.py
@@ -16,6 +16,7 @@
 SMEM = pl.BlockSpec(memory_space=pltpu.SMEM)
 ANY = pl.BlockSpec(memory_space=pl.ANY)
 BASE = 128
+GRANT = 24 << 20
 BLOCK = 256
 
 
@@ -363,6 +364,7 @@
         in_specs=[SMEM, VMEM, VMEM],
         out_specs=VMEM,
         name="pack_rows",
+        compiler_params=pltpu.CompilerParams(vmem_limit_bytes=GRANT),
     )(at, listed, hessian_inverse)
 
     def swapped(value, mask):
@@ -380,6 +382,7 @@
         in_specs=[SMEM, VMEM, VMEM],
         out_specs=(VMEM, VMEM, VMEM),
         name="gather_hand",
+        compiler_params=pltpu.CompilerParams(vmem_limit_bytes=GRANT),
     )(at, listed, hands)
     pieces = sent_to_all(pieces, "row")
     side = math.isqrt(tiles)
@@ -399,6 +402,7 @@
         out_specs=VMEM,
         scratch_shapes=[pltpu.VMEM((n + cap, 128), F32)],
         name="pack_slab",
+        compiler_params=pltpu.CompilerParams(vmem_limit_bytes=GRANT),
     )(listed, pieces)
     slab = sent_to_all(slab, "col")
     low, high = pl.pallas_call(
@@ -407,6 +411,7 @@
         in_specs=[VMEM] * (2 * side),
         out_specs=(VMEM, VMEM),
         name="join",
+        compiler_params=pltpu.CompilerParams(vmem_limit_bytes=GRANT),
     )(*lows, *highs)
     cols = [low] + [along_y(low, d) for d in range(1, side)]
     cols += [high] + [along_x(high, d) for d in range(1, side)]
@@ -420,6 +425,7 @@
         out_specs=VMEM,
         scratch_shapes=[pltpu.VMEM((8, BASE), F32)],
         name="invert",
+        compiler_params=pltpu.CompilerParams(vmem_limit_bytes=GRANT),
     )(at, slab, slab_twin)
     twin_far = swapped(far_rows, 1)
     h_new, w_new = pl.pallas_call(
@@ -437,6 +443,7 @@
             pltpu.SemaphoreType.DMA((rows_w // BLOCK + 1,)),
         ],
         name="update",
+        compiler_params=pltpu.CompilerParams(vmem_limit_bytes=GRANT),
     )(
         at, listed, inverse, near_rows, far_rows, twin_near, twin_far, *cols, hessian_inverse, weights
     )

time: 131 us -> 124 us (0.947)
  Pallas kernels: 42.2 us -> 32.6 us
  waiting for transfers between devices: 29 us -> 32.6 us
    pallas_call x1, Pallas kernels: 9.75 us -> 6.78 us  [on_device(): pl.pallas_call(update, out_shape=(jax.ShapeDtypeStruct(hessian_inverse.sh...]
    ppermute x6, waiting for transfers between devices: 0.31 us -> 2 us  [along_x(): lax.ppermute(value, 'col', [(c, c // side * side + (c + d) % side) for c...]
    pallas_call x1, Pallas kernels: 2.02 us -> 0.36 us  [on_device(): pl.pallas_call(functools.partial(pack_slab, width=tile_rows), out_shape=j...]
    pallas_call x1, Pallas kernels: 18.7 us -> 17.1 us  [on_device(): pl.pallas_call(invert, out_shape=jax.ShapeDtypeStruct((n // BASE, n, BASE...]
    unnamed x30 -> x26, local copies, waits for them, and re-layouts: 3.21 us -> 3.62 us
  transfers between devices with their start and end apart: 21 -> 21, of which waited for: 4 -> 4; matrix products, arithmetic and copies ran while one was open for 1% -> 1% of each run, Pallas kernels for 18% -> 16%
where the time goes in v7:
time: 124 us
  starting transfers between devices  34.8 us (28%)
  Pallas kernels  32.6 us (26%)
  waiting for transfers between devices  32.6 us (26%)
  blocking collectives  18 us (15%)
  local copies, waits for them, and re-layouts  3.62 us (3%)
    ppermute x7, waiting for transfers between devices, swapped(): return lax.ppermute(value, 'row', [(i, i ^ mask) for i in range(tiles)])  21.4 us
    all_to_all x1, blocking collectives, sent_to_all(): return lax.all_to_all(copies, axis, split_axis=0, concat_axis=0, tiled=True)  18 us
    pallas_call x1, Pallas kernels, on_device(): pl.pallas_call(invert, out_shape=jax.ShapeDtypeStruct((n // BASE, n, BASE...  17.1 us
    all_to_all x2, starting transfers between devices, sent_to_all(): return lax.all_to_all(copies, axis, split_axis=0, concat_axis=0, tiled=True)  11.2 us
    all_to_all x2, waiting for transfers between devices, sent_to_all(): return lax.all_to_all(copies, axis, split_axis=0, concat_axis=0, tiled=True)  9.15 us
    ppermute x6, starting transfers between devices, along_y(): lax.ppermute(value, 'col', [(c, (c + d * side) % tiles) for c in range(ti...  8.51 us
    ppermute x7, starting transfers between devices, swapped(): return lax.ppermute(value, 'row', [(i, i ^ mask) for i in range(tiles)])  8.08 us
    ppermute x6, starting transfers between devices, along_x(): lax.ppermute(value, 'col', [(c, c // side * side + (c + d) % side) for c...  7.01 us
  transfers between devices with their start and end apart: 21, of which 4 were waited for; matrix products, arithmetic and copies ran while one was open for 1% of the time, Pallas kernels for 16%

profile of v7, /device:TPU:1, one launch (start us, length us, event | category | flops | bytes accessed | tf_op | source)
XLA Modules:
  0.0 123.6 jit_solution(1962984349330092862)
XLA Ops:
  0.6 4.4 %pack_cols.1 = bf16[128,1536]{1,0:T(8,128)(2,1)} custom-call(s32[1,512]{1,0:T(1,128)} %bitcast.15, f32[416,416]{1,0:T(8,128)} %refs_8_.1, bf16[416,2048]{1,0:T(8,128)(2,1)} %bitcast.11), custom_call_target="tpu_custom_call" | custom-call | tf_op jit(solution)/shard_map/pack_cols/pallas_call | solution.py:347
  5.1 7.6 %all-to-all-start = ((bf16[16,8,1536]{2,1,0:T(8,128)(2,1)}), bf16[16,8,1536]{2,1,0:T(8,128)(2,1)S(1)}, u32[]{:S(2)}, u32[]{:S(2)}) async-start(bf16[16,8,1536]{2,1,0:T(8,128)(2,1)} %bitcast.20), calls=%async_computation | async-start | bytes 786432 | tf_op jit(solution)/shard_map/all_to_all | solution.py:334
  12.7 0.1 pad_add_fusion.at_ref
  12.8 9.1 %all-to-all-done = bf16[16,8,1536]{2,1,0:T(8,128)(2,1)S(1)} async-done(((bf16[16,8,1536]{2,1,0:T(8,128)(2,1)}), bf16[16,8,1536]{2,1,0:T(8,128)(2,1)S(1)}, u32[]{:S(2)}, u32[]{:S(2)}) %all-to-all-start) | async-done | bytes 393248 | tf_op jit(solution)/shard_map/all_to_all | solution.py:334
  21.9 1.5 %gather_hand.1 = (bf16[16,3072]{1,0:T(8,128)(2,1)S(1)}, bf16[16,3072]{1,0:T(8,128)(2,1)S(1)}, f32[16,8,128]{2,1,0:T(8,128)S(1)}) custom-call(s32[2]{0:T(128)S(1)} %pad_add_fusion.at_ref, s32[1,512]{1,0:T(1,128)S(1)} %bitcast.16, bf16[128,1536]{1,0:T(8,128)(2,1)S(1)} %bitcast.13), custom_call_target="tpu_custom_call" | custom-call | tf_op jit(solution)/shard_map/gather_hand/pallas_call | solution.py:375
  23.4 0.6 copy-done.3
  24.0 0.6 copy-done.5
  24.7 18.0 %all_to_all.21.got_ref = f32[16,8,128]{2,1,0:T(8,128)S(1)} all-to-all(f32[16,8,128]{2,1,0:T(8,128)S(1)} %get-tuple-element.9), channel_id=1, replica_groups=mesh['row'=16,'col'=16] {'row'}, dimensions={0} | all-to-all | bytes 131072 | tf_op jit(solution)/shard_map/all_to_all | solution.py:334
  42.6 0.4 pack_slab.1
  43.0 0.0 copy-start.2
  43.0 0.8 copy-done.2
  43.8 3.6 %all-to-all-start.2 = ((f32[16,16,512]{2,1,0:T(8,128)}), f32[16,16,512]{2,1,0:T(8,128)S(1)}, u32[]{:S(2)}, u32[]{:S(2)}) async-start(f32[16,16,512]{2,1,0:T(8,128)} %copy-done.2), calls=%async_computation.2 | async-start | bytes 1048576 | tf_op jit(solution)/shard_map/all_to_all | solution.py:334
  47.4 1.3 %pack_rows.1 = f32[208,128]{1,0:T(8,128)S(1)} custom-call(s32[2]{0:T(128)S(1)} %pad_add_fusion.at_ref, s32[1,512]{1,0:T(1,128)S(1)} %bitcast.18, f32[416,416]{1,0:T(8,128)S(1)} %copy-done), custom_call_target="tpu_custom_call" | custom-call | tf_op jit(solution)/shard_map/pack_rows/pallas_call | solution.py:361
  48.7 0.4 collective-permute-start.3
  49.1 1.1 collective-permute-start.2
  50.2 2.2 %collective-permute-start.1 = (f32[208,128]{1,0:T(8,128)S(1)}, f32[208,128]{1,0:T(8,128)S(1)}, u32[]{:S(2)}, u32[]{:S(2)}) collective-permute-start(f32[208,128]{1,0:T(8,128)S(1)} %pack_rows.1), channel_id=1, source_target_pairs={{0,32},{16,48},{32,0},{48,16},{64,96},{80,112},{96,64},{112,80},{1... | collective-permute-start | bytes 319496 | tf_op jit(solution)/shard_map/ppermute | solution.py:371
  52.3 2.5 %collective-permute-start.9 = (bf16[16,3072]{1,0:T(8,128)(2,1)}, bf16[16,3072]{1,0:T(8,128)(2,1)S(1)}, u32[]{:S(2)}, u32[]{:S(2)}) collective-permute-start(bf16[16,3072]{1,0:T(8,128)(2,1)} %copy-done.3), channel_id=1, source_target_pairs={{0,3},{1,0},{2,1},{3,2},{4,7},{5,4},{6,5},{7,6},{8,11},{9,8},{10,9... | collective-permute-start | bytes 294920 | tf_op jit(solution)/shard_map/ppermute | solution.py:391
  54.8 0.6 collective-permute-start.8
  55.4 0.6 collective-permute-start.7
  56.0 3.8 %collective-permute-done.2 = f32[208,128]{1,0:T(8,128)S(1)} collective-permute-done((f32[208,128]{1,0:T(8,128)S(1)}, f32[208,128]{1,0:T(8,128)S(1)}, u32[]{:S(2)}, u32[]{:S(2)}) %collective-permute-start.2) | collective-permute-done | bytes 106528 | tf_op jit(solution)/shard_map/ppermute | solution.py:371
  59.8 2.3 %collective-permute-start.12 = (bf16[16,3072]{1,0:T(8,128)(2,1)}, bf16[16,3072]{1,0:T(8,128)(2,1)}, u32[]{:S(2)}, u32[]{:S(2)}) collective-permute-start(bf16[16,3072]{1,0:T(8,128)(2,1)} %copy-done.5), channel_id=1, source_target_pairs={{0,12},{1,13},{2,14},{3,15},{4,0},{5,1},{6,2},{7,3},{8,4},{9,5},{1... | collective-permute-start | bytes 294920 | tf_op jit(solution)/shard_map/ppermute | solution.py:394
  62.1 0.0 collective-permute-done.1
  62.1 0.5 collective-permute-start.11
  62.6 0.0 collective-permute-done.9.refs_3_
  62.6 0.6 collective-permute-start.10
  63.2 0.0 collective-permute-done.8.refs_2_
  63.3 0.6 copy-done.7
  63.9 2.2 %collective-permute-start = (f32[16,16,512]{2,1,0:T(8,128)S(1)}, f32[16,16,512]{2,1,0:T(8,128)S(1)}, u32[]{:S(2)}, u32[]{:S(2)}) collective-permute-start(f32[16,16,512]{2,1,0:T(8,128)S(1)} %all-to-all-done.2.own_ref), channel_id=1, source_target_pairs={{0,16},{16,0},{32,48},{48,32},{64,80},{80,64},{96,112},{112,96},{1... | collective-permute-start | bytes 1572872 | tf_op jit(solution)/shard_map/ppermute | solution.py:371
  66.1 1.0 pad_maximum_fusion.near_ref
  67.1 0.0 collective-permute-done.7.refs_1_
  67.1 1.4 %collective-permute-start.4 = (f32[4,208,128]{2,1,0:T(8,128)S(1)}, f32[4,208,128]{2,1,0:T(8,128)S(1)}, u32[]{:S(2)}, u32[]{:S(2)}) collective-permute-start(f32[4,208,128]{2,1,0:T(8,128)S(1)} %pad_maximum_fusion.near_ref), channel_id=1, source_target_pairs={{0,128},{16,144},{32,160},{48,176},{64,192},{80,208},{96,224},{112... | collective-permute-start | bytes 1277960 | tf_op jit(solution)/shard_map/ppermute | solution.py:371
  68.6 0.3 collective-permute-start.5
  68.8 0.0 collective-permute-done.11.refs_6_
  68.8 0.0 collective-permute-done.10.refs_5_
  68.9 0.9 copy-done.8
  69.8 1.1 join.1
  70.8 2.6 %collective-permute-start.15 = (bf16[64,3072]{1,0:T(8,128)(2,1)S(1)}, bf16[64,3072]{1,0:T(8,128)(2,1)S(1)}, u32[]{:S(2)}, u32[]{:S(2)}) collective-permute-start(bf16[64,3072]{1,0:T(8,128)(2,1)S(1)} %get-tuple-element.12.refs_0_), channel_id=1, source_target_pairs={{0,12},{1,13},{2,14},{3,15},{4,0},{5,1},{6,2},{7,3},{8,4},{9,5},{1... | collective-permute-start | bytes 1179656 | tf_op jit(solution)/shard_map/ppermute | solution.py:394
  73.5 0.9 collective-permute-start.14
  74.4 17.6 %collective-permute-done.4.far_ref = f32[4,208,128]{2,1,0:T(8,128)S(1)} collective-permute-done((f32[4,208,128]{2,1,0:T(8,128)S(1)}, f32[4,208,128]{2,1,0:T(8,128)S(1)}, u32[]{:S(2)}, u32[]{:S(2)}) %collective-permute-start.4) | collective-permute-done | bytes 426016 | tf_op jit(solution)/shard_map/ppermute | solution.py:371
  92.0 0.6 collective-permute-start.6
  92.6 1.5 %collective-permute-start.13 = (bf16[64,3072]{1,0:T(8,128)(2,1)S(1)}, bf16[64,3072]{1,0:T(8,128)(2,1)S(1)}, u32[]{:S(2)}, u32[]{:S(2)}) collective-permute-start(bf16[64,3072]{1,0:T(8,128)(2,1)S(1)} %get-tuple-element.12.refs_0_), channel_id=1, source_target_pairs={{0,4},{1,5},{2,6},{3,7},{4,8},{5,9},{6,10},{7,11},{8,12},{9,13},{1... | collective-permute-start | bytes 1179656 | tf_op jit(solution)/shard_map/ppermute | solution.py:394
  94.1 1.5 %collective-permute-start.18 = (bf16[64,3072]{1,0:T(8,128)(2,1)S(1)}, bf16[64,3072]{1,0:T(8,128)(2,1)S(1)}, u32[]{:S(2)}, u32[]{:S(2)}) collective-permute-start(bf16[64,3072]{1,0:T(8,128)(2,1)S(1)} %get-tuple-element.13.refs_4_), channel_id=1, source_target_pairs={{0,3},{1,0},{2,1},{3,2},{4,7},{5,4},{6,5},{7,6},{8,11},{9,8},{10,9... | collective-permute-start | bytes 1179656 | tf_op jit(solution)/shard_map/ppermute | solution.py:391
  95.7 0.0 collective-permute-done.14.refs_2_
  95.7 1.4 %collective-permute-start.17 = (bf16[64,3072]{1,0:T(8,128)(2,1)S(1)}, bf16[64,3072]{1,0:T(8,128)(2,1)S(1)}, u32[]{:S(2)}, u32[]{:S(2)}) collective-permute-start(bf16[64,3072]{1,0:T(8,128)(2,1)S(1)} %get-tuple-element.13.refs_4_), channel_id=1, source_target_pairs={{0,2},{1,3},{2,0},{3,1},{4,6},{5,7},{6,4},{7,5},{8,10},{9,11},{10,... | collective-permute-start | bytes 1179656 | tf_op jit(solution)/shard_map/ppermute | solution.py:391
  97.1 0.4 collective-permute-start.16
  97.5 17.1 %invert.1.inv_ref = f32[4,512,128]{2,1,0:T(8,128)S(1)} custom-call(s32[2]{0:T(128)S(1)} %pad_add_fusion.at_ref, f32[16,16,512]{2,1,0:T(8,128)S(1)} %all-to-all-done.2.own_ref, f32[16,16,512]{2,1,0:T(8,128)S(1)} %collective-permute-done.other_ref), custom_call_target="tpu_custom_call" | custom-call | tf_op jit(solution)/shard_map/invert/pallas_call | solution.py:421
  114.6 2.0 %collective-permute-done.16.refs_5_ = bf16[64,3072]{1,0:T(8,128)(2,1)S(1)} collective-permute-done((bf16[64,3072]{1,0:T(8,128)(2,1)S(1)}, bf16[64,3072]{1,0:T(8,128)(2,1)S(1)}, u32[]{:S(2)}, u32[]{:S(2)}) %collective-permute-start.16) | collective-permute-done | bytes 393248 | tf_op jit(solution)/shard_map/ppermute | solution.py:391
  116.6 6.8 %update.1 = (f32[416,416]{1,0:T(8,128)}, f32[416,2048]{1,0:T(8,128)}) custom-call(s32[2]{0:T(128)S(1)} %pad_add_fusion.at_ref, s32[1,512]{1,0:T(1,128)S(1)} %bitcast.19, f32[4,512,128]{2,1,0:T(8,128)S(1)} %invert.1.inv_ref, f32[4,208,128]{2,1,0:T(8,128)S(1)} %pad_maximum_fusion.near_ref, f32[4,208,128]{2,1,0:T(8,128)S(1)} %collective-permute-done.4.far_ref, ...), custom_call_target="tpu_custom_call" | custom-call | tf_op jit(solution)/shard_map/update/pallas_call | solution.py:431
  (30 shorter events, 0.1 us)
Async XLA Ops:
  0.6 46.8 %copy-start = (f32[416,416]{1,0:T(8,128)S(1)}, f32[416,416]{1,0:T(8,128)}, u32[]{:S(2)}) copy-start(f32[416,416]{1,0:T(8,128)} %refs_8_.1) | copy-start | bytes 2076676
  0.6 21.3 %copy-start.9 = (s32[512]{0:T(512)S(1)}, s32[512]{0:T(512)}, u32[]{:S(2)}) copy-start(s32[512]{0:T(512)} %param.5) | copy-start | bytes 6148
  5.1 16.8 %all-to-all-start = ((bf16[16,8,1536]{2,1,0:T(8,128)(2,1)}), bf16[16,8,1536]{2,1,0:T(8,128)(2,1)S(1)}, u32[]{:S(2)}, u32[]{:S(2)}) async-start(bf16[16,8,1536]{2,1,0:T(8,128)(2,1)} %bitcast.20), calls=%async_computation | async-start | bytes 786432 | tf_op jit(solution)/shard_map/all_to_all | solution.py:334
  21.9 94.7 %copy-start.1 = (bf16[2048,416]{0,1:T(8,128)(2,1)S(1)}, bf16[2048,416]{0,1:T(8,128)(2,1)}, u32[]{:S(2)}) copy-start(bf16[2048,416]{0,1:T(8,128)(2,1)} %param.4) | copy-start | bytes 5111812
  23.4 0.7 copy-start.3
  24.0 0.6 copy-start.5
  24.7 44.2 %copy-start.4 = (bf16[16,3072]{1,0:T(8,128)(2,1)S(1)}, bf16[16,3072]{1,0:T(8,128)(2,1)}, u32[]{:S(2)}) copy-start(bf16[16,3072]{1,0:T(8,128)(2,1)} %copy-done.3) | copy-start | bytes 294916
  24.7 44.2 %copy-start.6 = (bf16[16,3072]{1,0:T(8,128)(2,1)S(1)}, bf16[16,3072]{1,0:T(8,128)(2,1)}, u32[]{:S(2)}) copy-start(bf16[16,3072]{1,0:T(8,128)(2,1)} %copy-done.5) | copy-start | bytes 294916
  43.0 0.8 copy-start.2
  43.8 20.1 %all-to-all-start.2 = ((f32[16,16,512]{2,1,0:T(8,128)}), f32[16,16,512]{2,1,0:T(8,128)S(1)}, u32[]{:S(2)}, u32[]{:S(2)}) async-start(f32[16,16,512]{2,1,0:T(8,128)} %copy-done.2), calls=%async_computation.2 | async-start | bytes 1048576 | tf_op jit(solution)/shard_map/all_to_all | solution.py:334
  48.7 6.6 %collective-permute-start.3 = (f32[208,128]{1,0:T(8,128)S(1)}, f32[208,128]{1,0:T(8,128)S(1)}, u32[]{:S(2)}, u32[]{:S(2)}) collective-permute-start(f32[208,128]{1,0:T(8,128)S(1)} %pack_rows.1), channel_id=1, source_target_pairs={{0,96},{16,112},{32,64},{48,80},{64,32},{80,48},{96,0},{112,16},{1... | collective-permute-start | bytes 319496 | tf_op jit(solution)/shard_map/ppermute | solution.py:371
  49.1 10.7 %collective-permute-start.2 = (f32[208,128]{1,0:T(8,128)S(1)}, f32[208,128]{1,0:T(8,128)S(1)}, u32[]{:S(2)}, u32[]{:S(2)}) collective-permute-start(f32[208,128]{1,0:T(8,128)S(1)} %pack_rows.1), channel_id=1, source_target_pairs={{0,64},{16,80},{32,96},{48,112},{64,0},{80,16},{96,32},{112,48},{1... | collective-permute-start | bytes 319496 | tf_op jit(solution)/shard_map/ppermute | solution.py:371
  50.2 11.9 %collective-permute-start.1 = (f32[208,128]{1,0:T(8,128)S(1)}, f32[208,128]{1,0:T(8,128)S(1)}, u32[]{:S(2)}, u32[]{:S(2)}) collective-permute-start(f32[208,128]{1,0:T(8,128)S(1)} %pack_rows.1), channel_id=1, source_target_pairs={{0,32},{16,48},{32,0},{48,16},{64,96},{80,112},{96,64},{112,80},{1... | collective-permute-start | bytes 319496 | tf_op jit(solution)/shard_map/ppermute | solution.py:371
  52.3 10.3 %collective-permute-start.9 = (bf16[16,3072]{1,0:T(8,128)(2,1)}, bf16[16,3072]{1,0:T(8,128)(2,1)S(1)}, u32[]{:S(2)}, u32[]{:S(2)}) collective-permute-start(bf16[16,3072]{1,0:T(8,128)(2,1)} %copy-done.3), channel_id=1, source_target_pairs={{0,3},{1,0},{2,1},{3,2},{4,7},{5,4},{6,5},{7,6},{8,11},{9,8},{10,9... | collective-permute-start | bytes 294920 | tf_op jit(solution)/shard_map/ppermute | solution.py:391
  54.8 8.4 %collective-permute-start.8 = (bf16[16,3072]{1,0:T(8,128)(2,1)}, bf16[16,3072]{1,0:T(8,128)(2,1)S(1)}, u32[]{:S(2)}, u32[]{:S(2)}) collective-permute-start(bf16[16,3072]{1,0:T(8,128)(2,1)} %copy-done.3), channel_id=1, source_target_pairs={{0,2},{1,3},{2,0},{3,1},{4,6},{5,7},{6,4},{7,5},{8,10},{9,11},{10,... | collective-permute-start | bytes 294920 | tf_op jit(solution)/shard_map/ppermute | solution.py:391
  55.4 7.9 %copy-start.10 = (f32[208,128]{1,0:T(8,128)}, f32[208,128]{1,0:T(8,128)S(1)}, u32[]{:S(2)}) copy-start(f32[208,128]{1,0:T(8,128)S(1)} %collective-permute-done.3) | copy-start | bytes 319492
  55.4 11.8 %collective-permute-start.7 = (bf16[16,3072]{1,0:T(8,128)(2,1)}, bf16[16,3072]{1,0:T(8,128)(2,1)}, u32[]{:S(2)}, u32[]{:S(2)}) collective-permute-start(bf16[16,3072]{1,0:T(8,128)(2,1)} %copy-done.3), channel_id=1, source_target_pairs={{0,1},{1,2},{2,3},{3,0},{4,5},{5,6},{6,7},{7,4},{8,9},{9,10},{10,1... | collective-permute-start | bytes 294920 | tf_op jit(solution)/shard_map/ppermute | solution.py:391
  59.8 3.4 %copy-start.11 = (f32[208,128]{1,0:T(8,128)}, f32[208,128]{1,0:T(8,128)S(1)}, u32[]{:S(2)}) copy-start(f32[208,128]{1,0:T(8,128)S(1)} %collective-permute-done.2) | copy-start | bytes 319492
  59.8 8.8 %collective-permute-start.12 = (bf16[16,3072]{1,0:T(8,128)(2,1)}, bf16[16,3072]{1,0:T(8,128)(2,1)}, u32[]{:S(2)}, u32[]{:S(2)}) collective-permute-start(bf16[16,3072]{1,0:T(8,128)(2,1)} %copy-done.5), channel_id=1, source_target_pairs={{0,12},{1,13},{2,14},{3,15},{4,0},{5,1},{6,2},{7,3},{8,4},{9,5},{1... | collective-permute-start | bytes 294920 | tf_op jit(solution)/shard_map/ppermute | solution.py:394
  62.1 1.1 copy-start.12
  62.1 6.8 %collective-permute-start.11 = (bf16[16,3072]{1,0:T(8,128)(2,1)}, bf16[16,3072]{1,0:T(8,128)(2,1)}, u32[]{:S(2)}, u32[]{:S(2)}) collective-permute-start(bf16[16,3072]{1,0:T(8,128)(2,1)} %copy-done.5), channel_id=1, source_target_pairs={{0,8},{1,9},{2,10},{3,11},{4,12},{5,13},{6,14},{7,15},{8,0},{9,1},... | collective-permute-start | bytes 294920 | tf_op jit(solution)/shard_map/ppermute | solution.py:394
  62.6 6.2 %collective-permute-start.10 = (bf16[16,3072]{1,0:T(8,128)(2,1)}, bf16[16,3072]{1,0:T(8,128)(2,1)}, u32[]{:S(2)}, u32[]{:S(2)}) collective-permute-start(bf16[16,3072]{1,0:T(8,128)(2,1)} %copy-done.5), channel_id=1, source_target_pairs={{0,4},{1,5},{2,6},{3,7},{4,8},{5,9},{6,10},{7,11},{8,12},{9,13},{1... | collective-permute-start | bytes 294920 | tf_op jit(solution)/shard_map/ppermute | solution.py:394
  63.2 0.6 copy-start.7
  63.9 33.2 %collective-permute-start = (f32[16,16,512]{2,1,0:T(8,128)S(1)}, f32[16,16,512]{2,1,0:T(8,128)S(1)}, u32[]{:S(2)}, u32[]{:S(2)}) collective-permute-start(f32[16,16,512]{2,1,0:T(8,128)S(1)} %all-to-all-done.2.own_ref), channel_id=1, source_target_pairs={{0,16},{16,0},{32,48},{48,32},{64,80},{80,64},{96,112},{112,96},{1... | collective-permute-start | bytes 1572872 | tf_op jit(solution)/shard_map/ppermute | solution.py:371
  67.1 24.9 %collective-permute-start.4 = (f32[4,208,128]{2,1,0:T(8,128)S(1)}, f32[4,208,128]{2,1,0:T(8,128)S(1)}, u32[]{:S(2)}, u32[]{:S(2)}) collective-permute-start(f32[4,208,128]{2,1,0:T(8,128)S(1)} %pad_maximum_fusion.near_ref), channel_id=1, source_target_pairs={{0,128},{16,144},{32,160},{48,176},{64,192},{80,208},{96,224},{112... | collective-permute-start | bytes 1277960 | tf_op jit(solution)/shard_map/ppermute | solution.py:371
  68.6 24.0 %collective-permute-start.5 = (f32[4,208,128]{2,1,0:T(8,128)S(1)}, f32[4,208,128]{2,1,0:T(8,128)S(1)}, u32[]{:S(2)}, u32[]{:S(2)}) collective-permute-start(f32[4,208,128]{2,1,0:T(8,128)S(1)} %pad_maximum_fusion.near_ref), channel_id=1, source_target_pairs={{0,16},{16,0},{32,48},{48,32},{64,80},{80,64},{96,112},{112,96},{1... | collective-permute-start | bytes 1277960 | tf_op jit(solution)/shard_map/ppermute | solution.py:371
  68.9 0.9 copy-start.8
  70.8 23.3 %collective-permute-start.15 = (bf16[64,3072]{1,0:T(8,128)(2,1)S(1)}, bf16[64,3072]{1,0:T(8,128)(2,1)S(1)}, u32[]{:S(2)}, u32[]{:S(2)}) collective-permute-start(bf16[64,3072]{1,0:T(8,128)(2,1)S(1)} %get-tuple-element.12.refs_0_), channel_id=1, source_target_pairs={{0,12},{1,13},{2,14},{3,15},{4,0},{5,1},{6,2},{7,3},{8,4},{9,5},{1... | collective-permute-start | bytes 1179656 | tf_op jit(solution)/shard_map/ppermute | solution.py:394
  73.5 22.2 %collective-permute-start.14 = (bf16[64,3072]{1,0:T(8,128)(2,1)S(1)}, bf16[64,3072]{1,0:T(8,128)(2,1)S(1)}, u32[]{:S(2)}, u32[]{:S(2)}) collective-permute-start(bf16[64,3072]{1,0:T(8,128)(2,1)S(1)} %get-tuple-element.12.refs_0_), channel_id=1, source_target_pairs={{0,8},{1,9},{2,10},{3,11},{4,12},{5,13},{6,14},{7,15},{8,0},{9,1},... | collective-permute-start | bytes 1179656 | tf_op jit(solution)/shard_map/ppermute | solution.py:394
  92.0 24.6 %collective-permute-start.6 = (f32[4,208,128]{2,1,0:T(8,128)S(1)}, f32[4,208,128]{2,1,0:T(8,128)S(1)}, u32[]{:S(2)}, u32[]{:S(2)}) collective-permute-start(f32[4,208,128]{2,1,0:T(8,128)S(1)} %collective-permute-done.4.far_ref), channel_id=1, source_target_pairs={{0,16},{16,0},{32,48},{48,32},{64,80},{80,64},{96,112},{112,96},{1... | collective-permute-start | bytes 1277960 | tf_op jit(solution)/shard_map/ppermute | solution.py:371
  92.6 22.0 %collective-permute-start.13 = (bf16[64,3072]{1,0:T(8,128)(2,1)S(1)}, bf16[64,3072]{1,0:T(8,128)(2,1)S(1)}, u32[]{:S(2)}, u32[]{:S(2)}) collective-permute-start(bf16[64,3072]{1,0:T(8,128)(2,1)S(1)} %get-tuple-element.12.refs_0_), channel_id=1, source_target_pairs={{0,4},{1,5},{2,6},{3,7},{4,8},{5,9},{6,10},{7,11},{8,12},{9,13},{1... | collective-permute-start | bytes 1179656 | tf_op jit(solution)/shard_map/ppermute | solution.py:394
  94.1 20.5 %collective-permute-start.18 = (bf16[64,3072]{1,0:T(8,128)(2,1)S(1)}, bf16[64,3072]{1,0:T(8,128)(2,1)S(1)}, u32[]{:S(2)}, u32[]{:S(2)}) collective-permute-start(bf16[64,3072]{1,0:T(8,128)(2,1)S(1)} %get-tuple-element.13.refs_4_), channel_id=1, source_target_pairs={{0,3},{1,0},{2,1},{3,2},{4,7},{5,4},{6,5},{7,6},{8,11},{9,8},{10,9... | collective-permute-start | bytes 1179656 | tf_op jit(solution)/shard_map/ppermute | solution.py:391
  95.7 19.0 %collective-permute-start.17 = (bf16[64,3072]{1,0:T(8,128)(2,1)S(1)}, bf16[64,3072]{1,0:T(8,128)(2,1)S(1)}, u32[]{:S(2)}, u32[]{:S(2)}) collective-permute-start(bf16[64,3072]{1,0:T(8,128)(2,1)S(1)} %get-tuple-element.13.refs_4_), channel_id=1, source_target_pairs={{0,2},{1,3},{2,0},{3,1},{4,6},{5,7},{6,4},{7,5},{8,10},{9,11},{10,... | collective-permute-start | bytes 1179656 | tf_op jit(solution)/shard_map/ppermute | solution.py:391
  97.1 19.5 %collective-permute-start.16 = (bf16[64,3072]{1,0:T(8,128)(2,1)S(1)}, bf16[64,3072]{1,0:T(8,128)(2,1)S(1)}, u32[]{:S(2)}, u32[]{:S(2)}) collective-permute-start(bf16[64,3072]{1,0:T(8,128)(2,1)S(1)} %get-tuple-element.13.refs_4_), channel_id=1, source_target_pairs={{0,1},{1,2},{2,3},{3,0},{4,5},{5,6},{6,7},{7,4},{8,9},{9,10},{10,1... | collective-permute-start | bytes 1179656 | tf_op jit(solution)/shard_map/ppermute | solution.py:391
